TPU v7x, 256 devices: a whole 4x4x8 slice. The times are simulated.
256 devices in a mesh: replica: 16 (over z, core), tile: 16 (over x, y).
Axes of the slice: x: 4, y: 4, z: 8, core: 2. Of those that a mesh axis runs over, the one named last changes fastest.
Arguments:
- public_tokens: bfloat16 [4096, 5120], P('replica', 'tile'), may hold values from -6 to 6
- public_targets: bfloat16 [4096, 4096], P(('replica', 'tile')), may hold values from -6 to 6
- private_tokens: bfloat16 [6144, 5120], P('replica', 'tile'), may hold values from -6 to 6
- private_targets: bfloat16 [6144, 4096], P(('replica', 'tile')), may hold values from -6 to 6
- token_counts: int32 [16, 3], P('replica'), may hold values from 1 to 128, 320 in all within a row
- weight: float32 [5120, 4096], P('tile', 'replica'), may hold values from -0.078125 to 0.078125
- public_moment: float32 [5120, 4096], P('tile', 'replica'), may hold values from 1 to 10
- adam_first: float32 [5120, 4096], P('tile', 'replica'), may hold values from -3 to 3
- adam_second: float32 [5120, 4096], P('tile', 'replica'), may hold values from 0.1 to 1
- noise_draw: float32 [5120, 4096], P('tile', 'replica'), may hold values from -6 to 6
Outputs:
- new_weight: float32 [5120, 4096], P('tile', 'replica')
- new_first: float32 [5120, 4096], P('tile', 'replica')
- new_second: float32 [5120, 4096], P('tile', 'replica')
- new_public: float32 [5120, 4096], P('tile', 'replica')
Inputs may be any that keep to these rules, and one draw needn't show every extreme that they name: `token_counts`: each row holds the live token counts of one replica's 3 private examples; every row sums to 320 and its largest entry is 128.
All inputs are finite; a program needn't handle non-finite values.
Results may differ from a plain program's by a relative error of at most 0.0031.
Values may be sent and summed in bfloat16 or wider, within the bound.
No kernel may reach another device: no remote copies, remote signals or barrier semaphores. Data moves between devices by JAX's collectives and lax.ppermute only.
A program may use at most 64 MiB of HBM per device.

v0:
```python
import math

import jax
import jax.numpy as jnp
from jax import lax
from jax.sharding import PartitionSpec as P

D = 5120
L = 128
Q = 4096


beta_first = 0.9
beta_second = 0.99
beta_public = 0.9
public_epsilon = 0.001
adam_epsilon = 1e-08
clip_factor = 0.6
noise_level = 4.0
learn_rate = 0.01
contract_rows = (((0,), (0,)), ((), ()))


def slot_owner(first_row, span, seq_len):
    rows_at = first_row + jnp.arange(span, dtype=jnp.int32)
    return (rows_at, rows_at // seq_len)


def per_slot(owners, values):
    picks = jnp.arange(values.shape[0], dtype=jnp.int32)
    return jnp.sum(jnp.where(owners[:, None] == picks[None, :], values[None, :], 0), axis=1)


def live_slots(first_row, span, counts_row, seq_len):
    rows_at, owners = slot_owner(first_row, span, seq_len)
    return rows_at % seq_len < per_slot(owners, counts_row)


def on_device(
    public_tokens,
    public_targets,
    private_tokens,
    private_targets,
    token_counts,
    weight,
    public_moment,
    adam_first,
    adam_second,
    noise_draw,
):
    replicas = lax.axis_size("replica")
    tile_pos = lax.axis_index("tile")
    seq_len = L
    w_half = lax.all_gather(weight.astype(jnp.bfloat16), "replica", axis=1, tiled=True)
    public_total = public_tokens.shape[0] * replicas
    block_x = public_tokens
    public_out = lax.psum_scatter(
        jnp.dot(block_x, w_half, preferred_element_type=jnp.float32),
        "tile",
        scatter_dimension=0,
        tiled=True,
    )
    public_delta = (public_out - public_targets.astype(jnp.float32)).astype(jnp.bfloat16)
    block_x = public_tokens
    public_grad = lax.dot_general(
        block_x,
        lax.all_gather(public_delta, "tile", axis=0, tiled=True),
        contract_rows,
        preferred_element_type=jnp.float32,
    )
    grad_owned = lax.psum_scatter(
        public_grad, "replica", scatter_dimension=1, tiled=True
    ) / math.sqrt(public_total)
    new_public = beta_public * public_moment + (1.0 - beta_public) * grad_owned * grad_owned
    precond_owned = 1.0 / (jnp.sqrt(new_public) + public_epsilon)
    precond = lax.all_gather(precond_owned, "replica", axis=1, tiled=True)
    counts_row = token_counts[0]
    slots_all = private_tokens.shape[0]
    slot_rows = private_targets.shape[0]
    block_x = private_tokens
    private_out = lax.psum_scatter(
        jnp.dot(block_x, w_half, preferred_element_type=jnp.float32),
        "tile",
        scatter_dimension=0,
        tiled=True,
    )
    local_live = live_slots(tile_pos * slot_rows, slot_rows, counts_row, seq_len)
    local_delta = jnp.where(
        local_live[:, None], private_out - private_targets.astype(jnp.float32), 0.0
    ).astype(jnp.bfloat16)
    private_delta = lax.all_gather(local_delta, "tile", axis=0, tiled=True)

    def example_norm(example):
        first_row = example * seq_len
        block_x = lax.dynamic_slice_in_dim(private_tokens, first_row, seq_len, 0)
        block_d = lax.dynamic_slice_in_dim(private_delta, first_row, seq_len, 0)
        grads = lax.dot_general(block_x, block_d, contract_rows, preferred_element_type=jnp.float32)
        scaled = grads * precond
        return jnp.sum(scaled * scaled)

    examples_here = token_counts.shape[1]
    partial_norms = lax.map(example_norm, jnp.arange(examples_here, dtype=jnp.int32))
    squares = lax.psum(partial_norms, "tile")
    clip_norm = clip_factor * math.sqrt(L * D * Q)
    factors = clip_norm / jnp.maximum(jnp.sqrt(squares), clip_norm)
    rows_at, owners = slot_owner(0, slots_all, seq_len)
    slot_factor = per_slot(owners, factors)
    weighted = (slot_factor[:, None] * private_delta.astype(jnp.float32)).astype(jnp.bfloat16)
    summed = precond * lax.dot_general(
        private_tokens, weighted, contract_rows, preferred_element_type=jnp.float32
    )
    summed_owned = lax.psum_scatter(summed, "replica", scatter_dimension=1, tiled=True)
    examples_total = examples_here * replicas
    noise_scale = noise_level * clip_factor * math.sqrt(L)
    gradient = (summed_owned + noise_scale * noise_draw) / examples_total
    new_first = beta_first * adam_first + (1.0 - beta_first) * gradient
    new_second = beta_second * adam_second + (1.0 - beta_second) * gradient * gradient
    first_hat = new_first / (1.0 - beta_first**2)
    second_hat = new_second / (1.0 - beta_second**2)
    new_weight = weight - learn_rate * first_hat / (jnp.sqrt(second_hat) + adam_epsilon)
    return (new_weight, new_first, new_second, new_public)


def solution(mesh):
    placed = (
        P("replica", "tile"),
        P(("replica", "tile"), None),
        P("replica", "tile"),
        P(("replica", "tile"), None),
        P("replica", None),
        P("tile", "replica"),
        P("tile", "replica"),
        P("tile", "replica"),
        P("tile", "replica"),
        P("tile", "replica"),
    )
    return jax.shard_map(
        on_device,
        mesh=mesh,
        in_specs=placed,
        out_specs=(
            P("tile", "replica"),
            P("tile", "replica"),
            P("tile", "replica"),
            P("tile", "replica"),
        ),
        check_vma=False,
    )
```

profile of v0, /device:TPU:1, one launch (start us, length us, event | category | flops | bytes accessed | tf_op | source)
XLA Modules:
  0.0 586.0 jit_solution(9840578557947384932)
XLA Ops:
  7.2 1.7 convert_element_type.23
  9.0 48.0 %all-gather.5.cloned.1.call-done = bf16[320,4096]{1,0:T(8,128)(2,1)} async-done(((bf16[320,256]{1,0:T(8,128)(2,1)}), bf16[320,4096]{1,0:T(8,128)(2,1)}) %all-gather.5.cloned.1.call-update) | async-done | bytes 2621456 | tf_op jit(solution)/shard_map/all_gather | solution.py:54
  57.1 5.2 fusion.11
  62.4 80.7 %reduce-scatter.7.cloned.1.call-done = f32[16,4096]{1,0:T(8,128)} async-done(((f32[256,4096]{1,0:T(8,128)}), f32[16,4096]{1,0:T(8,128)}) %reduce-scatter.7.cloned.1.call-update) | async-done | bytes 262160 | tf_op jit(solution)/shard_map/reduce_scatter | solution.py:57
  143.0 1.6 subtract_convert_fusion
  144.7 0.0 reduce-scatter.13.cloned.1.call-start
  144.8 4.5 fusion.12
  149.4 46.1 %all-gather.7.cloned.1.call-done = bf16[256,4096]{1,0:T(8,128)(2,1)} async-done(((bf16[16,4096]{1,0:T(8,128)(2,1)}), bf16[256,4096]{1,0:T(8,128)(2,1)}) %all-gather.7.cloned.1.call-update) | async-done | bytes 2097168 | tf_op jit(solution)/shard_map/all_gather | solution.py:67
  195.4 4.8 convolution_bitcast_fusion.1
  200.3 0.6 copy-done.10
  200.8 0.1 select_reduce_fusion.1
  201.0 83.9 %reduce-scatter.13.cloned.1.call-done = f32[24,4096]{1,0:T(8,128)} async-done(((f32[384,4096]{1,0:T(8,128)}), f32[24,4096]{1,0:T(8,128)}) %reduce-scatter.13.cloned.1.call-update) | async-done | bytes 393232
  284.9 1.8 select_convert_fusion
  286.7 63.9 %reduce-scatter.9.cloned.1.call-done = f32[320,256]{1,0:T(8,128)} async-done(((f32[320,4096]{1,0:T(8,128)}), f32[320,256]{1,0:T(8,128)}) %reduce-scatter.9.cloned.1.call-update) | async-done | bytes 327696 | tf_op jit(solution)/shard_map/reduce_scatter | solution.py:71
  350.6 1.9 add_divide_fusion
  352.6 54.8 %all-gather.11.cloned.1.call-done = bf16[384,4096]{1,0:T(8,128)(2,1)} async-done(((bf16[24,4096]{1,0:T(8,128)(2,1)}), bf16[384,4096]{1,0:T(8,128)(2,1)}) %all-gather.11.cloned.1.call-update) | async-done | bytes 3145744 | tf_op jit(solution)/shard_map/all_gather | solution.py:91
  407.5 45.5 %all-gather.9.cloned.1.call-done = f32[320,4096]{1,0:T(8,128)} async-done(((f32[320,256]{1,0:T(8,128)}), f32[320,4096]{1,0:T(8,128)}) %all-gather.9.cloned.1.call-update) | async-done | bytes 5242896 | tf_op jit(solution)/shard_map/all_gather | solution.py:76
  453.0 20.8 %while.10 = (s32[]{:T(128)}, f32[3]{0:T(128)S(1)}, s32[3]{0:T(128)S(1)}, bf16[384,320]{0,1:T(8,128)(2,1)S(1)}, bf16[384,4096]{1,0:T(8,128)(2,1)}, /*index=5*/f32...) while((s32[]{:T(128)}, f32[3]{0:T(128)S(1)}, s32[3]{0:T(128)S(1)}, ...), condition=%wide.region_6.7_spmd, body=%wide.region_4.6_spmd.sunk | while | flops 339476480 | bytes 6374575 | solution.py:102
  453.0 0.6 dynamic_slice.19
  454.2 4.9 fusion.25
  459.2 0.8 dynamic_update_slice.5
  459.9 0.6 dynamic_slice.19
  461.1 5.0 fusion.25
  466.1 0.8 dynamic_update_slice.5
  466.9 0.6 dynamic_slice.19
  468.1 5.0 fusion.25
  473.1 0.8 dynamic_update_slice.5
  473.8 33.2 %psum.7 = f32[3]{0:T(128)S(1)} all-reduce(f32[3]{0:T(128)S(1)} %get-tuple-element.36), channel_id=1, replica_groups=mesh['replica'=16,'tile'=16] {'tile'}, use_global_device_ids=true, to_apply=%region_7.8 | all-reduce | flops 3 | bytes 24 | tf_op jit(solution)/shard_map/psum | solution.py:103
  507.0 0.1 select_reduce_fusion
  507.1 7.4 %fusion.5 = f32[320,4096]{1,0:T(8,128)} fusion(f32[320,4096]{1,0:T(8,128)} %get-tuple-element.130, bf16[384,320]{0,1:T(8,128)(2,1)S(1)} %get-tuple-element.142, bf16[384,4096]{1,0:T(8,128)(2,1)} %get-tuple-element.138, f32[384]{0:T(512)S(1)} %select_reduce_fusion), kind=kOutput, calls=%fused_computation.9 | convolution fusion | flops 1012662272 | bytes 13878784 | tf_op jit(solution)/shard_map/dot_general | solution.py:109
  514.6 62.5 %reduce-scatter.11.cloned.1.call-done = f32[320,256]{1,0:T(8,128)} async-done(((f32[320,4096]{1,0:T(8,128)}), f32[320,256]{1,0:T(8,128)}) %reduce-scatter.11.cloned.1.call-update) | async-done | bytes 327696 | tf_op jit(solution)/shard_map/reduce_scatter | solution.py:112
  577.1 2.1 divide_subtract_fusion
  (42 shorter events, 0.5 us)
Async XLA Ops:
  7.2 49.9 %copy-start = (bf16[256,320]{0,1:T(8,128)(2,1)S(1)}, bf16[256,320]{0,1:T(8,128)(2,1)}, u32[]{:S(2)}) copy-start(bf16[256,320]{0,1:T(8,128)(2,1)} %param.12) | copy-start | bytes 491524
  7.2 49.9 %all-gather.5.cloned.1.call-start = ((), (), s32[]{:S(2)}) async-start(), calls=%async_computation.4 | async-start | bytes 2785280 | tf_op jit(solution)/shard_map/all_gather | solution.py:54
  8.9 134.1 %copy-start.9 = (bf16[16,4096]{1,0:T(8,128)(2,1)S(1)}, bf16[16,4096]{1,0:T(8,128)(2,1)}, u32[]{:S(2)}) copy-start(bf16[16,4096]{1,0:T(8,128)(2,1)} %param.13) | copy-start | bytes 393220
  9.0 135.8 %copy-start.2 = (bf16[384,320]{0,1:T(8,128)(2,1)S(1)}, bf16[384,320]{0,1:T(8,128)(2,1)}, u32[]{:S(2)}) copy-start(bf16[384,320]{0,1:T(8,128)(2,1)} %param.14) | copy-start | bytes 737284
  9.0 134.1 %reduce-scatter.7.cloned.1.call-start = ((), (), s32[]{:S(2)}) async-start(), calls=%async_computation.5 | async-start | bytes 4456448 | tf_op jit(solution)/shard_map/reduce_scatter | solution.py:57
  57.1 87.7 %copy-start.1 = (bf16[320,4096]{1,0:T(8,128)(2,1)S(1)}, bf16[320,4096]{1,0:T(8,128)(2,1)}, u32[]{:S(2)}) copy-start(bf16[320,4096]{1,0:T(8,128)(2,1)} %all-gather.5.cloned.1.call-done) | copy-start | bytes 7864324
  62.3 133.1 %all-gather.7.cloned.1.call-start = ((), (), s32[]{:S(2)}) async-start(), calls=%async_computation.6 | async-start | bytes 2228224 | tf_op jit(solution)/shard_map/all_gather | solution.py:67
  144.7 140.2 %reduce-scatter.13.cloned.1.call-start = ((), (), s32[]{:S(2)}) async-start(), calls=%async_computation.11 | async-start | bytes 6684672
  149.3 201.3 %reduce-scatter.9.cloned.1.call-start = ((), (), s32[]{:S(2)}) async-start(), calls=%async_computation.7 | async-start | bytes 5570560 | tf_op jit(solution)/shard_map/reduce_scatter | solution.py:71
  200.2 0.7 copy-start.10
  200.2 84.7 %copy-start.8 = (bf16[24,4096]{1,0:T(8,128)(2,1)S(1)}, bf16[24,4096]{1,0:T(8,128)(2,1)}, u32[]{:S(2)}) copy-start(bf16[24,4096]{1,0:T(8,128)(2,1)} %param.15) | copy-start | bytes 589828
  200.2 150.4 %copy-start.4 = (f32[320,256]{1,0:T(8,128)S(1)}, f32[320,256]{1,0:T(8,128)}, u32[]{:S(2)}) copy-start(f32[320,256]{1,0:T(8,128)} %param.18) | copy-start | bytes 983044
  200.2 207.2 %all-gather.11.cloned.1.call-start = ((), (), s32[]{:S(2)}) async-start(), calls=%async_computation.9 | async-start | bytes 3342336 | tf_op jit(solution)/shard_map/all_gather | solution.py:91
  286.7 166.3 %all-gather.9.cloned.1.call-start = ((), (), s32[]{:S(2)}) async-start(), calls=%async_computation.8 | async-start | bytes 5570560 | tf_op jit(solution)/shard_map/all_gather | solution.py:76
  352.6 224.6 %reduce-scatter.11.cloned.1.call-start = ((), (), s32[]{:S(2)}) async-start(), calls=%async_computation.10 | async-start | bytes 5570560 | tf_op jit(solution)/shard_map/reduce_scatter | solution.py:112
  514.5 62.6 %copy-start.3 = (f32[320,256]{1,0:T(8,128)S(1)}, f32[320,256]{1,0:T(8,128)}, u32[]{:S(2)}) copy-start(f32[320,256]{1,0:T(8,128)} %param.17) | copy-start | bytes 983044
  514.5 62.6 %copy-start.5 = (f32[320,256]{1,0:T(8,128)S(1)}, f32[320,256]{1,0:T(8,128)}, u32[]{:S(2)}) copy-start(f32[320,256]{1,0:T(8,128)} %param.21) | copy-start | bytes 983044
  514.5 62.6 %copy-start.6 = (f32[320,256]{1,0:T(8,128)S(1)}, f32[320,256]{1,0:T(8,128)}, u32[]{:S(2)}) copy-start(f32[320,256]{1,0:T(8,128)} %param.19) | copy-start | bytes 983044
  514.5 62.6 %copy-start.7 = (f32[320,256]{1,0:T(8,128)S(1)}, f32[320,256]{1,0:T(8,128)}, u32[]{:S(2)}) copy-start(f32[320,256]{1,0:T(8,128)} %param.20) | copy-start | bytes 983044
Sparse Core Ops, SparseCore 0:
  10.3 46.6 all-gather.4
  62.4 80.5 reduce-scatter.6
  146.0 49.3 all-gather.6
  199.0 85.8 reduce-scatter.12
  287.3 63.2 reduce-scatter.8
  353.5 53.9 all-gather.10
  409.9 43.0 all-gather.8
  514.7 62.3 reduce-scatter.10
where the time goes:
time: 589 us; the launch traced here: 586 us
  waiting for transfers between devices  486 us (83%)
  matrix products  36.8 us (6%)
  blocking collectives  33.2 us (6%)
  between operations  14.2 us (2%)
  other arithmetic  9.32 us (2%)
    unnamed x9, waiting for transfers between devices  84 us
    reduce_scatter x1, waiting for transfers between devices, on_device(): lax.psum_scatter(jnp.dot(block_x, w_half, preferred_element_type=jnp.floa...  80.7 us
    reduce_scatter x1, waiting for transfers between devices, on_device(): lax.psum_scatter(public_grad, 'replica', scatter_dimension=1, tiled=True)  63.9 us
    reduce_scatter x1, waiting for transfers between devices, on_device(): lax.psum_scatter(summed, 'replica', scatter_dimension=1, tiled=True)  62.5 us
    all_gather x1, waiting for transfers between devices, on_device(): private_delta = lax.all_gather(local_delta, 'tile', axis=0, tiled=True)  54.8 us
    all_gather x1, waiting for transfers between devices, on_device(): lax.all_gather(weight.astype(jnp.bfloat16), 'replica', axis=1, tiled=True)  48 us
    all_gather x1, waiting for transfers between devices, on_device(): lax.all_gather(public_delta, 'tile', axis=0, tiled=True)  46.1 us
    all_gather x1, waiting for transfers between devices, on_device(): precond = lax.all_gather(precond_owned, 'replica', axis=1, tiled=True)  45.5 us
  transfers between devices with their start and end apart: 8, of which 8 were waited for; matrix products, arithmetic and copies ran while one was open for 2% of the time, Pallas kernels for 0%

commit v1 on v0

v1 whole, which is shorter than its diff:
```python
import math

import jax
import jax.numpy as jnp
from jax import lax
from jax.sharding import PartitionSpec as P

D = 5120
L = 128
Q = 4096


beta_first = 0.9
beta_second = 0.99
beta_public = 0.9
public_epsilon = 0.001
adam_epsilon = 1e-08
clip_factor = 0.6
noise_level = 4.0
learn_rate = 0.01


def regroup(rows, tiles):
    groups, span, cols = rows.shape
    split = rows.reshape(groups, tiles, span // tiles, cols)
    return split.transpose(1, 0, 2, 3).reshape(tiles, groups * (span // tiles), cols)


def ungroup(rows, groups):
    tiles, span, cols = rows.shape
    split = rows.reshape(tiles, groups, span // groups, cols)
    return split.transpose(1, 0, 2, 3).reshape(groups, tiles * (span // groups), cols)


def sum_everywhere(values, axis):
    parts = lax.axis_size(axis)
    sent = jnp.broadcast_to(values[None], (parts, *values.shape))
    return jnp.sum(lax.all_to_all(sent, axis, 0, 0, tiled=True), axis=0)


def on_device(
    public_tokens,
    public_targets,
    private_tokens,
    private_targets,
    token_counts,
    weight,
    public_moment,
    adam_first,
    adam_second,
    noise_draw,
):
    replicas = lax.axis_size("replica")
    tiles = lax.axis_size("tile")
    pub = public_tokens.shape[0]
    priv = private_tokens.shape[0]
    cols = weight.shape[1]
    examples_here = token_counts.shape[1]

    live = (
        jnp.arange(L, dtype=jnp.int32)[None, :] < token_counts[0][:, None]
    ).reshape(priv)
    live_tokens = jnp.where(live[:, None], private_tokens, jnp.zeros_like(private_tokens))
    local = jnp.concatenate([public_tokens.T, live_tokens.T], axis=1)
    tokens = lax.all_gather(local, "replica", axis=0)

    targets = jnp.concatenate([public_targets, private_targets], axis=0)
    targets = targets.reshape(-1, replicas, cols).transpose(1, 0, 2)
    targets = lax.all_to_all(targets, "replica", 0, 0, tiled=True)
    pub_rows = public_targets.shape[0]
    targets = jnp.concatenate(
        [
            targets[:, :pub_rows].reshape(pub, cols),
            targets[:, pub_rows:].reshape(priv, cols),
        ],
        axis=0,
    )

    out = jnp.einsum(
        "rfn,fc->rnc",
        tokens,
        weight.astype(jnp.bfloat16),
        preferred_element_type=jnp.float32,
    ).astype(jnp.bfloat16)
    sent = jnp.concatenate(
        [regroup(out[:, :pub], tiles), regroup(out[:, pub:], tiles)], axis=1
    )
    got = lax.all_to_all(sent, "tile", 0, 0, tiled=True)
    total = jnp.sum(got.astype(jnp.float32), axis=0)
    delta = (total - targets.astype(jnp.float32)).astype(jnp.bfloat16)
    deltas = lax.all_gather(delta, "tile", axis=0)
    public_delta = ungroup(deltas[:, :pub], replicas)
    private_delta = ungroup(deltas[:, pub:], replicas)

    public_grad = jnp.einsum(
        "rfn,rnc->fc", tokens[:, :, :pub], public_delta, preferred_element_type=jnp.float32
    ) / math.sqrt(pub * replicas)
    new_public = beta_public * public_moment + (1.0 - beta_public) * public_grad * public_grad
    precond = 1.0 / (jnp.sqrt(new_public) + public_epsilon)

    grads = jnp.einsum(
        "rfek,rekc->refc",
        tokens[:, :, pub:].reshape(replicas, -1, examples_here, L),
        private_delta.reshape(replicas, examples_here, L, cols),
        preferred_element_type=jnp.float32,
    )
    scaled = grads * precond
    squares = jnp.sum(scaled * scaled, axis=(2, 3))
    squares = sum_everywhere(sum_everywhere(squares, "tile"), "replica")
    clip_norm = clip_factor * math.sqrt(L * D * Q)
    factors = clip_norm / jnp.maximum(jnp.sqrt(squares), clip_norm)
    summed = precond * jnp.sum(factors[:, :, None, None] * grads, axis=(0, 1))

    examples_total = examples_here * replicas
    noise_scale = noise_level * clip_factor * math.sqrt(L)
    gradient = (summed + noise_scale * noise_draw) / examples_total
    new_first = beta_first * adam_first + (1.0 - beta_first) * gradient
    new_second = beta_second * adam_second + (1.0 - beta_second) * gradient * gradient
    first_hat = new_first / (1.0 - beta_first**2)
    second_hat = new_second / (1.0 - beta_second**2)
    new_weight = weight - learn_rate * first_hat / (jnp.sqrt(second_hat) + adam_epsilon)
    return (new_weight, new_first, new_second, new_public)


def solution(mesh):
    placed = (
        P("replica", "tile"),
        P(("replica", "tile"), None),
        P("replica", "tile"),
        P(("replica", "tile"), None),
        P("replica", None),
        P("tile", "replica"),
        P("tile", "replica"),
        P("tile", "replica"),
        P("tile", "replica"),
        P("tile", "replica"),
    )
    return jax.shard_map(
        on_device,
        mesh=mesh,
        in_specs=placed,
        out_specs=(
            P("tile", "replica"),
            P("tile", "replica"),
            P("tile", "replica"),
            P("tile", "replica"),
        ),
        check_vma=False,
    )
```

time: 589 us -> 290 us (0.49)
  waiting for transfers between devices: 486 us -> 176 us
  matrix products: 36.8 us -> 17.4 us
  starting transfers between devices: 0.33 us -> 16.9 us
  local copies, waits for them, and re-layouts: 4.62 us -> 16.7 us
  other arithmetic: 9.32 us -> 19.7 us
    reduce_scatter x3 -> x0, waiting for transfers between devices: 207 us -> none  [the longest x1 80.7 us: on_device(): lax.psum_scatter(jnp.dot(block_x, w_half, preferred_element_type=jnp.floa...]
    all_gather x4 -> x2, waiting for transfers between devices: 194 us -> 101 us  [the longest x1 57.9 us: on_device(): deltas = lax.all_gather(delta, 'tile', axis=0)]
    unnamed x9 -> x2, waiting for transfers between devices: 84 us -> 0.03 us
    all_to_all x0 -> x2, waiting for transfers between devices: none -> 74.9 us  [the longest x1 74.9 us: on_device(): got = lax.all_to_all(sent, 'tile', 0, 0, tiled=True)]
    psum x1 -> x0, blocking collectives: 33.2 us -> none  [on_device(): squares = lax.psum(partial_norms, 'tile')]
    all_to_all x0 -> x2, blocking collectives: none -> 27.7 us  [sum_everywhere(): return jnp.sum(lax.all_to_all(sent, axis, 0, 0, tiled=True), axis=0)]
    dot_general x7 -> x3, matrix products: 36.8 us -> 17.4 us  [the longest x1 8.75 us: on_device(): jnp.einsum('rfek,rekc->refc', tokens[:, :, pub:].reshape(replicas, -1, ex...]
    all_to_all x0 -> x2, starting transfers between devices: none -> 16.8 us  [the longest x1 9.97 us: on_device(): targets = lax.all_to_all(targets, 'replica', 0, 0, tiled=True)]
  transfers between devices with their start and end apart: 8 -> 4, of which waited for: 8 -> 3; matrix products, arithmetic and copies ran while one was open for 2% -> 8% of each run, Pallas kernels for 0% -> 0%
where the time goes in v1:
time: 290 us; the launch traced here: 289 us
  waiting for transfers between devices  176 us (61%)
  blocking collectives  27.7 us (10%)
  other arithmetic  19.7 us (7%)
  matrix products  17.4 us (6%)
  starting transfers between devices  16.9 us (6%)
  local copies, waits for them, and re-layouts  16.7 us (6%)
  between operations  14.3 us (5%)
    all_to_all x1, waiting for transfers between devices, on_device(): got = lax.all_to_all(sent, 'tile', 0, 0, tiled=True)  74.9 us
    all_gather x1, waiting for transfers between devices, on_device(): deltas = lax.all_gather(delta, 'tile', axis=0)  57.9 us
    all_gather x1, waiting for transfers between devices, on_device(): tokens = lax.all_gather(local, 'replica', axis=0)  43.5 us
    all_to_all x2, blocking collectives, sum_everywhere(): return jnp.sum(lax.all_to_all(sent, axis, 0, 0, tiled=True), axis=0)  27.7 us
    slice x2, local copies, waits for them, and re-layouts, on_device(): tokens[:, :, pub:].reshape(replicas, -1, examples_here, L)  10.8 us
    all_to_all x1, starting transfers between devices, on_device(): targets = lax.all_to_all(targets, 'replica', 0, 0, tiled=True)  9.97 us
    dot_general x1, matrix products, on_device(): jnp.einsum('rfek,rekc->refc', tokens[:, :, pub:].reshape(replicas, -1, ex...  8.75 us
    reduce_sum x1, other arithmetic, on_device(): summed = precond * jnp.sum(factors[:, :, None, None] * grads, axis=(0, 1))  7.22 us
  transfers between devices with their start and end apart: 4, of which 3 were waited for; matrix products, arithmetic and copies ran while one was open for 8% of the time, Pallas kernels for 0%

profile of v1, /device:TPU:1, one launch (start us, length us, event | category | flops | bytes accessed | tf_op | source)
XLA Modules:
  0.0 288.9 jit_solution(16349363249404939296)
XLA Ops:
  7.2 0.7 fusion.10
  7.9 1.0 select_bitcast_fusion
  8.9 1.7 pad_maximum_fusion.1
  10.7 1.0 pad_maximum_fusion.2
  11.8 0.8 copy.38
  12.6 10.0 %all-to-all-start.1 = ((bf16[16,40,256]{2,1,0:T(8,128)(2,1)}), bf16[16,40,256]{2,1,0:T(8,128)(2,1)S(1)}, u32[]{:S(2)}, u32[]{:S(2)}) async-start(bf16[16,40,256]{2,1,0:T(8,128)(2,1)} %copy.38), calls=%async_computation.1 | async-start | bytes 655360 | tf_op jit(solution)/shard_map/all_to_all | solution.py:69
  22.5 43.5 %all-gather.6.cloned.1.call-done = bf16[5120,640]{1,0:T(8,128)(2,1)} async-done(((bf16[320,640]{1,0:T(8,128)(2,1)}), bf16[5120,640]{1,0:T(8,128)(2,1)}) %all-gather.6.cloned.1.call-update) | async-done | bytes 6553616 | tf_op jit(solution)/shard_map/all_gather | solution.py:65
  66.1 5.8 %convolution_convert_fusion = bf16[16,640,256]{2,1,0:T(8,128)(2,1)S(1)} fusion(bf16[16,320,640]{2,1,0:T(8,128)(2,1)} %bitcast.55, f32[320,256]{1,0:T(8,128)} %param.15), kind=kOutput, calls=%fused_computation.4 | convolution fusion | flops 1680424960 | bytes 12124160 | tf_op jit(solution)/shard_map/rfn,fc->rnc/dot_general | solution.py:79
  71.9 0.1 slice.33
  72.0 0.2 slice.34
  72.3 0.3 copy.37
  72.6 0.2 copy.36
  72.8 2.6 pad_maximum_fusion
  75.4 6.8 %all-to-all-start = ((bf16[16,640,256]{2,1,0:T(8,128)(2,1)}), bf16[16,640,256]{2,1,0:T(8,128)(2,1)}, u32[]{:S(2)}, u32[]{:S(2)}) async-start(bf16[16,640,256]{2,1,0:T(8,128)(2,1)} %pad_maximum_fusion), calls=%async_computation | async-start | bytes 10485760 | tf_op jit(solution)/shard_map/all_to_all | solution.py:88
  82.3 74.9 %all-to-all-done = bf16[16,640,256]{2,1,0:T(8,128)(2,1)} async-done(((bf16[16,640,256]{2,1,0:T(8,128)(2,1)}), bf16[16,640,256]{2,1,0:T(8,128)(2,1)}, u32[]{:S(2)}, u32[]{:S(2)}) %all-to-all-start) | async-done | bytes 5242912 | tf_op jit(solution)/shard_map/all_to_all | solution.py:88
  157.2 3.3 %convert_reduce_fusion = f32[640,256]{1,0:T(8,128)S(1)} fusion(bf16[16,640,256]{2,1,0:T(8,128)(2,1)} %all-to-all-done), kind=kLoop, calls=%fused_computation.2 | loop fusion | flops 5079040 | bytes 5898240 | tf_op jit(solution)/shard_map/reduce_sum | solution.py:89
  160.5 0.8 fusion.5
  161.4 4.4 %slice.38 = bf16[16,320,384]{2,1,0:T(8,128)(2,1)} slice(bf16[16,320,640]{2,1,0:T(8,128)(2,1)} %bitcast.56), slice={[0:16], [0:320], [256:640]} | slice | bytes 7864320 | tf_op jit(solution)/shard_map/slice | solution.py:103
  165.7 6.4 %copy.40 = bf16[16,320,384]{1,2,0:T(8,128)(2,1)} copy(bf16[16,320,384]{2,1,0:T(8,128)(2,1)} %slice.38) | data formatting | bytes 7864320 | tf_op jit(solution)/shard_map/slice | solution.py:103
  172.2 57.9 %all-gather.4.cloned.1.call-done = bf16[16,640,256]{2,1,0:T(8,128)(2,1)} async-done(((bf16[1,640,256]{2,1,0:T(8,128)(2,1)}), bf16[16,640,256]{2,1,0:T(8,128)(2,1)}) %all-gather.4.cloned.1.call-update) | async-done | bytes 5242896 | tf_op jit(solution)/shard_map/all_gather | solution.py:91
  230.1 1.9 slice-done.2
  232.0 0.3 copy.41
  232.3 1.3 slice-done.3
  233.5 0.2 copy.39
  233.8 2.8 add_divide_fusion
  236.7 0.1 slice-done
  236.8 0.1 slice-done.1
  236.9 8.7 %multiply_reduce_fusion.1 = (f32[16,3]{1,0:T(8,128)S(1)}, f32[16,3,320,256]{3,2,1,0:T(8,128)}) fusion(f32[320,256]{1,0:T(8,128)S(1)} %get-tuple-element.7, bf16[16,320,3,128]{1,3,2,0:T(8,128)(2,1)S(1)} %bitcast.47, bf16[16,3,128,256]{3,2,1,0:T(8,128)(2,1)S(1)} %bitcast.52), kind=kOutput, calls=%fused_computation.1 | convolution fusion | flops 1018429376 | bytes 23134400 | tf_op jit(solution)/shard_map/rfek,rekc->refc/dot_general | solution.py:101
  245.7 11.2 %all_to_all.20 = f32[16,16,3]{1,2,0:T(4,128)S(1)} all-to-all(f32[16,16,3]{1,2,0:T(4,128)S(1)} %broadcast_in_dim.16), channel_id=1, replica_groups=mesh['replica'=16,'tile'=16] {'tile'}, dimensions={0} | all-to-all | bytes 6144 | tf_op jit(solution)/shard_map/all_to_all | solution.py:38
  257.0 16.5 %all_to_all.21 = f32[16,16,3]{1,2,0:T(4,128)S(1)} all-to-all(f32[16,16,3]{1,2,0:T(4,128)S(1)} %broadcast_in_dim.17), channel_id=1, replica_groups=mesh['replica'=16,'tile'=16] {'replica'}, dimensions={0} | all-to-all | bytes 6144 | tf_op jit(solution)/shard_map/all_to_all | solution.py:38
  273.6 7.2 %multiply_reduce_fusion = f32[320,256]{1,0:T(8,128)S(1)} fusion(f32[16,3,320,256]{3,2,1,0:T(8,128)} %get-tuple-element.10, f32[16,3]{1,0:T(8,128)S(1)} %copy.44), kind=kLoop, calls=%fused_computation | loop fusion | flops 7782400 | bytes 16056512 | tf_op jit(solution)/shard_map/reduce_sum | solution.py:112
  280.9 1.2 divide_subtract_fusion
  (36 shorter events, 0.5 us)
Async XLA Ops:
  7.2 58.9 %all-gather.6.cloned.1.call-start = ((), (), s32[]{:S(2)}) async-start(), calls=%async_computation.5 | async-start | bytes 6963200 | tf_op jit(solution)/shard_map/all_gather | solution.py:65
  12.6 62.9 %all-to-all-start.1 = ((bf16[16,40,256]{2,1,0:T(8,128)(2,1)}), bf16[16,40,256]{2,1,0:T(8,128)(2,1)S(1)}, u32[]{:S(2)}, u32[]{:S(2)}) async-start(bf16[16,40,256]{2,1,0:T(8,128)(2,1)} %copy.38), calls=%async_computation.1 | async-start | bytes 655360 | tf_op jit(solution)/shard_map/all_to_all | solution.py:69
  75.4 6.9 %copy-start = (bf16[16,40,256]{2,1,0:T(8,128)(2,1)}, bf16[16,40,256]{2,1,0:T(8,128)(2,1)S(1)}, u32[]{:S(2)}) copy-start(bf16[16,40,256]{2,1,0:T(8,128)(2,1)S(1)} %all-to-all-done.1) | copy-start | bytes 983044
  75.4 81.8 %all-to-all-start = ((bf16[16,640,256]{2,1,0:T(8,128)(2,1)}), bf16[16,640,256]{2,1,0:T(8,128)(2,1)}, u32[]{:S(2)}, u32[]{:S(2)}) async-start(bf16[16,640,256]{2,1,0:T(8,128)(2,1)} %pad_maximum_fusion), calls=%async_computation | async-start | bytes 10485760 | tf_op jit(solution)/shard_map/all_to_all | solution.py:88
  82.3 147.8 %all-gather.4.cloned.1.call-start = ((), (), s32[]{:S(2)}) async-start(), calls=%async_computation.4 | async-start | bytes 5570560 | tf_op jit(solution)/shard_map/all_gather | solution.py:91
  82.3 78.2 %slice-start.4 = ((bf16[16,40,256]{2,1,0:T(8,128)(2,1)}), bf16[16,16,256]{2,1,0:T(8,128)(2,1)S(1)}, s32[]{:S(2)}) async-start(bf16[16,40,256]{2,1,0:T(8,128)(2,1)} %copy-done), calls=%async_computation.10 | async-start | bytes 262144 | tf_op jit(solution)/shard_map/slice | solution.py:73
  82.3 78.2 %slice-start.5 = ((bf16[16,40,256]{2,1,0:T(8,128)(2,1)}), bf16[16,24,256]{2,1,0:T(8,128)(2,1)S(1)}, s32[]{:S(2)}) async-start(bf16[16,40,256]{2,1,0:T(8,128)(2,1)} %copy-done), calls=%async_computation.11 | async-start | bytes 393216 | tf_op jit(solution)/shard_map/slice | solution.py:74
  230.1 1.9 slice-start.2
  232.0 1.6 slice-start.3
  232.3 1.5 copy-start.6
  233.8 3.0 %slice-start = ((s8[4718592]{0:T(1024)(128)(4,1)}), s8[4194304]{0:T(1024)(128)(4,1)S(1)}, s32[]{:S(2)}) async-start(s8[4718592]{0:T(1024)(128)(4,1)} %bitcast.45), calls=%async_computation.6 | async-start | bytes 8388608
  233.8 3.1 %slice-start.1 = ((s8[4718592]{0:T(1024)(128)(4,1)}), s8[524288]{0:T(1024)(128)(4,1)S(1)}, s32[]{:S(2)}) async-start(s8[4718592]{0:T(1024)(128)(4,1)} %bitcast.45), calls=%async_computation.7 | async-start | bytes 1048576
  236.6 44.2 %copy-start.5 = (f32[320,256]{1,0:T(8,128)}, f32[320,256]{1,0:T(8,128)S(1)}, u32[]{:S(2)}) copy-start(f32[320,256]{1,0:T(8,128)S(1)} %get-tuple-element.8) | copy-start | bytes 983044
  273.6 7.3 %copy-start.1 = (f32[320,256]{1,0:T(8,128)S(1)}, f32[320,256]{1,0:T(8,128)}, u32[]{:S(2)}) copy-start(f32[320,256]{1,0:T(8,128)} %param.15) | copy-start | bytes 983044
  273.6 7.3 %copy-start.2 = (f32[320,256]{1,0:T(8,128)S(1)}, f32[320,256]{1,0:T(8,128)}, u32[]{:S(2)}) copy-start(f32[320,256]{1,0:T(8,128)} %param.19) | copy-start | bytes 983044
  273.6 7.3 %copy-start.3 = (f32[320,256]{1,0:T(8,128)S(1)}, f32[320,256]{1,0:T(8,128)}, u32[]{:S(2)}) copy-start(f32[320,256]{1,0:T(8,128)} %param.17) | copy-start | bytes 983044
  273.6 7.3 %copy-start.4 = (f32[320,256]{1,0:T(8,128)S(1)}, f32[320,256]{1,0:T(8,128)}, u32[]{:S(2)}) copy-start(f32[320,256]{1,0:T(8,128)} %param.18) | copy-start | bytes 983044
Sparse Core Ops, SparseCore 0:
  10.8 55.2 all-gather.5
  161.5 68.5 all-gather.3

commit v2 on v1

--- a/solution.py
+++ b/solution.py
@@ -8,6 +8,7 @@
 D = 5120
 L = 128
 Q = 4096
+CORES = 2
 
 
 beta_first = 0.9
@@ -32,10 +33,14 @@
     return split.transpose(1, 0, 2, 3).reshape(groups, tiles * (span // groups), cols)
 
 
-def sum_everywhere(values, axis):
-    parts = lax.axis_size(axis)
-    sent = jnp.broadcast_to(values[None], (parts, *values.shape))
-    return jnp.sum(lax.all_to_all(sent, axis, 0, 0, tiled=True), axis=0)
+def exchange(sent, axis, groups, kept=()):
+    sent, kept = lax.optimization_barrier((sent, kept))
+    got = lax.all_to_all(sent, axis, 0, 0, tiled=True, axis_index_groups=groups)
+    return lax.optimization_barrier((got, kept))
+
+
+def everywhere(values, parts):
+    return jnp.broadcast_to(values[None], (parts, *values.shape))
 
 
 def on_device(
@@ -52,64 +57,87 @@
 ):
     replicas = lax.axis_size("replica")
     tiles = lax.axis_size("tile")
+    chips = replicas // CORES
+    core = lax.axis_index("replica") % CORES
+    stacks = [[CORES * z + c for z in range(chips)] for c in range(CORES)]
     pub = public_tokens.shape[0]
     priv = private_tokens.shape[0]
+    rows = weight.shape[0]
     cols = weight.shape[1]
+    wide = CORES * cols
     examples_here = token_counts.shape[1]
+    pub_rows = public_targets.shape[0]
+    priv_rows = private_targets.shape[0]
+
+    def partner(values):
+        swap = [(r, r ^ 1) for r in range(replicas)]
+        return lax.ppermute(values, "replica", swap)
 
     live = (
         jnp.arange(L, dtype=jnp.int32)[None, :] < token_counts[0][:, None]
     ).reshape(priv)
     live_tokens = jnp.where(live[:, None], private_tokens, jnp.zeros_like(private_tokens))
     local = jnp.concatenate([public_tokens.T, live_tokens.T], axis=1)
-    tokens = lax.all_gather(local, "replica", axis=0)
+    tokens = lax.all_gather(local, "replica", axis=0, axis_index_groups=stacks)
+
+    w_half = weight.astype(jnp.bfloat16)
+    w_wide = jnp.concatenate([w_half, partner(w_half)], axis=1)
 
     targets = jnp.concatenate([public_targets, private_targets], axis=0)
-    targets = targets.reshape(-1, replicas, cols).transpose(1, 0, 2)
-    targets = lax.all_to_all(targets, "replica", 0, 0, tiled=True)
-    pub_rows = public_targets.shape[0]
+    targets = targets.reshape(-1, chips, CORES, cols)
+    targets = jnp.where(core == 0, targets, targets[:, :, ::-1])
+    targets = targets.reshape(-1, chips, wide).transpose(1, 0, 2)
+    targets = lax.all_to_all(
+        targets, "replica", 0, 0, tiled=True, axis_index_groups=stacks
+    )
     targets = jnp.concatenate(
         [
-            targets[:, :pub_rows].reshape(pub, cols),
-            targets[:, pub_rows:].reshape(priv, cols),
+            targets[:, :pub_rows].reshape(chips * pub_rows, wide),
+            targets[:, pub_rows:].reshape(chips * priv_rows, wide),
         ],
         axis=0,
     )
 
     out = jnp.einsum(
-        "rfn,fc->rnc",
-        tokens,
-        weight.astype(jnp.bfloat16),
-        preferred_element_type=jnp.float32,
+        "zfn,fk->znk", tokens, w_wide, preferred_element_type=jnp.float32
     ).astype(jnp.bfloat16)
     sent = jnp.concatenate(
         [regroup(out[:, :pub], tiles), regroup(out[:, pub:], tiles)], axis=1
     )
-    got = lax.all_to_all(sent, "tile", 0, 0, tiled=True)
+    got, (targets, tokens) = exchange(sent, "tile", None, (targets, tokens))
     total = jnp.sum(got.astype(jnp.float32), axis=0)
     delta = (total - targets.astype(jnp.float32)).astype(jnp.bfloat16)
-    deltas = lax.all_gather(delta, "tile", axis=0)
-    public_delta = ungroup(deltas[:, :pub], replicas)
-    private_delta = ungroup(deltas[:, pub:], replicas)
+    deltas, (tokens, public_moment) = exchange(
+        everywhere(delta, tiles), "tile", None, (tokens, public_moment)
+    )
+    pub_all = chips * pub_rows
+    public_delta = ungroup(deltas[:, :pub_all], chips)
+    private_delta = ungroup(deltas[:, pub_all:], chips)
 
     public_grad = jnp.einsum(
-        "rfn,rnc->fc", tokens[:, :, :pub], public_delta, preferred_element_type=jnp.float32
-    ) / math.sqrt(pub * replicas)
+        "zfn,znk->fk", tokens[:, :, :pub], public_delta, preferred_element_type=jnp.float32
+    )
+    public_grad = (public_grad[:, :cols] + partner(public_grad[:, cols:])) / math.sqrt(
+        pub * replicas
+    )
     new_public = beta_public * public_moment + (1.0 - beta_public) * public_grad * public_grad
     precond = 1.0 / (jnp.sqrt(new_public) + public_epsilon)
+    precond_wide = jnp.concatenate([precond, partner(precond)], axis=1)
 
     grads = jnp.einsum(
-        "rfek,rekc->refc",
-        tokens[:, :, pub:].reshape(replicas, -1, examples_here, L),
-        private_delta.reshape(replicas, examples_here, L, cols),
+        "zfel,zelk->zefk",
+        tokens[:, :, pub:].reshape(chips, rows, examples_here, L),
+        private_delta.reshape(chips, examples_here, L, wide),
         preferred_element_type=jnp.float32,
     )
-    scaled = grads * precond
+    scaled = grads * precond_wide
     squares = jnp.sum(scaled * scaled, axis=(2, 3))
-    squares = sum_everywhere(sum_everywhere(squares, "tile"), "replica")
+    squares = jnp.sum(exchange(everywhere(squares, tiles), "tile", None)[0], axis=0)
+    squares = jnp.sum(exchange(everywhere(squares, chips), "replica", stacks)[0], axis=0)
     clip_norm = clip_factor * math.sqrt(L * D * Q)
     factors = clip_norm / jnp.maximum(jnp.sqrt(squares), clip_norm)
-    summed = precond * jnp.sum(factors[:, :, None, None] * grads, axis=(0, 1))
+    summed = jnp.sum(factors[:, :, None, None] * grads, axis=(0, 1))
+    summed = precond * (summed[:, :cols] + partner(summed[:, cols:]))
 
     examples_total = examples_here * replicas
     noise_scale = noise_level * clip_factor * math.sqrt(L)

time: 290 us -> 276 us (0.952)
  waiting for transfers between devices: 176 us -> 43.6 us
  blocking collectives: 27.7 us -> 152 us
  matrix products: 17.4 us -> 12.7 us
    all_to_all x2 -> x4, blocking collectives: 27.7 us -> 152 us  [exchange(): got = lax.all_to_all(sent, axis, 0, 0, tiled=True, axis_index_groups=groups)]
    all_gather x2 -> x1, waiting for transfers between devices: 101 us -> 25.9 us  [on_device(): tokens = lax.all_gather(local, 'replica', axis=0, axis_index_groups=stacks)]
    all_to_all x2 -> x1, waiting for transfers between devices: 74.9 us -> 15.2 us  [on_device(): lax.all_to_all(targets, 'replica', 0, 0, tiled=True, axis_index_groups=st...]
    slice x10 -> x9, local copies, waits for them, and re-layouts: 14 us -> 6.08 us  [the longest x2 5.81 us: on_device(): tokens[:, :, pub:].reshape(chips, rows, examples_here, L)]
    all_to_all x2 -> x1, starting transfers between devices: 16.8 us -> 9 us  [on_device(): lax.all_to_all(targets, 'replica', 0, 0, tiled=True, axis_index_groups=st...]
    ppermute x0 -> x4, starting transfers between devices: none -> 7.62 us  [partner(): return lax.ppermute(values, 'replica', swap)]
    unnamed x19 -> x20, local copies, waits for them, and re-layouts: 0.33 us -> 5.69 us
    dot_general x3, matrix products: 17.4 us -> 12.7 us  [the longest x1 6.78 us: on_device(): jnp.einsum('zfel,zelk->zefk', tokens[:, :, pub:].reshape(chips, rows, exa...]
  transfers between devices with their start and end apart: 4 -> 6, of which waited for: 3 -> 4; matrix products, arithmetic and copies ran while one was open for 8% -> 4% of each run, Pallas kernels for 0% -> 0%
where the time goes in v2:
time: 276 us; the launch traced here: 275 us
  blocking collectives  152 us (55%)
  waiting for transfers between devices  43.6 us (16%)
  local copies, waits for them, and re-layouts  18.6 us (7%)
  other arithmetic  17.5 us (6%)
  starting transfers between devices  16.7 us (6%)
  between operations  14.3 us (5%)
  matrix products  12.7 us (5%)
    all_to_all x4, blocking collectives, exchange(): got = lax.all_to_all(sent, axis, 0, 0, tiled=True, axis_index_groups=groups)  152 us
    all_gather x1, waiting for transfers between devices, on_device(): tokens = lax.all_gather(local, 'replica', axis=0, axis_index_groups=stacks)  25.9 us
    all_to_all x1, waiting for transfers between devices, on_device(): lax.all_to_all(targets, 'replica', 0, 0, tiled=True, axis_index_groups=st...  15.2 us
    all_to_all x1, starting transfers between devices, on_device(): lax.all_to_all(targets, 'replica', 0, 0, tiled=True, axis_index_groups=st...  9 us
    reduce_sum x1, other arithmetic, on_device(): summed = jnp.sum(factors[:, :, None, None] * grads, axis=(0, 1))  7.78 us
    ppermute x4, starting transfers between devices, partner(): return lax.ppermute(values, 'replica', swap)  7.62 us
    dot_general x1, matrix products, on_device(): jnp.einsum('zfel,zelk->zefk', tokens[:, :, pub:].reshape(chips, rows, exa...  6.78 us
    slice x2, local copies, waits for them, and re-layouts, on_device(): tokens[:, :, pub:].reshape(chips, rows, examples_here, L)  5.81 us
  transfers between devices with their start and end apart: 6, of which 4 were waited for; matrix products, arithmetic and copies ran while one was open for 4% of the time, Pallas kernels for 0%

profile of v2, /device:TPU:1, one launch (start us, length us, event | category | flops | bytes accessed | tf_op | source)
XLA Modules:
  0.0 275.2 jit_solution(13952830898900686579)
XLA Ops:
  7.2 0.7 fusion.9
  7.9 1.0 select_bitcast_fusion
  9.0 1.7 pad_maximum_fusion.2
  10.7 1.0 pad_maximum_fusion.3
  12.2 2.2 rev.3
  14.8 0.9 reshape.73
  15.7 9.0 %all-to-all-start = ((bf16[8,40,512]{2,1,0:T(8,128)(2,1)}), bf16[8,40,512]{2,1,0:T(8,128)(2,1)S(1)}, u32[]{:S(2)}, u32[]{:S(2)}) async-start(bf16[8,40,512]{2,1,0:T(8,128)(2,1)} %bitcast.12), calls=%async_computation | async-start | bytes 655360 | tf_op jit(solution)/shard_map/all_to_all | solution.py:90
  24.7 1.0 collective-permute-start
  25.8 15.2 %all-to-all-done = bf16[8,40,512]{2,1,0:T(8,128)(2,1)S(1)} async-done(((bf16[8,40,512]{2,1,0:T(8,128)(2,1)}), bf16[8,40,512]{2,1,0:T(8,128)(2,1)S(1)}, u32[]{:S(2)}, u32[]{:S(2)}) %all-to-all-start) | async-done | bytes 327712 | tf_op jit(solution)/shard_map/all_to_all | solution.py:90
  41.0 25.9 %all-gather.3.cloned.1.call-done = bf16[2560,640]{1,0:T(8,128)(2,1)} async-done(((bf16[320,640]{1,0:T(8,128)(2,1)}), bf16[2560,640]{1,0:T(8,128)(2,1)}) %all-gather.3.cloned.1.call-update) | async-done | bytes 3276816 | tf_op jit(solution)/shard_map/all_gather | solution.py:81
  66.9 5.1 %convolution_convert_fusion = bf16[8,640,512]{2,1,0:T(8,128)(2,1)S(1)} fusion(bf16[8,320,640]{2,1,0:T(8,128)(2,1)} %bitcast.47, bf16[320,256]{1,0:T(8,128)(2,1)S(1)} %collective-permute-done, bf16[320,256]{1,0:T(8,128)(2,1)S(1)} %convert_element_type.15), kind=kOutput, calls=%fused_computation.4 | convolution fusion | flops 1680998400 | bytes 8847360 | tf_op jit(solution)/shard_map/zfn,fk->znk/dot_general | solution.py:101
  72.3 2.1 copy-done.2
  74.7 1.2 slice-done.1
  76.6 67.1 %all_to_all.25 = bf16[16,320,512]{2,1,0:T(8,128)(2,1)S(1)} all-to-all(bf16[16,320,512]{2,1,0:T(8,128)(2,1)S(1)} %pad_maximum_fusion), channel_id=1, replica_groups=mesh['replica'=16,'tile'=16] {'tile'}, dimensions={0} | all-to-all | bytes 10485760 | tf_op jit(solution)/shard_map/all_to_all | solution.py:38
  143.8 0.7 convert_reduce_fusion
  144.6 0.5 broadcast_in_dim.18
  145.1 64.3 %all_to_all.26 = bf16[16,320,512]{2,1,0:T(8,128)(2,1)S(1)} all-to-all(bf16[16,320,512]{2,1,0:T(8,128)(2,1)S(1)} %broadcast_in_dim.18), channel_id=1, replica_groups=mesh['replica'=16,'tile'=16] {'tile'}, dimensions={0} | all-to-all | bytes 10485760 | tf_op jit(solution)/shard_map/all_to_all | solution.py:38
  209.9 3.4 %copy-done.5 = bf16[2560,640]{1,0:T(8,128)(2,1)S(1)} copy-done((bf16[2560,640]{1,0:T(8,128)(2,1)S(1)}, bf16[2560,640]{1,0:T(8,128)(2,1)}, u32[]{:S(2)}) %copy-start.5) | copy-done | bytes 3276824
  213.2 0.8 fusion.2
  214.1 3.1 %collective-permute-start.1 = (f32[320,256]{1,0:T(8,128)S(1)}, f32[320,256]{1,0:T(8,128)S(1)}, u32[]{:S(2)}, u32[]{:S(2)}) collective-permute-start(f32[320,256]{1,0:T(8,128)S(1)} %slice.53), channel_id=1, source_target_pairs={{0,16},{16,0},{32,48},{48,32},{64,80},{80,64},{96,112},{112,96},{1... | collective-permute-start | bytes 983048 | tf_op jit(solution)/shard_map/ppermute | solution.py:74
  217.2 1.3 collective-permute-done.1
  218.5 1.0 add_divide_fusion
  219.9 1.6 slice.44
  221.4 4.2 %copy.36 = bf16[8,320,384]{1,2,0:T(8,128)(2,1)} copy(bf16[8,320,384]{2,1,0:T(8,128)(2,1)} %slice.44) | data formatting | bytes 3932160 | tf_op jit(solution)/shard_map/slice | solution.py:129
  226.0 1.3 pad_maximum_fusion.1
  227.5 6.8 %multiply_reduce_fusion.1 = (f32[8,3]{1,0:T(8,128)S(1)}, f32[8,3,320,512]{3,2,1,0:T(8,128)}) fusion(f32[320,512]{1,0:T(8,128)S(1)} %pad_maximum_fusion.1, bf16[8,320,3,128]{1,3,2,0:T(8,128)(2,1)S(1)} %bitcast.40, bf16[8,3,128,512]{3,2,1,0:T(8,128)(2,1)S(1)} %bitcast.39), kind=kOutput, calls=%fused_computation.1 | convolution fusion | flops 1018429440 | bytes 21495904 | tf_op jit(solution)/shard_map/zfel,zelk->zefk/dot_general | solution.py:127
  234.4 9.4 %all_to_all.27 = f32[16,8,3]{1,2,0:T(4,128)S(1)} all-to-all(f32[16,8,3]{1,2,0:T(4,128)S(1)} %broadcast_in_dim.19), channel_id=1, replica_groups=mesh['replica'=16,'tile'=16] {'tile'}, dimensions={0} | all-to-all | bytes 3072 | tf_op jit(solution)/shard_map/all_to_all | solution.py:38
  243.9 11.0 %all_to_all.28 = f32[8,8,3]{1,2,0:T(4,128)S(1)} all-to-all(f32[8,8,3]{1,2,0:T(4,128)S(1)} %broadcast_in_dim.20), channel_id=1, replica_groups={{0,32,64,96,128,160,192,224},{16,48,80,112,144,176,208,240},{1,33,65,97..., dimensions={0} | all-to-all | bytes 1536 | tf_op jit(solution)/shard_map/all_to_all | solution.py:38
  255.0 7.8 %multiply_reduce_fusion = f32[320,512]{1,0:T(8,128)S(1)} fusion(f32[8,3,320,512]{3,2,1,0:T(8,128)} %get-tuple-element.34, f32[8,3]{1,0:T(8,128)S(1)} %copy.40), kind=kLoop, calls=%fused_computation | loop fusion | flops 7700480 | bytes 16384096 | tf_op jit(solution)/shard_map/reduce_sum | solution.py:139
  262.8 3.1 %collective-permute-start.3 = (f32[320,256]{1,0:T(8,128)S(1)}, f32[320,256]{1,0:T(8,128)S(1)}, u32[]{:S(2)}, u32[]{:S(2)}) collective-permute-start(f32[320,256]{1,0:T(8,128)S(1)} %slice.55), channel_id=1, source_target_pairs={{0,16},{16,0},{32,48},{48,32},{64,80},{80,64},{96,112},{112,96},{1... | collective-permute-start | bytes 983048 | tf_op jit(solution)/shard_map/ppermute | solution.py:74
  265.9 1.3 collective-permute-done.3
  267.2 1.2 divide_subtract_fusion
  (50 shorter events, 3.9 us)
Async XLA Ops:
  7.2 59.8 %all-gather.3.cloned.1.call-start = ((), (), s32[]{:S(2)}) async-start(), calls=%async_computation.5 | async-start | bytes 3686400 | tf_op jit(solution)/shard_map/all_gather | solution.py:81
  7.9 16.8 %copy-start.3 = (f32[320,256]{1,0:T(8,128)S(1)}, f32[320,256]{1,0:T(8,128)}, u32[]{:S(2)}) copy-start(f32[320,256]{1,0:T(8,128)} %param.15) | copy-start | bytes 983044
  15.7 25.2 %all-to-all-start = ((bf16[8,40,512]{2,1,0:T(8,128)(2,1)}), bf16[8,40,512]{2,1,0:T(8,128)(2,1)S(1)}, u32[]{:S(2)}, u32[]{:S(2)}) async-start(bf16[8,40,512]{2,1,0:T(8,128)(2,1)} %bitcast.12), calls=%async_computation | async-start | bytes 655360 | tf_op jit(solution)/shard_map/all_to_all | solution.py:90
  24.7 16.3 %collective-permute-start = (bf16[320,256]{1,0:T(8,128)(2,1)S(1)}, bf16[320,256]{1,0:T(8,128)(2,1)S(1)}, u32[]{:S(2)}, u32[]{:S(2)}) collective-permute-start(bf16[320,256]{1,0:T(8,128)(2,1)S(1)} %convert_element_type.15), channel_id=1, source_target_pairs={{0,16},{16,0},{32,48},{48,32},{64,80},{80,64},{96,112},{112,96},{1... | collective-permute-start | bytes 491528 | tf_op jit(solution)/shard_map/ppermute | solution.py:74
  72.1 2.3 copy-start.2
  74.3 1.6 slice-start.1
  209.4 12.0 %copy-start = (bf16[16,320,512]{2,1,0:T(8,128)(2,1)}, bf16[16,320,512]{2,1,0:T(8,128)(2,1)S(1)}, u32[]{:S(2)}) copy-start(bf16[16,320,512]{2,1,0:T(8,128)(2,1)S(1)} %all_to_all.26) | copy-start | bytes 15728644
  209.4 3.8 %copy-start.5 = (bf16[2560,640]{1,0:T(8,128)(2,1)S(1)}, bf16[2560,640]{1,0:T(8,128)(2,1)}, u32[]{:S(2)}) copy-start(bf16[2560,640]{1,0:T(8,128)(2,1)} %all-gather.3.cloned.1.call-done) | copy-start | bytes 9830404
  209.9 8.6 %copy-start.9 = (f32[320,256]{1,0:T(8,128)S(1)}, f32[320,256]{1,0:T(8,128)}, u32[]{:S(2)}) copy-start(f32[320,256]{1,0:T(8,128)} %param.16) | copy-start | bytes 983044
  214.1 4.4 %collective-permute-start.1 = (f32[320,256]{1,0:T(8,128)S(1)}, f32[320,256]{1,0:T(8,128)S(1)}, u32[]{:S(2)}, u32[]{:S(2)}) collective-permute-start(f32[320,256]{1,0:T(8,128)S(1)} %slice.53), channel_id=1, source_target_pairs={{0,16},{16,0},{32,48},{48,32},{64,80},{80,64},{96,112},{112,96},{1... | collective-permute-start | bytes 983048 | tf_op jit(solution)/shard_map/ppermute | solution.py:74
  219.5 6.5 %collective-permute-start.2 = (f32[320,256]{1,0:T(8,128)}, f32[320,256]{1,0:T(8,128)}, u32[]{:S(2)}, u32[]{:S(2)}) collective-permute-start(f32[320,256]{1,0:T(8,128)} %get-tuple-element.31), channel_id=1, source_target_pairs={{0,16},{16,0},{32,48},{48,32},{64,80},{80,64},{96,112},{112,96},{1... | collective-permute-start | bytes 983048 | tf_op jit(solution)/shard_map/ppermute | solution.py:74
  221.4 4.3 %slice-start = ((bf16[16,320,512]{2,1,0:T(8,128)(2,1)}), bf16[16,192,512]{2,1,0:T(8,128)(2,1)S(1)}, s32[]{:S(2)}) async-start(bf16[16,320,512]{2,1,0:T(8,128)(2,1)} %copy-done), calls=%async_computation.6 | async-start | bytes 6291456 | tf_op jit(solution)/shard_map/slice | solution.py:115
  225.7 1.9 copy-start.1
  255.0 12.2 %copy-start.4 = (f32[320,256]{1,0:T(8,128)S(1)}, f32[320,256]{1,0:T(8,128)}, u32[]{:S(2)}) copy-start(f32[320,256]{1,0:T(8,128)} %get-tuple-element.32) | copy-start | bytes 983044
  255.0 12.2 %copy-start.6 = (f32[320,256]{1,0:T(8,128)S(1)}, f32[320,256]{1,0:T(8,128)}, u32[]{:S(2)}) copy-start(f32[320,256]{1,0:T(8,128)} %param.17) | copy-start | bytes 983044
  255.0 12.2 %copy-start.7 = (f32[320,256]{1,0:T(8,128)S(1)}, f32[320,256]{1,0:T(8,128)}, u32[]{:S(2)}) copy-start(f32[320,256]{1,0:T(8,128)} %param.18) | copy-start | bytes 983044
  255.0 12.2 %copy-start.8 = (f32[320,256]{1,0:T(8,128)S(1)}, f32[320,256]{1,0:T(8,128)}, u32[]{:S(2)}) copy-start(f32[320,256]{1,0:T(8,128)} %param.19) | copy-start | bytes 983044
  262.8 4.3 %collective-permute-start.3 = (f32[320,256]{1,0:T(8,128)S(1)}, f32[320,256]{1,0:T(8,128)S(1)}, u32[]{:S(2)}, u32[]{:S(2)}) collective-permute-start(f32[320,256]{1,0:T(8,128)S(1)} %slice.55), channel_id=1, source_target_pairs={{0,16},{16,0},{32,48},{48,32},{64,80},{80,64},{96,112},{112,96},{1... | collective-permute-start | bytes 983048 | tf_op jit(solution)/shard_map/ppermute | solution.py:74
Sparse Core Ops, SparseCore 0:
  10.8 56.0 all-gather.2

commit v3 on v1

v3 whole, which is shorter than its diff:
```python
import math

import jax
import jax.numpy as jnp
from jax import lax
from jax.sharding import PartitionSpec as P

D = 5120
L = 128
Q = 4096
CORES = 2
SIDE = 4


beta_first = 0.9
beta_second = 0.99
beta_public = 0.9
public_epsilon = 0.001
adam_epsilon = 1e-08
clip_factor = 0.6
noise_level = 4.0
learn_rate = 0.01


def exchange(sent, axis, groups, kept=()):
    sent, kept = lax.optimization_barrier((sent, kept))
    got = lax.all_to_all(sent, axis, 0, 0, tiled=True, axis_index_groups=groups)
    return lax.optimization_barrier((got, kept))


def everywhere(values, parts):
    return jnp.broadcast_to(values[None], (parts, *values.shape))


def to_class(replicas):
    tiles = SIDE * SIDE
    moves = []
    for replica in range(replicas):
        quad, inner = divmod(replica, CORES * 2)
        odd, core = divmod(inner, CORES)
        for tile in range(tiles):
            x, y = divmod(tile, SIDE)
            target = (quad * SIDE + x) * tiles + (odd + 2 * core) * SIDE + y
            moves.append((replica * tiles + tile, target))
    return moves


def on_device(
    public_tokens,
    public_targets,
    private_tokens,
    private_targets,
    token_counts,
    weight,
    public_moment,
    adam_first,
    adam_second,
    noise_draw,
):
    replicas = lax.axis_size("replica")
    along_x = [[x * SIDE + y for x in range(SIDE)] for y in range(SIDE)]
    along_y = [[x * SIDE + y for y in range(SIDE)] for x in range(SIDE)]
    quads = replicas // SIDE
    pub = public_tokens.shape[0]
    priv = private_tokens.shape[0]
    rows, cols = weight.shape
    examples_here = token_counts.shape[1]
    pub_rows = public_targets.shape[0]
    priv_rows = private_targets.shape[0]
    pub_all = quads * SIDE * pub_rows
    priv_all = quads * SIDE * priv_rows
    moves = to_class(replicas)

    live = (
        jnp.arange(L, dtype=jnp.int32)[None, :] < token_counts[0][:, None]
    ).reshape(priv)
    live_tokens = jnp.where(live[:, None], private_tokens, jnp.zeros_like(private_tokens))
    local = jnp.concatenate([public_tokens.T, live_tokens.T], axis=1)
    local = lax.ppermute(local, ("replica", "tile"), moves)
    tokens = lax.all_gather(local, "replica", axis=0)
    tokens = tokens.reshape(quads, SIDE, rows, pub + priv)

    w_half = weight.astype(jnp.bfloat16)
    w_group = lax.all_to_all(
        everywhere(w_half, SIDE), "tile", 0, 0, tiled=True, axis_index_groups=along_x
    )

    targets = jnp.concatenate([public_targets, private_targets], axis=0)
    targets = lax.ppermute(targets, ("replica", "tile"), moves)
    targets = targets.reshape(-1, replicas, cols).transpose(1, 0, 2)
    targets = lax.all_to_all(targets, "replica", 0, 0, tiled=True)
    targets = jnp.concatenate(
        [
            targets[:, :pub_rows].reshape(pub_all, cols),
            targets[:, pub_rows:].reshape(priv_all, cols),
        ],
        axis=0,
    )

    def by_owner(part, span):
        part = part.reshape(quads, SIDE, SIDE, span, cols)
        return part.transpose(2, 0, 1, 3, 4).reshape(SIDE, quads * SIDE * span, cols)

    def by_token(part, span):
        part = part.reshape(SIDE, quads, SIDE, span, cols)
        return part.transpose(1, 2, 0, 3, 4).reshape(quads, SIDE * SIDE * span, cols)

    out = jnp.einsum(
        "qxfn,xfk->qnk", tokens, w_group, preferred_element_type=jnp.float32
    ).astype(jnp.bfloat16)
    sent = jnp.concatenate(
        [by_owner(out[:, :pub], pub_rows), by_owner(out[:, pub:], priv_rows)], axis=1
    )
    got, (targets, tokens) = exchange(sent, "tile", along_y, (targets, tokens))
    total = jnp.sum(got.astype(jnp.float32), axis=0)
    delta = (total - targets.astype(jnp.float32)).astype(jnp.bfloat16)
    deltas, (tokens, public_moment) = exchange(
        everywhere(delta, SIDE), "tile", along_y, (tokens, public_moment)
    )
    public_delta = by_token(deltas[:, :pub_all], pub_rows)
    private_delta = by_token(deltas[:, pub_all:], priv_rows)

    def over_classes(part):
        got, _ = exchange(part.astype(jnp.bfloat16), "tile", along_x)
        return jnp.sum(got.astype(jnp.float32), axis=0)

    public_grad = over_classes(
        jnp.einsum(
            "qxfn,qnk->xfk",
            tokens[:, :, :, :pub],
            public_delta,
            preferred_element_type=jnp.float32,
        )
    ) / math.sqrt(pub * replicas)
    new_public = beta_public * public_moment + (1.0 - beta_public) * public_grad * public_grad
    precond = 1.0 / (jnp.sqrt(new_public) + public_epsilon)
    precond_group, _ = exchange(
        everywhere(precond.astype(jnp.bfloat16), SIDE), "tile", along_x
    )

    grads = jnp.einsum(
        "qxfel,qelk->qexfk",
        tokens[:, :, :, pub:].reshape(quads, SIDE, rows, examples_here, L),
        private_delta.reshape(quads, examples_here, L, cols),
        preferred_element_type=jnp.float32,
    )
    scaled = grads * precond_group.astype(jnp.float32)
    squares = jnp.sum(scaled * scaled, axis=(2, 3, 4))
    squares = jnp.sum(exchange(everywhere(squares, SIDE), "tile", along_y)[0], axis=0)
    squares = jnp.sum(exchange(everywhere(squares, replicas), "replica", None)[0], axis=0)
    clip_norm = clip_factor * math.sqrt(L * D * Q)
    factors = clip_norm / jnp.maximum(jnp.sqrt(squares), clip_norm)
    summed = jnp.sum(factors[:, :, None, None, None] * grads, axis=(0, 1))
    summed = precond * over_classes(summed)

    examples_total = examples_here * replicas
    noise_scale = noise_level * clip_factor * math.sqrt(L)
    gradient = (summed + noise_scale * noise_draw) / examples_total
    new_first = beta_first * adam_first + (1.0 - beta_first) * gradient
    new_second = beta_second * adam_second + (1.0 - beta_second) * gradient * gradient
    first_hat = new_first / (1.0 - beta_first**2)
    second_hat = new_second / (1.0 - beta_second**2)
    new_weight = weight - learn_rate * first_hat / (jnp.sqrt(second_hat) + adam_epsilon)
    return (new_weight, new_first, new_second, new_public)


def solution(mesh):
    placed = (
        P("replica", "tile"),
        P(("replica", "tile"), None),
        P("replica", "tile"),
        P(("replica", "tile"), None),
        P("replica", None),
        P("tile", "replica"),
        P("tile", "replica"),
        P("tile", "replica"),
        P("tile", "replica"),
        P("tile", "replica"),
    )
    return jax.shard_map(
        on_device,
        mesh=mesh,
        in_specs=placed,
        out_specs=(
            P("tile", "replica"),
            P("tile", "replica"),
            P("tile", "replica"),
            P("tile", "replica"),
        ),
        check_vma=False,
    )
```

time: 290 us -> 226 us (0.78)
  waiting for transfers between devices: 176 us -> 43.7 us
  blocking collectives: 27.7 us -> 88.8 us
  starting transfers between devices: 16.9 us -> 31 us
  other arithmetic: 19.7 us -> 12.8 us
    all_to_all x1 -> x2, waiting for transfers between devices: 74.9 us -> 10.6 us  [the longest x1 10.6 us: on_device(): lax.all_to_all(everywhere(w_half, SIDE), 'tile', 0, 0, tiled=True, axis_i...]
    all_to_all x2 -> x6, blocking collectives: 27.7 us -> 88.8 us  [exchange(): got = lax.all_to_all(sent, axis, 0, 0, tiled=True, axis_index_groups=groups)]
    all_gather x1 -> x0, waiting for transfers between devices: 57.9 us -> none  [on_device(): deltas = lax.all_gather(delta, 'tile', axis=0)]
    all_gather x1, waiting for transfers between devices: 43.5 us -> 0.01 us  [on_device(): tokens = lax.all_gather(local, 'replica', axis=0)]
    ppermute x0 -> x2, waiting for transfers between devices: none -> 16.7 us  [the longest x1 9.2 us: on_device(): local = lax.ppermute(local, ('replica', 'tile'), moves)]
    all_to_all x1, waiting for transfers between devices: 0.01 us -> 16.3 us  [on_device(): targets = lax.all_to_all(targets, 'replica', 0, 0, tiled=True)]
    ppermute x0 -> x2, starting transfers between devices: none -> 11.9 us  [the longest x1 6.03 us: on_device(): local = lax.ppermute(local, ('replica', 'tile'), moves)]
    reduce_sum x1, other arithmetic: 3.28 us -> 0.19 us  [on_device(): total = jnp.sum(got.astype(jnp.float32), axis=0)]
  transfers between devices with their start and end apart: 4 -> 6, of which waited for: 3 -> 4; matrix products, arithmetic and copies ran while one was open for 8% -> 6% of each run, Pallas kernels for 0% -> 0%
where the time goes in v3:
time: 226 us; the launch traced here: 225 us
  blocking collectives  88.8 us (39%)
  waiting for transfers between devices  43.7 us (19%)
  starting transfers between devices  31 us (14%)
  matrix products  19.1 us (8%)
  local copies, waits for them, and re-layouts  15.1 us (7%)
  between operations  14.3 us (6%)
  other arithmetic  12.8 us (6%)
    all_to_all x6, blocking collectives, exchange(): got = lax.all_to_all(sent, axis, 0, 0, tiled=True, axis_index_groups=groups)  88.8 us
    all_to_all x1, waiting for transfers between devices, on_device(): targets = lax.all_to_all(targets, 'replica', 0, 0, tiled=True)  16.3 us
    dot_general x1, matrix products, on_device(): jnp.einsum('qxfel,qelk->qexfk', tokens[:, :, :, pub:].reshape(quads, SIDE...  11.3 us
    slice x2, local copies, waits for them, and re-layouts, on_device(): tokens[:, :, :, pub:].reshape(quads, SIDE, rows, examples_here, L)  11 us
    all_to_all x1, starting transfers between devices, on_device(): targets = lax.all_to_all(targets, 'replica', 0, 0, tiled=True)  10.9 us
    all_to_all x1, waiting for transfers between devices, on_device(): lax.all_to_all(everywhere(w_half, SIDE), 'tile', 0, 0, tiled=True, axis_i...  10.6 us
    ppermute x1, waiting for transfers between devices, on_device(): local = lax.ppermute(local, ('replica', 'tile'), moves)  9.2 us
    ppermute x1, waiting for transfers between devices, on_device(): targets = lax.ppermute(targets, ('replica', 'tile'), moves)  7.51 us
  transfers between devices with their start and end apart: 6, of which 4 were waited for; matrix products, arithmetic and copies ran while one was open for 6% of the time, Pallas kernels for 0%

profile of v3, /device:TPU:1, one launch (start us, length us, event | category | flops | bytes accessed | tf_op | source)
XLA Modules:
  0.0 224.7 jit_solution(8206492310850571064)
XLA Ops:
  7.2 0.8 fusion.12
  8.0 1.0 select_bitcast_fusion
  9.0 1.0 pad_maximum_fusion.1
  9.9 6.0 %collective-permute-start = (bf16[320,640]{1,0:T(8,128)(2,1)S(1)}, bf16[320,640]{1,0:T(8,128)(2,1)S(1)}, u32[]{:S(2)}, u32[]{:S(2)}) collective-permute-start(bf16[320,640]{1,0:T(8,128)(2,1)S(1)} %pad_maximum_fusion.1), channel_id=1, source_target_pairs={{0,0},{1,1},{2,2},{3,3},{4,16},{5,17},{6,18},{7,19},{8,32},{9,33},... | collective-permute-start | bytes 1228808 | tf_op jit(solution)/shard_map/ppermute | solution.py:79
  16.0 9.2 %collective-permute-done = bf16[320,640]{1,0:T(8,128)(2,1)S(1)} collective-permute-done((bf16[320,640]{1,0:T(8,128)(2,1)S(1)}, bf16[320,640]{1,0:T(8,128)(2,1)S(1)}, u32[]{:S(2)}, u32[]{:S(2)}) %collective-permute-start) | collective-permute-done | bytes 409632 | tf_op jit(solution)/shard_map/ppermute | solution.py:79
  25.2 0.8 copy-done.3
  26.0 1.0 pad_maximum_fusion.2
  27.0 5.9 %collective-permute-start.1 = (bf16[40,4096]{1,0:T(8,128)(2,1)S(1)}, bf16[40,4096]{1,0:T(8,128)(2,1)S(1)}, u32[]{:S(2)}, u32[]{:S(2)}) collective-permute-start(bf16[40,4096]{1,0:T(8,128)(2,1)S(1)} %pad_maximum_fusion.2), channel_id=1, source_target_pairs={{0,0},{1,1},{2,2},{3,3},{4,16},{5,17},{6,18},{7,19},{8,32},{9,33},... | collective-permute-start | bytes 983048 | tf_op jit(solution)/shard_map/ppermute | solution.py:89
  32.9 7.5 %collective-permute-done.1 = bf16[40,4096]{1,0:T(8,128)(2,1)S(1)} collective-permute-done((bf16[40,4096]{1,0:T(8,128)(2,1)S(1)}, bf16[40,4096]{1,0:T(8,128)(2,1)S(1)}, u32[]{:S(2)}, u32[]{:S(2)}) %collective-permute-start.1) | collective-permute-done | bytes 327712 | tf_op jit(solution)/shard_map/ppermute | solution.py:89
  40.5 0.8 copy.40
  41.3 10.9 %all-to-all-start.1 = ((bf16[16,40,256]{2,1,0:T(8,128)(2,1)}), bf16[16,40,256]{2,1,0:T(8,128)(2,1)S(1)}, u32[]{:S(2)}, u32[]{:S(2)}) async-start(bf16[16,40,256]{2,1,0:T(8,128)(2,1)} %copy.40), calls=%async_computation.1 | async-start | bytes 655360 | tf_op jit(solution)/shard_map/all_to_all | solution.py:91
  52.3 16.3 %all-to-all-done.1 = bf16[16,40,256]{2,1,0:T(8,128)(2,1)S(1)} async-done(((bf16[16,40,256]{2,1,0:T(8,128)(2,1)}), bf16[16,40,256]{2,1,0:T(8,128)(2,1)S(1)}, u32[]{:S(2)}, u32[]{:S(2)}) %all-to-all-start.1) | async-done | bytes 327712 | tf_op jit(solution)/shard_map/all_to_all | solution.py:91
  68.6 0.9 broadcast_in_dim.22
  69.5 4.6 %all-to-all-start = ((bf16[4,320,256]{2,1,0:T(8,128)(2,1)}), bf16[4,320,256]{2,1,0:T(8,128)(2,1)S(1)}, u32[]{:S(2)}, u32[]{:S(2)}) async-start(bf16[4,320,256]{2,1,0:T(8,128)(2,1)} %broadcast_in_dim.22), calls=%async_computation | async-start | bytes 1310720 | tf_op jit(solution)/shard_map/all_to_all | solution.py:84
  74.2 10.6 %all-to-all-done = bf16[4,320,256]{2,1,0:T(8,128)(2,1)S(1)} async-done(((bf16[4,320,256]{2,1,0:T(8,128)(2,1)}), bf16[4,320,256]{2,1,0:T(8,128)(2,1)S(1)}, u32[]{:S(2)}, u32[]{:S(2)}) %all-to-all-start) | async-done | bytes 655392 | tf_op jit(solution)/shard_map/all_to_all | solution.py:84
  84.8 4.8 %bitcast_convert_fusion = bf16[4,640,256]{2,1,0:T(8,128)(2,1)S(1)} fusion(bf16[4,4,320,640]{3,2,1,0:T(8,128)(2,1)} %bitcast.56, bf16[4,320,256]{2,1,0:T(8,128)(2,1)S(1)} %all-to-all-done), kind=kOutput, calls=%fused_computation.4 | convolution fusion | flops 1678376960 | bytes 8519680 | tf_op jit(solution)/shard_map/qxfn,xfk->qnk/dot_general | solution.py:108
  89.9 20.1 %all_to_all.45 = bf16[4,640,256]{2,1,0:T(8,128)(2,1)S(1)} all-to-all(bf16[4,640,256]{2,1,0:T(8,128)(2,1)S(1)} %pad_maximum_fusion), channel_id=1, replica_groups={{0,1,2,3},{4,5,6,7},{8,9,10,11},{12,13,14,15},{16,17,18,19},{20,21,22,2..., dimensions={0} | all-to-all | bytes 2621440 | tf_op jit(solution)/shard_map/all_to_all | solution.py:27
  110.1 0.2 convert_reduce_fusion
  110.5 17.8 %all_to_all.46 = bf16[4,640,256]{2,1,0:T(8,128)(2,1)S(1)} all-to-all(bf16[4,640,256]{2,1,0:T(8,128)(2,1)S(1)} %broadcast_in_dim.23), channel_id=1, replica_groups={{0,1,2,3},{4,5,6,7},{8,9,10,11},{12,13,14,15},{16,17,18,19},{20,21,22,2..., dimensions={0} | all-to-all | bytes 2621440 | tf_op jit(solution)/shard_map/all_to_all | solution.py:27
  128.4 3.0 %fusion.7 = bf16[4,320,256]{2,1,0:T(8,128)(2,1)S(1)} fusion(bf16[4,256,256,1]{2,1,3,0:T(8,128)(2,1)S(1)} %bitcast.65, bf16[4,4,320,640]{3,2,1,0:T(8,128)(2,1)} %bitcast.57), kind=kOutput, calls=%fused_computation.9 | convolution fusion | flops 671416320 | bytes 3801088 | tf_op jit(solution)/shard_map/qxfn,qnk->xfk/dot_general | solution.py:128
  131.3 13.5 %all_to_all.47 = bf16[4,320,256]{2,1,0:T(8,128)(2,1)S(1)} all-to-all(bf16[4,320,256]{2,1,0:T(8,128)(2,1)S(1)} %fusion.7), channel_id=1, replica_groups={{0,4,8,12},{1,5,9,13},{2,6,10,14},{3,7,11,15},{16,20,24,28},{17,21,25,2..., dimensions={0} | all-to-all | bytes 1310720 | tf_op jit(solution)/shard_map/all_to_all | solution.py:27
  145.0 0.2 fusion.11
  145.2 0.9 broadcast_in_dim.24
  146.1 3.5 %all-to-all-start.5 = ((bf16[4,320,256]{2,1,0:T(8,128)(2,1)}), bf16[4,320,256]{2,1,0:T(8,128)(2,1)S(1)}, u32[]{:S(2)}, u32[]{:S(2)}) async-start(bf16[4,320,256]{2,1,0:T(8,128)(2,1)} %broadcast_in_dim.24), calls=%async_computation.5 | async-start | bytes 1310720 | tf_op jit(solution)/shard_map/all_to_all | solution.py:27
  149.6 4.6 %slice.30 = bf16[4,4,320,384]{3,2,1,0:T(8,128)(2,1)} slice(bf16[4,4,320,640]{3,2,1,0:T(8,128)(2,1)} %bitcast.58), slice={[0:4], [0:4], [0:320], [256:640]} | slice | bytes 7864320 | tf_op jit(solution)/shard_map/slice | solution.py:143
  154.3 6.4 %copy.42 = bf16[4,4,320,384]{2,3,1,0:T(8,128)(2,1)} copy(bf16[4,4,320,384]{3,2,1,0:T(8,128)(2,1)} %slice.30) | data formatting | bytes 7864320 | tf_op jit(solution)/shard_map/slice | solution.py:143
  160.8 11.3 %multiply_reduce_fusion.1 = (f32[4,3]{1,0:T(4,128)S(1)}, f32[4,3,4,320,256]{4,3,2,1,0:T(8,128)}) fusion(f32[4,320,256]{2,1,0:T(8,128)S(1)} %convert_element_type.41, bf16[4,3,128,256,1]{3,2,4,1,0:T(8,128)(2,1)S(1)} %bitcast.53, bf16[4,4,320,3,128]{2,4,3,1,0:T(8,128)(2,1)} %bitcast.51), kind=kOutput, calls=%fused_computation.1 | convolution fusion | flops 1018429440 | bytes 21758000 | tf_op jit(solution)/shard_map/qxfel,qelk->qexfk/dot_general | solution.py:141
  172.2 6.5 %all_to_all.48 = f32[4,4,3]{2,1,0:T(4,128)S(1)} all-to-all(f32[4,4,3]{2,1,0:T(4,128)S(1)} %broadcast_in_dim.25), channel_id=1, replica_groups={{0,1,2,3},{4,5,6,7},{8,9,10,11},{12,13,14,15},{16,17,18,19},{20,21,22,2..., dimensions={0} | all-to-all | bytes 384 | tf_op jit(solution)/shard_map/all_to_all | solution.py:27
  178.7 16.6 %all_to_all.49 = f32[16,4,3]{2,1,0:T(4,128)S(1)} all-to-all(f32[16,4,3]{2,1,0:T(4,128)S(1)} %broadcast_in_dim.26), channel_id=1, replica_groups=mesh['replica'=16,'tile'=16] {'replica'}, dimensions={0} | all-to-all | bytes 1536 | tf_op jit(solution)/shard_map/all_to_all | solution.py:27
  195.3 6.9 %multiply_reduce_fusion = bf16[4,320,256]{2,1,0:T(8,128)(2,1)S(1)} fusion(f32[4,3,4,320,256]{4,3,2,1,0:T(8,128)} %get-tuple-element.34, f32[4,3]{1,0:T(4,128)S(1)} %maximum_divide_fusion), kind=kLoop, calls=%fused_computation | loop fusion | flops 7536640 | bytes 16384048 | tf_op jit(solution)/shard_map/reduce_sum | solution.py:153
  202.3 14.3 %all_to_all.50 = bf16[4,320,256]{2,1,0:T(8,128)(2,1)S(1)} all-to-all(bf16[4,320,256]{2,1,0:T(8,128)(2,1)S(1)} %multiply_reduce_fusion), channel_id=1, replica_groups={{0,4,8,12},{1,5,9,13},{2,6,10,14},{3,7,11,15},{16,20,24,28},{17,21,25,2..., dimensions={0} | all-to-all | bytes 1310720 | tf_op jit(solution)/shard_map/all_to_all | solution.py:27
  216.7 1.2 divide_subtract_fusion
  (44 shorter events, 1.2 us)
Async XLA Ops:
  7.2 45.1 %copy-start.1 = (f32[320,256]{1,0:T(8,128)S(1)}, f32[320,256]{1,0:T(8,128)}, u32[]{:S(2)}) copy-start(f32[320,256]{1,0:T(8,128)} %param.15) | copy-start | bytes 983044
  7.2 77.6 %all-gather.3.cloned.1.call-start = ((), (), s32[]{:S(2)}) async-start(), calls=%async_computation.9 | async-start | bytes 6963200 | tf_op jit(solution)/shard_map/all_gather | solution.py:80
  9.9 15.2 %collective-permute-start = (bf16[320,640]{1,0:T(8,128)(2,1)S(1)}, bf16[320,640]{1,0:T(8,128)(2,1)S(1)}, u32[]{:S(2)}, u32[]{:S(2)}) collective-permute-start(bf16[320,640]{1,0:T(8,128)(2,1)S(1)} %pad_maximum_fusion.1), channel_id=1, source_target_pairs={{0,0},{1,1},{2,2},{3,3},{4,16},{5,17},{6,18},{7,19},{8,32},{9,33},... | collective-permute-start | bytes 1228808 | tf_op jit(solution)/shard_map/ppermute | solution.py:79
  25.2 0.8 copy-start.3
  27.0 13.4 %collective-permute-start.1 = (bf16[40,4096]{1,0:T(8,128)(2,1)S(1)}, bf16[40,4096]{1,0:T(8,128)(2,1)S(1)}, u32[]{:S(2)}, u32[]{:S(2)}) collective-permute-start(bf16[40,4096]{1,0:T(8,128)(2,1)S(1)} %pad_maximum_fusion.2), channel_id=1, source_target_pairs={{0,0},{1,1},{2,2},{3,3},{4,16},{5,17},{6,18},{7,19},{8,32},{9,33},... | collective-permute-start | bytes 983048 | tf_op jit(solution)/shard_map/ppermute | solution.py:89
  41.3 27.3 %all-to-all-start.1 = ((bf16[16,40,256]{2,1,0:T(8,128)(2,1)}), bf16[16,40,256]{2,1,0:T(8,128)(2,1)S(1)}, u32[]{:S(2)}, u32[]{:S(2)}) async-start(bf16[16,40,256]{2,1,0:T(8,128)(2,1)} %copy.40), calls=%async_computation.1 | async-start | bytes 655360 | tf_op jit(solution)/shard_map/all_to_all | solution.py:91
  69.5 15.3 %all-to-all-start = ((bf16[4,320,256]{2,1,0:T(8,128)(2,1)}), bf16[4,320,256]{2,1,0:T(8,128)(2,1)S(1)}, u32[]{:S(2)}, u32[]{:S(2)}) async-start(bf16[4,320,256]{2,1,0:T(8,128)(2,1)} %broadcast_in_dim.22), calls=%async_computation | async-start | bytes 1310720 | tf_op jit(solution)/shard_map/all_to_all | solution.py:84
  128.3 21.4 %copy-start = (bf16[4,640,256]{2,1,0:T(8,128)(2,1)}, bf16[4,640,256]{2,1,0:T(8,128)(2,1)S(1)}, u32[]{:S(2)}) copy-start(bf16[4,640,256]{2,1,0:T(8,128)(2,1)S(1)} %all_to_all.46) | copy-start | bytes 3932164
  128.3 16.6 %copy-start.4 = (f32[320,256]{1,0:T(8,128)S(1)}, f32[320,256]{1,0:T(8,128)}, u32[]{:S(2)}) copy-start(f32[320,256]{1,0:T(8,128)} %param.16) | copy-start | bytes 983044
  145.2 71.5 %copy-start.2 = (f32[320,256]{1,0:T(8,128)}, f32[320,256]{1,0:T(8,128)S(1)}, u32[]{:S(2)}) copy-start(f32[320,256]{1,0:T(8,128)S(1)} %get-tuple-element.32) | copy-start | bytes 983044
  146.1 14.6 %all-to-all-start.5 = ((bf16[4,320,256]{2,1,0:T(8,128)(2,1)}), bf16[4,320,256]{2,1,0:T(8,128)(2,1)S(1)}, u32[]{:S(2)}, u32[]{:S(2)}) async-start(bf16[4,320,256]{2,1,0:T(8,128)(2,1)} %broadcast_in_dim.24), calls=%async_computation.5 | async-start | bytes 1310720 | tf_op jit(solution)/shard_map/all_to_all | solution.py:27
  149.6 4.6 %slice-start = ((bf16[4,640,256]{2,1,0:T(8,128)(2,1)}), bf16[4,384,256]{2,1,0:T(8,128)(2,1)S(1)}, s32[]{:S(2)}) async-start(bf16[4,640,256]{2,1,0:T(8,128)(2,1)} %copy-done), calls=%async_computation.10 | async-start | bytes 1572864 | tf_op jit(solution)/shard_map/slice | solution.py:121
  195.3 21.3 %copy-start.5 = (f32[320,256]{1,0:T(8,128)S(1)}, f32[320,256]{1,0:T(8,128)}, u32[]{:S(2)}) copy-start(f32[320,256]{1,0:T(8,128)} %param.19) | copy-start | bytes 983044
  195.3 21.3 %copy-start.6 = (f32[320,256]{1,0:T(8,128)S(1)}, f32[320,256]{1,0:T(8,128)}, u32[]{:S(2)}) copy-start(f32[320,256]{1,0:T(8,128)} %param.17) | copy-start | bytes 983044
  195.3 21.3 %copy-start.7 = (f32[320,256]{1,0:T(8,128)S(1)}, f32[320,256]{1,0:T(8,128)}, u32[]{:S(2)}) copy-start(f32[320,256]{1,0:T(8,128)} %param.18) | copy-start | bytes 983044
Sparse Core Ops, SparseCore 0:
  26.1 58.5 all-gather.2

commit v4 on v3

--- a/solution.py
+++ b/solution.py
@@ -3,6 +3,8 @@
 import jax
 import jax.numpy as jnp
 from jax import lax
+from jax.experimental import pallas as pl
+from jax.experimental.pallas import tpu as pltpu
 from jax.sharding import PartitionSpec as P
 
 D = 5120
@@ -43,6 +45,91 @@
             target = (quad * SIDE + x) * tiles + (odd + 2 * core) * SIDE + y
             moves.append((replica * tiles + tile, target))
     return moves
+
+
+def norms_kernel(pub, tokens_ref, delta_ref, precond_ref, out_ref):
+    sides, rows = tokens_ref.shape[1], tokens_ref.shape[2]
+    examples = delta_ref.shape[1] // L
+    row_at = lax.broadcasted_iota(jnp.int32, out_ref.shape[1:], 0)
+    found = jnp.zeros(out_ref.shape[1:], jnp.float32)
+    for example in range(examples):
+        block_d = delta_ref[0, example * L : (example + 1) * L, :]
+        first = pub + example * L
+        acc = jnp.zeros((8, block_d.shape[1]), jnp.float32)
+        for side in range(sides):
+            grads = jnp.dot(
+                tokens_ref[0, side, :, first : first + L],
+                block_d,
+                preferred_element_type=jnp.float32,
+            )
+            scaled = grads * precond_ref[side].astype(jnp.float32)
+            acc = acc + jnp.sum((scaled * scaled).reshape(rows // 8, 8, -1), axis=0)
+        found = jnp.where(row_at == example, jnp.sum(acc), found)
+    out_ref[0] = found
+
+
+def example_squares(tokens, deltas, precond, pub):
+    quads, sides, rows, span = tokens.shape
+    priv, cols = deltas.shape[1:]
+    out = pl.pallas_call(
+        lambda *refs: norms_kernel(pub, *refs),
+        grid=(quads,),
+        in_specs=[
+            pl.BlockSpec((1, sides, rows, span), lambda q: (q, 0, 0, 0)),
+            pl.BlockSpec((1, priv, cols), lambda q: (q, 0, 0)),
+            pl.BlockSpec((sides, rows, cols), lambda q: (0, 0, 0)),
+        ],
+        out_specs=pl.BlockSpec((1, 8, L), lambda q: (q, 0, 0)),
+        out_shape=jax.ShapeDtypeStruct((quads, 8, L), jnp.float32),
+        name="example_squares",
+    )(tokens, deltas, precond)
+    return out[:, : priv // L, 0]
+
+
+def clipped_kernel(pub, factors_ref, tokens_ref, delta_ref, out_ref, acc_ref):
+    quad = pl.program_id(0)
+    examples = delta_ref.shape[1] // L
+    weighted = jnp.concatenate(
+        [
+            (
+                factors_ref[quad, example]
+                * delta_ref[0, example * L : (example + 1) * L, :].astype(jnp.float32)
+            ).astype(jnp.bfloat16)
+            for example in range(examples)
+        ],
+        axis=0,
+    )
+
+    @pl.when(quad == 0)
+    def _():
+        acc_ref[...] = jnp.zeros_like(acc_ref)
+
+    for side in range(tokens_ref.shape[1]):
+        acc_ref[side] += jnp.dot(
+            tokens_ref[0, side, :, pub:], weighted, preferred_element_type=jnp.float32
+        )
+
+    @pl.when(quad == pl.num_programs(0) - 1)
+    def _():
+        out_ref[...] = acc_ref[...].astype(out_ref.dtype)
+
+
+def clipped_sum(factors, tokens, deltas, pub):
+    quads, sides, rows, span = tokens.shape
+    priv, cols = deltas.shape[1:]
+    return pl.pallas_call(
+        lambda *refs: clipped_kernel(pub, *refs),
+        grid=(quads,),
+        in_specs=[
+            pl.BlockSpec(memory_space=pltpu.SMEM),
+            pl.BlockSpec((1, sides, rows, span), lambda q: (q, 0, 0, 0)),
+            pl.BlockSpec((1, priv, cols), lambda q: (q, 0, 0)),
+        ],
+        out_specs=pl.BlockSpec((sides, rows, cols), lambda q: (0, 0, 0)),
+        out_shape=jax.ShapeDtypeStruct((sides, rows, cols), jnp.bfloat16),
+        scratch_shapes=[pltpu.VMEM((sides, rows, cols), jnp.float32)],
+        name="clipped_sum",
+    )(factors, tokens, deltas)
 
 
 def on_device(
@@ -138,20 +225,14 @@
         everywhere(precond.astype(jnp.bfloat16), SIDE), "tile", along_x
     )
 
-    grads = jnp.einsum(
-        "qxfel,qelk->qexfk",
-        tokens[:, :, :, pub:].reshape(quads, SIDE, rows, examples_here, L),
-        private_delta.reshape(quads, examples_here, L, cols),
-        preferred_element_type=jnp.float32,
-    )
-    scaled = grads * precond_group.astype(jnp.float32)
-    squares = jnp.sum(scaled * scaled, axis=(2, 3, 4))
+    squares = example_squares(
+        tokens, private_delta, precond_group, pub
+    )
     squares = jnp.sum(exchange(everywhere(squares, SIDE), "tile", along_y)[0], axis=0)
     squares = jnp.sum(exchange(everywhere(squares, replicas), "replica", None)[0], axis=0)
     clip_norm = clip_factor * math.sqrt(L * D * Q)
     factors = clip_norm / jnp.maximum(jnp.sqrt(squares), clip_norm)
-    summed = jnp.sum(factors[:, :, None, None, None] * grads, axis=(0, 1))
-    summed = precond * over_classes(summed)
+    summed = precond * over_classes(clipped_sum(factors, tokens, private_delta, pub))
 
     examples_total = examples_here * replicas
     noise_scale = noise_level * clip_factor * math.sqrt(L)

time: 226 us -> 219 us (0.969)
  Pallas kernels: 0 us -> 12.5 us
  matrix products: 19.1 us -> 7.41 us
  local copies, waits for them, and re-layouts: 15.1 us -> 6.65 us
  other arithmetic: 12.8 us -> 6.3 us
  waiting for transfers between devices: 43.7 us -> 50.2 us
    pallas_call x0 -> x2, Pallas kernels: none -> 12.5 us  [the longest x1 6.75 us: example_squares(): pl.pallas_call(lambda *refs: norms_kernel(pub, *refs), grid=(quads,), in_...]
    dot_general x1 -> x0, matrix products: 11.3 us -> none  [on_device(): jnp.einsum('qxfel,qelk->qexfk', tokens[:, :, :, pub:].reshape(quads, SIDE...]
    slice x2 -> x1, local copies, waits for them, and re-layouts: 11 us -> 0.8 us  [example_squares(): return out[:, :priv // L, 0]]
    reduce_sum x1 -> x0, other arithmetic: 6.92 us -> none  [on_device(): summed = jnp.sum(factors[:, :, None, None, None] * grads, axis=(0, 1))]
    all_to_all x1, waiting for transfers between devices: 0.01 us -> 6.53 us  [exchange(): got = lax.all_to_all(sent, axis, 0, 0, tiled=True, axis_index_groups=groups)]
  transfers between devices with their start and end apart: 6 -> 6, of which waited for: 4 -> 5; matrix products, arithmetic and copies ran while one was open for 6% -> 2% of each run, Pallas kernels for 0% -> 0%
where the time goes in v4:
time: 219 us; the launch traced here: 218 us
  blocking collectives  89.7 us (41%)
  waiting for transfers between devices  50.2 us (23%)
  starting transfers between devices  31 us (14%)
  between operations  14.3 us (7%)
  Pallas kernels  12.5 us (6%)
  matrix products  7.41 us (3%)
  local copies, waits for them, and re-layouts  6.65 us (3%)
  other arithmetic  6.3 us (3%)
    all_to_all x6, blocking collectives, exchange(): got = lax.all_to_all(sent, axis, 0, 0, tiled=True, axis_index_groups=groups)  89.7 us
    all_to_all x1, waiting for transfers between devices, on_device(): targets = lax.all_to_all(targets, 'replica', 0, 0, tiled=True)  16.3 us
    all_to_all x1, starting transfers between devices, on_device(): targets = lax.all_to_all(targets, 'replica', 0, 0, tiled=True)  10.9 us
    all_to_all x1, waiting for transfers between devices, on_device(): lax.all_to_all(everywhere(w_half, SIDE), 'tile', 0, 0, tiled=True, axis_i...  10.6 us
    ppermute x1, waiting for transfers between devices, on_device(): local = lax.ppermute(local, ('replica', 'tile'), moves)  9.2 us
    ppermute x1, waiting for transfers between devices, on_device(): targets = lax.ppermute(targets, ('replica', 'tile'), moves)  7.51 us
    pallas_call x1, Pallas kernels, example_squares(): pl.pallas_call(lambda *refs: norms_kernel(pub, *refs), grid=(quads,), in_...  6.75 us
    all_to_all x1, waiting for transfers between devices, exchange(): got = lax.all_to_all(sent, axis, 0, 0, tiled=True, axis_index_groups=groups)  6.53 us
  transfers between devices with their start and end apart: 6, of which 5 were waited for; matrix products, arithmetic and copies ran while one was open for 2% of the time, Pallas kernels for 0%

profile of v4, /device:TPU:1, one launch (start us, length us, event | category | flops | bytes accessed | tf_op | source)
XLA Modules:
  0.0 218.1 jit_solution(4389370560876436906)
XLA Ops:
  7.2 0.8 fusion.10
  8.0 1.0 select_bitcast_fusion
  9.0 1.0 pad_maximum_fusion.1
  9.9 6.0 %collective-permute-start = (bf16[320,640]{1,0:T(8,128)(2,1)S(1)}, bf16[320,640]{1,0:T(8,128)(2,1)S(1)}, u32[]{:S(2)}, u32[]{:S(2)}) collective-permute-start(bf16[320,640]{1,0:T(8,128)(2,1)S(1)} %pad_maximum_fusion.1), channel_id=1, source_target_pairs={{0,0},{1,1},{2,2},{3,3},{4,16},{5,17},{6,18},{7,19},{8,32},{9,33},... | collective-permute-start | bytes 1228808 | tf_op jit(solution)/shard_map/ppermute | solution.py:166
  16.0 9.2 %collective-permute-done = bf16[320,640]{1,0:T(8,128)(2,1)S(1)} collective-permute-done((bf16[320,640]{1,0:T(8,128)(2,1)S(1)}, bf16[320,640]{1,0:T(8,128)(2,1)S(1)}, u32[]{:S(2)}, u32[]{:S(2)}) %collective-permute-start) | collective-permute-done | bytes 409632 | tf_op jit(solution)/shard_map/ppermute | solution.py:166
  25.2 0.8 copy-done.3
  26.0 1.0 pad_maximum_fusion.2
  27.0 5.9 %collective-permute-start.1 = (bf16[40,4096]{1,0:T(8,128)(2,1)S(1)}, bf16[40,4096]{1,0:T(8,128)(2,1)S(1)}, u32[]{:S(2)}, u32[]{:S(2)}) collective-permute-start(bf16[40,4096]{1,0:T(8,128)(2,1)S(1)} %pad_maximum_fusion.2), channel_id=1, source_target_pairs={{0,0},{1,1},{2,2},{3,3},{4,16},{5,17},{6,18},{7,19},{8,32},{9,33},... | collective-permute-start | bytes 983048 | tf_op jit(solution)/shard_map/ppermute | solution.py:176
  32.9 7.5 %collective-permute-done.1 = bf16[40,4096]{1,0:T(8,128)(2,1)S(1)} collective-permute-done((bf16[40,4096]{1,0:T(8,128)(2,1)S(1)}, bf16[40,4096]{1,0:T(8,128)(2,1)S(1)}, u32[]{:S(2)}, u32[]{:S(2)}) %collective-permute-start.1) | collective-permute-done | bytes 327712 | tf_op jit(solution)/shard_map/ppermute | solution.py:176
  40.5 0.8 copy.28
  41.3 10.9 %all-to-all-start.1 = ((bf16[16,40,256]{2,1,0:T(8,128)(2,1)}), bf16[16,40,256]{2,1,0:T(8,128)(2,1)S(1)}, u32[]{:S(2)}, u32[]{:S(2)}) async-start(bf16[16,40,256]{2,1,0:T(8,128)(2,1)} %copy.28), calls=%async_computation.1 | async-start | bytes 655360 | tf_op jit(solution)/shard_map/all_to_all | solution.py:178
  52.3 16.3 %all-to-all-done.1 = bf16[16,40,256]{2,1,0:T(8,128)(2,1)S(1)} async-done(((bf16[16,40,256]{2,1,0:T(8,128)(2,1)}), bf16[16,40,256]{2,1,0:T(8,128)(2,1)S(1)}, u32[]{:S(2)}, u32[]{:S(2)}) %all-to-all-start.1) | async-done | bytes 327712 | tf_op jit(solution)/shard_map/all_to_all | solution.py:178
  68.6 0.9 broadcast_in_dim.24
  69.5 4.6 %all-to-all-start = ((bf16[4,320,256]{2,1,0:T(8,128)(2,1)}), bf16[4,320,256]{2,1,0:T(8,128)(2,1)S(1)}, u32[]{:S(2)}, u32[]{:S(2)}) async-start(bf16[4,320,256]{2,1,0:T(8,128)(2,1)} %broadcast_in_dim.24), calls=%async_computation | async-start | bytes 1310720 | tf_op jit(solution)/shard_map/all_to_all | solution.py:171
  74.2 10.6 %all-to-all-done = bf16[4,320,256]{2,1,0:T(8,128)(2,1)S(1)} async-done(((bf16[4,320,256]{2,1,0:T(8,128)(2,1)}), bf16[4,320,256]{2,1,0:T(8,128)(2,1)S(1)}, u32[]{:S(2)}, u32[]{:S(2)}) %all-to-all-start) | async-done | bytes 655392 | tf_op jit(solution)/shard_map/all_to_all | solution.py:171
  84.8 4.8 %bitcast_convert_fusion = bf16[4,640,256]{2,1,0:T(8,128)(2,1)S(1)} fusion(bf16[4,4,320,640]{3,2,1,0:T(8,128)(2,1)} %bitcast.45, bf16[4,320,256]{2,1,0:T(8,128)(2,1)S(1)} %all-to-all-done), kind=kOutput, calls=%fused_computation | convolution fusion | flops 1678376960 | bytes 8519680 | tf_op jit(solution)/shard_map/qxfn,xfk->qnk/dot_general | solution.py:195
  89.9 20.1 %all_to_all.45 = bf16[4,640,256]{2,1,0:T(8,128)(2,1)S(1)} all-to-all(bf16[4,640,256]{2,1,0:T(8,128)(2,1)S(1)} %pad_maximum_fusion), channel_id=1, replica_groups={{0,1,2,3},{4,5,6,7},{8,9,10,11},{12,13,14,15},{16,17,18,19},{20,21,22,2..., dimensions={0} | all-to-all | bytes 2621440 | tf_op jit(solution)/shard_map/all_to_all | solution.py:29
  110.4 17.8 %all_to_all.46 = bf16[4,640,256]{2,1,0:T(8,128)(2,1)S(1)} all-to-all(bf16[4,640,256]{2,1,0:T(8,128)(2,1)S(1)} %broadcast_in_dim.25), channel_id=1, replica_groups={{0,1,2,3},{4,5,6,7},{8,9,10,11},{12,13,14,15},{16,17,18,19},{20,21,22,2..., dimensions={0} | all-to-all | bytes 2621440 | tf_op jit(solution)/shard_map/all_to_all | solution.py:29
  128.4 2.6 %fusion.5 = bf16[4,320,256]{2,1,0:T(8,128)(2,1)S(1)} fusion(bf16[4,256,256,1]{2,1,3,0:T(8,128)(2,1)S(1)} %bitcast.60, bf16[4,4,320,640]{3,2,1,0:T(8,128)(2,1)} %bitcast.46), kind=kOutput, calls=%fused_computation.5 | convolution fusion | flops 671416320 | bytes 3801088 | tf_op jit(solution)/shard_map/qxfn,qnk->xfk/dot_general | solution.py:215
  131.0 13.5 %all_to_all.47 = bf16[4,320,256]{2,1,0:T(8,128)(2,1)S(1)} all-to-all(bf16[4,320,256]{2,1,0:T(8,128)(2,1)S(1)} %fusion.5), channel_id=1, replica_groups={{0,4,8,12},{1,5,9,13},{2,6,10,14},{3,7,11,15},{16,20,24,28},{17,21,25,2..., dimensions={0} | all-to-all | bytes 1310720 | tf_op jit(solution)/shard_map/all_to_all | solution.py:29
  144.8 0.9 broadcast_in_dim.26
  145.7 3.5 %all-to-all-start.5 = ((bf16[4,320,256]{2,1,0:T(8,128)(2,1)}), bf16[4,320,256]{2,1,0:T(8,128)(2,1)S(1)}, u32[]{:S(2)}, u32[]{:S(2)}) async-start(bf16[4,320,256]{2,1,0:T(8,128)(2,1)} %broadcast_in_dim.26), calls=%async_computation.5 | async-start | bytes 1310720 | tf_op jit(solution)/shard_map/all_to_all | solution.py:29
  149.3 1.0 copy.30
  150.3 6.5 %all-to-all-done.5.refs_2_ = bf16[4,320,256]{2,1,0:T(8,128)(2,1)S(1)} async-done(((bf16[4,320,256]{2,1,0:T(8,128)(2,1)}), bf16[4,320,256]{2,1,0:T(8,128)(2,1)S(1)}, u32[]{:S(2)}, u32[]{:S(2)}) %all-to-all-start.5) | async-done | bytes 655392 | tf_op jit(solution)/shard_map/all_to_all | solution.py:29
  156.8 0.8 copy-done
  157.7 6.7 %example_squares.1 = f32[4,8,128]{2,1,0:T(8,128)} custom-call(bf16[4,4,320,640]{3,2,1,0:T(8,128)(2,1)} %bitcast.47, bf16[4,384,256]{2,1,0:T(8,128)(2,1)} %bitcast.49, bf16[4,320,256]{2,1,0:T(8,128)(2,1)} %copy-done), custom_call_target="tpu_custom_call" | custom-call | tf_op jit(solution)/shard_map/example_squares/pallas_call | solution.py:74
  164.4 0.8 slice_reduce_fusion
  165.2 6.5 %all_to_all.48 = f32[4,4,3]{2,1,0:T(4,128)S(1)} all-to-all(f32[4,4,3]{2,1,0:T(4,128)S(1)} %broadcast_in_dim.49), channel_id=1, replica_groups={{0,1,2,3},{4,5,6,7},{8,9,10,11},{12,13,14,15},{16,17,18,19},{20,21,22,2..., dimensions={0} | all-to-all | bytes 384 | tf_op jit(solution)/shard_map/all_to_all | solution.py:29
  171.7 17.8 %all_to_all.49 = f32[16,4,3]{2,1,0:T(4,128)S(1)} all-to-all(f32[16,4,3]{2,1,0:T(4,128)S(1)} %broadcast_in_dim.50), channel_id=1, replica_groups=mesh['replica'=16,'tile'=16] {'replica'}, dimensions={0} | all-to-all | bytes 1536 | tf_op jit(solution)/shard_map/all_to_all | solution.py:29
  190.1 5.7 %clipped_sum.1 = bf16[4,320,256]{2,1,0:T(8,128)(2,1)} custom-call(f32[4,3]{1,0:T(4,128)} %maximum_divide_fusion.refs_0_, bf16[4,4,320,640]{3,2,1,0:T(8,128)(2,1)} %bitcast.48, bf16[4,384,256]{2,1,0:T(8,128)(2,1)} %bitcast.50), custom_call_target="tpu_custom_call" | custom-call | tf_op jit(solution)/shard_map/clipped_sum/pallas_call | solution.py:120
  195.9 14.0 %all_to_all.50 = bf16[4,320,256]{2,1,0:T(8,128)(2,1)S(1)} all-to-all(bf16[4,320,256]{2,1,0:T(8,128)(2,1)} %clipped_sum.1), channel_id=1, replica_groups={{0,4,8,12},{1,5,9,13},{2,6,10,14},{3,7,11,15},{16,20,24,28},{17,21,25,2..., dimensions={0} | all-to-all | bytes 1310720 | tf_op jit(solution)/shard_map/all_to_all | solution.py:29
  210.0 1.2 divide_subtract_fusion
  (41 shorter events, 2.0 us)
Async XLA Ops:
  7.2 45.1 %copy-start.1 = (f32[320,256]{1,0:T(8,128)S(1)}, f32[320,256]{1,0:T(8,128)}, u32[]{:S(2)}) copy-start(f32[320,256]{1,0:T(8,128)} %param.15) | copy-start | bytes 983044
  7.2 77.6 %all-gather.3.cloned.1.call-start = ((), (), s32[]{:S(2)}) async-start(), calls=%async_computation.9 | async-start | bytes 6963200 | tf_op jit(solution)/shard_map/all_gather | solution.py:167
  9.9 15.2 %collective-permute-start = (bf16[320,640]{1,0:T(8,128)(2,1)S(1)}, bf16[320,640]{1,0:T(8,128)(2,1)S(1)}, u32[]{:S(2)}, u32[]{:S(2)}) collective-permute-start(bf16[320,640]{1,0:T(8,128)(2,1)S(1)} %pad_maximum_fusion.1), channel_id=1, source_target_pairs={{0,0},{1,1},{2,2},{3,3},{4,16},{5,17},{6,18},{7,19},{8,32},{9,33},... | collective-permute-start | bytes 1228808 | tf_op jit(solution)/shard_map/ppermute | solution.py:166
  25.2 0.8 copy-start.3
  27.0 13.4 %collective-permute-start.1 = (bf16[40,4096]{1,0:T(8,128)(2,1)S(1)}, bf16[40,4096]{1,0:T(8,128)(2,1)S(1)}, u32[]{:S(2)}, u32[]{:S(2)}) collective-permute-start(bf16[40,4096]{1,0:T(8,128)(2,1)S(1)} %pad_maximum_fusion.2), channel_id=1, source_target_pairs={{0,0},{1,1},{2,2},{3,3},{4,16},{5,17},{6,18},{7,19},{8,32},{9,33},... | collective-permute-start | bytes 983048 | tf_op jit(solution)/shard_map/ppermute | solution.py:176
  41.3 27.3 %all-to-all-start.1 = ((bf16[16,40,256]{2,1,0:T(8,128)(2,1)}), bf16[16,40,256]{2,1,0:T(8,128)(2,1)S(1)}, u32[]{:S(2)}, u32[]{:S(2)}) async-start(bf16[16,40,256]{2,1,0:T(8,128)(2,1)} %copy.28), calls=%async_computation.1 | async-start | bytes 655360 | tf_op jit(solution)/shard_map/all_to_all | solution.py:178
  69.5 15.3 %all-to-all-start = ((bf16[4,320,256]{2,1,0:T(8,128)(2,1)}), bf16[4,320,256]{2,1,0:T(8,128)(2,1)S(1)}, u32[]{:S(2)}, u32[]{:S(2)}) async-start(bf16[4,320,256]{2,1,0:T(8,128)(2,1)} %broadcast_in_dim.24), calls=%async_computation | async-start | bytes 1310720 | tf_op jit(solution)/shard_map/all_to_all | solution.py:171
  128.3 16.3 %copy-start.4 = (f32[320,256]{1,0:T(8,128)S(1)}, f32[320,256]{1,0:T(8,128)}, u32[]{:S(2)}) copy-start(f32[320,256]{1,0:T(8,128)} %param.16) | copy-start | bytes 983044
  144.8 65.2 %copy-start.2 = (f32[320,256]{1,0:T(8,128)}, f32[320,256]{1,0:T(8,128)S(1)}, u32[]{:S(2)}) copy-start(f32[320,256]{1,0:T(8,128)S(1)} %get-tuple-element.32) | copy-start | bytes 983044
  145.7 11.1 %all-to-all-start.5 = ((bf16[4,320,256]{2,1,0:T(8,128)(2,1)}), bf16[4,320,256]{2,1,0:T(8,128)(2,1)S(1)}, u32[]{:S(2)}, u32[]{:S(2)}) async-start(bf16[4,320,256]{2,1,0:T(8,128)(2,1)} %broadcast_in_dim.26), calls=%async_computation.5 | async-start | bytes 1310720 | tf_op jit(solution)/shard_map/all_to_all | solution.py:29
  156.8 0.8 copy-start
  190.1 19.9 %copy-start.5 = (f32[320,256]{1,0:T(8,128)S(1)}, f32[320,256]{1,0:T(8,128)}, u32[]{:S(2)}) copy-start(f32[320,256]{1,0:T(8,128)} %param.19) | copy-start | bytes 983044
  190.1 19.9 %copy-start.6 = (f32[320,256]{1,0:T(8,128)S(1)}, f32[320,256]{1,0:T(8,128)}, u32[]{:S(2)}) copy-start(f32[320,256]{1,0:T(8,128)} %param.17) | copy-start | bytes 983044
  190.1 19.9 %copy-start.7 = (f32[320,256]{1,0:T(8,128)S(1)}, f32[320,256]{1,0:T(8,128)}, u32[]{:S(2)}) copy-start(f32[320,256]{1,0:T(8,128)} %param.18) | copy-start | bytes 983044
Sparse Core Ops, SparseCore 0:
  26.1 58.5 all-gather.2

commit v5 on v4

--- a/solution.py
+++ b/solution.py
@@ -47,8 +47,100 @@
     return moves
 
 
+def token_sides(tokens_ref):
+    return [(b, h) for b in range(tokens_ref.shape[0]) for h in range(tokens_ref.shape[2])]
+
+
+def token_spec(tokens):
+    cores, _, halves, rows, span = tokens.shape
+    return pl.BlockSpec((cores, 1, halves, rows, span), lambda q: (0, q, 0, 0, 0))
+
+
+def outputs_kernel(pub, spans, tokens_ref, w_ref, out_ref):
+    span = tokens_ref.shape[4]
+    total = jnp.zeros((span, w_ref.shape[2]), jnp.float32)
+    for side, (b, h) in enumerate(token_sides(tokens_ref)):
+        total = total + lax.dot_general(
+            tokens_ref[b, 0, h],
+            w_ref[side],
+            (((0,), (0,)), ((), ())),
+            preferred_element_type=jnp.float32,
+        )
+    for owner in range(SIDE):
+        pieces = []
+        for first, rows in ((0, spans[0]), (pub, spans[1])):
+            for x in range(SIDE):
+                at = first + (x * SIDE + owner) * rows
+                pieces.append(total[at : at + rows])
+        out_ref[owner, 0] = jnp.concatenate(pieces, axis=0).astype(out_ref.dtype)
+
+
+def outputs_by_owner(tokens, w_group, pub, spans):
+    quads = tokens.shape[1]
+    chunk, cols = SIDE * sum(spans), w_group.shape[2]
+    return pl.pallas_call(
+        lambda *refs: outputs_kernel(pub, spans, *refs),
+        grid=(quads,),
+        in_specs=[token_spec(tokens), pl.BlockSpec(w_group.shape, lambda q: (0, 0, 0))],
+        out_specs=pl.BlockSpec((SIDE, 1, chunk, cols), lambda q: (0, q, 0, 0)),
+        out_shape=jax.ShapeDtypeStruct((SIDE, quads, chunk, cols), jnp.bfloat16),
+        name="outputs_by_owner",
+    )(tokens, w_group)
+
+
+def public_kernel(pub, spans, tokens_ref, deltas_ref, out_ref, private_ref, acc_ref):
+    quad = pl.program_id(0)
+    deltas = deltas_ref[:, 0].astype(jnp.float32)
+    ordered = []
+    for first, rows in ((0, spans[0]), (SIDE * spans[0], spans[1])):
+        pieces = [
+            deltas[owner, first + x * rows : first + (x + 1) * rows]
+            for x in range(SIDE)
+            for owner in range(SIDE)
+        ]
+        ordered.append(jnp.concatenate(pieces, axis=0).astype(jnp.bfloat16))
+    private_ref[0] = ordered[1]
+
+    @pl.when(quad == 0)
+    def _():
+        acc_ref[...] = jnp.zeros_like(acc_ref)
+
+    for side, (b, h) in enumerate(token_sides(tokens_ref)):
+        acc_ref[side] += jnp.dot(
+            tokens_ref[b, 0, h, :, :pub], ordered[0], preferred_element_type=jnp.float32
+        )
+
+    @pl.when(quad == pl.num_programs(0) - 1)
+    def _():
+        out_ref[...] = acc_ref[...].astype(out_ref.dtype)
+
+
+def public_product(tokens, deltas, pub, spans):
+    cores, quads, halves, rows, span = tokens.shape
+    chunk, cols = deltas.shape[2:]
+    whole = (cores * halves, rows, cols)
+    return pl.pallas_call(
+        lambda *refs: public_kernel(pub, spans, *refs),
+        grid=(quads,),
+        in_specs=[
+            token_spec(tokens),
+            pl.BlockSpec((SIDE, 1, chunk, cols), lambda q: (0, q, 0, 0)),
+        ],
+        out_specs=[
+            pl.BlockSpec(whole, lambda q: (0, 0, 0)),
+            pl.BlockSpec((1, span - pub, cols), lambda q: (q, 0, 0)),
+        ],
+        out_shape=[
+            jax.ShapeDtypeStruct(whole, jnp.bfloat16),
+            jax.ShapeDtypeStruct((quads, span - pub, cols), jnp.bfloat16),
+        ],
+        scratch_shapes=[pltpu.VMEM(whole, jnp.float32)],
+        name="public_product",
+    )(tokens, deltas)
+
+
 def norms_kernel(pub, tokens_ref, delta_ref, precond_ref, out_ref):
-    sides, rows = tokens_ref.shape[1], tokens_ref.shape[2]
+    rows = tokens_ref.shape[3]
     examples = delta_ref.shape[1] // L
     row_at = lax.broadcasted_iota(jnp.int32, out_ref.shape[1:], 0)
     found = jnp.zeros(out_ref.shape[1:], jnp.float32)
@@ -56,9 +148,9 @@
         block_d = delta_ref[0, example * L : (example + 1) * L, :]
         first = pub + example * L
         acc = jnp.zeros((8, block_d.shape[1]), jnp.float32)
-        for side in range(sides):
+        for side, (b, h) in enumerate(token_sides(tokens_ref)):
             grads = jnp.dot(
-                tokens_ref[0, side, :, first : first + L],
+                tokens_ref[b, 0, h, :, first : first + L],
                 block_d,
                 preferred_element_type=jnp.float32,
             )
@@ -69,15 +161,14 @@
 
 
 def example_squares(tokens, deltas, precond, pub):
-    quads, sides, rows, span = tokens.shape
-    priv, cols = deltas.shape[1:]
+    quads, priv, cols = deltas.shape
     out = pl.pallas_call(
         lambda *refs: norms_kernel(pub, *refs),
         grid=(quads,),
         in_specs=[
-            pl.BlockSpec((1, sides, rows, span), lambda q: (q, 0, 0, 0)),
+            token_spec(tokens),
             pl.BlockSpec((1, priv, cols), lambda q: (q, 0, 0)),
-            pl.BlockSpec((sides, rows, cols), lambda q: (0, 0, 0)),
+            pl.BlockSpec(precond.shape, lambda q: (0, 0, 0)),
         ],
         out_specs=pl.BlockSpec((1, 8, L), lambda q: (q, 0, 0)),
         out_shape=jax.ShapeDtypeStruct((quads, 8, L), jnp.float32),
@@ -104,9 +195,9 @@
     def _():
         acc_ref[...] = jnp.zeros_like(acc_ref)
 
-    for side in range(tokens_ref.shape[1]):
+    for side, (b, h) in enumerate(token_sides(tokens_ref)):
         acc_ref[side] += jnp.dot(
-            tokens_ref[0, side, :, pub:], weighted, preferred_element_type=jnp.float32
+            tokens_ref[b, 0, h, :, pub:], weighted, preferred_element_type=jnp.float32
         )
 
     @pl.when(quad == pl.num_programs(0) - 1)
@@ -115,21 +206,53 @@
 
 
 def clipped_sum(factors, tokens, deltas, pub):
-    quads, sides, rows, span = tokens.shape
+    cores, quads, halves, rows, span = tokens.shape
     priv, cols = deltas.shape[1:]
+    whole = (cores * halves, rows, cols)
     return pl.pallas_call(
         lambda *refs: clipped_kernel(pub, *refs),
         grid=(quads,),
         in_specs=[
             pl.BlockSpec(memory_space=pltpu.SMEM),
-            pl.BlockSpec((1, sides, rows, span), lambda q: (q, 0, 0, 0)),
+            token_spec(tokens),
             pl.BlockSpec((1, priv, cols), lambda q: (q, 0, 0)),
         ],
-        out_specs=pl.BlockSpec((sides, rows, cols), lambda q: (0, 0, 0)),
-        out_shape=jax.ShapeDtypeStruct((sides, rows, cols), jnp.bfloat16),
-        scratch_shapes=[pltpu.VMEM((sides, rows, cols), jnp.float32)],
+        out_specs=pl.BlockSpec(whole, lambda q: (0, 0, 0)),
+        out_shape=jax.ShapeDtypeStruct(whole, jnp.bfloat16),
+        scratch_shapes=[pltpu.VMEM(whole, jnp.float32)],
         name="clipped_sum",
     )(factors, tokens, deltas)
+
+
+def gather_tokens(own, replicas):
+    chips = replicas // CORES
+    z = lax.div(lax.axis_index("replica"), CORES)
+    up = [(r, (r + CORES) % replicas) for r in range(replicas)]
+    down = [(r, (r - CORES) % replicas) for r in range(replicas)]
+    swap = [(r, r ^ 1) for r in range(replicas)]
+    held = jnp.zeros((CORES, chips, *own.shape), own.dtype)
+
+    def place(held, block, chip):
+        pair = jnp.stack([block, lax.ppermute(block, "replica", swap)])[:, None]
+        return lax.dynamic_update_slice(held, pair, (0, lax.rem(chip, chips), 0, 0))
+
+    held = place(held, own, z)
+    below, above = own, own
+    for step in range(1, chips // 2):
+        below = lax.ppermute(below, "replica", up)
+        above = lax.ppermute(above, "replica", down)
+        held = place(held, below, z + chips - step)
+        held = place(held, above, z + step)
+    half = own.shape[0] // 2
+    last = jnp.concatenate(
+        [
+            lax.ppermute(below[:half], "replica", up),
+            lax.ppermute(above[half:], "replica", down),
+        ],
+        axis=0,
+    )
+    held = place(held, last, z + chips // 2)
+    return held.reshape(CORES, chips // 2, 2, *own.shape)
 
 
 def on_device(
@@ -150,12 +273,10 @@
     quads = replicas // SIDE
     pub = public_tokens.shape[0]
     priv = private_tokens.shape[0]
-    rows, cols = weight.shape
+    cols = weight.shape[1]
     examples_here = token_counts.shape[1]
     pub_rows = public_targets.shape[0]
     priv_rows = private_targets.shape[0]
-    pub_all = quads * SIDE * pub_rows
-    priv_all = quads * SIDE * priv_rows
     moves = to_class(replicas)
 
     live = (
@@ -164,70 +285,64 @@
     live_tokens = jnp.where(live[:, None], private_tokens, jnp.zeros_like(private_tokens))
     local = jnp.concatenate([public_tokens.T, live_tokens.T], axis=1)
     local = lax.ppermute(local, ("replica", "tile"), moves)
-    tokens = lax.all_gather(local, "replica", axis=0)
-    tokens = tokens.reshape(quads, SIDE, rows, pub + priv)
+    tokens = gather_tokens(local, replicas)
+    core = lax.rem(lax.axis_index("replica"), CORES)
+
+    def own_core_first(sides):
+        split = sides.reshape(2, CORES, *sides.shape[1:])
+        split = jnp.where(core == 0, split, split[:, ::-1])
+        return split.transpose(1, 0, 2, 3).reshape(sides.shape)
+
+    def by_side(mine):
+        split = mine.reshape(CORES, 2, *mine.shape[1:])
+        split = jnp.where(core == 0, split, split[::-1])
+        return split.transpose(1, 0, 2, 3).reshape(mine.shape)
 
     w_half = weight.astype(jnp.bfloat16)
-    w_group = lax.all_to_all(
-        everywhere(w_half, SIDE), "tile", 0, 0, tiled=True, axis_index_groups=along_x
-    )
-
+    w_group = own_core_first(
+        lax.all_to_all(
+            everywhere(w_half, SIDE), "tile", 0, 0, tiled=True, axis_index_groups=along_x
+        )
+    )
+
+    spans = (pub_rows, priv_rows)
+    chunk = SIDE * (pub_rows + priv_rows)
     targets = jnp.concatenate([public_targets, private_targets], axis=0)
     targets = lax.ppermute(targets, ("replica", "tile"), moves)
     targets = targets.reshape(-1, replicas, cols).transpose(1, 0, 2)
     targets = lax.all_to_all(targets, "replica", 0, 0, tiled=True)
+    targets = targets.reshape(quads, SIDE, pub_rows + priv_rows, cols)
     targets = jnp.concatenate(
         [
-            targets[:, :pub_rows].reshape(pub_all, cols),
-            targets[:, pub_rows:].reshape(priv_all, cols),
-        ],
-        axis=0,
-    )
-
-    def by_owner(part, span):
-        part = part.reshape(quads, SIDE, SIDE, span, cols)
-        return part.transpose(2, 0, 1, 3, 4).reshape(SIDE, quads * SIDE * span, cols)
-
-    def by_token(part, span):
-        part = part.reshape(SIDE, quads, SIDE, span, cols)
-        return part.transpose(1, 2, 0, 3, 4).reshape(quads, SIDE * SIDE * span, cols)
-
-    out = jnp.einsum(
-        "qxfn,xfk->qnk", tokens, w_group, preferred_element_type=jnp.float32
-    ).astype(jnp.bfloat16)
-    sent = jnp.concatenate(
-        [by_owner(out[:, :pub], pub_rows), by_owner(out[:, pub:], priv_rows)], axis=1
-    )
+            targets[:, :, :pub_rows].reshape(quads, SIDE * pub_rows, cols),
+            targets[:, :, pub_rows:].reshape(quads, SIDE * priv_rows, cols),
+        ],
+        axis=1,
+    ).reshape(quads * chunk, cols)
+
+    sent = outputs_by_owner(tokens, w_group, pub, spans).reshape(SIDE, quads * chunk, cols)
     got, (targets, tokens) = exchange(sent, "tile", along_y, (targets, tokens))
     total = jnp.sum(got.astype(jnp.float32), axis=0)
     delta = (total - targets.astype(jnp.float32)).astype(jnp.bfloat16)
     deltas, (tokens, public_moment) = exchange(
         everywhere(delta, SIDE), "tile", along_y, (tokens, public_moment)
     )
-    public_delta = by_token(deltas[:, :pub_all], pub_rows)
-    private_delta = by_token(deltas[:, pub_all:], priv_rows)
 
     def over_classes(part):
-        got, _ = exchange(part.astype(jnp.bfloat16), "tile", along_x)
+        got, _ = exchange(by_side(part), "tile", along_x)
         return jnp.sum(got.astype(jnp.float32), axis=0)
 
-    public_grad = over_classes(
-        jnp.einsum(
-            "qxfn,qnk->xfk",
-            tokens[:, :, :, :pub],
-            public_delta,
-            preferred_element_type=jnp.float32,
-        )
-    ) / math.sqrt(pub * replicas)
+    product, private_delta = public_product(
+        tokens, deltas.reshape(SIDE, quads, chunk, cols), pub, spans
+    )
+    public_grad = over_classes(product) / math.sqrt(pub * replicas)
     new_public = beta_public * public_moment + (1.0 - beta_public) * public_grad * public_grad
     precond = 1.0 / (jnp.sqrt(new_public) + public_epsilon)
     precond_group, _ = exchange(
         everywhere(precond.astype(jnp.bfloat16), SIDE), "tile", along_x
     )
 
-    squares = example_squares(
-        tokens, private_delta, precond_group, pub
-    )
+    squares = example_squares(tokens, private_delta, own_core_first(precond_group), pub)
     squares = jnp.sum(exchange(everywhere(squares, SIDE), "tile", along_y)[0], axis=0)
     squares = jnp.sum(exchange(everywhere(squares, replicas), "replica", None)[0], axis=0)
     clip_norm = clip_factor * math.sqrt(L * D * Q)

time: 219 us -> 221 us (level)
  waiting for transfers between devices: 50.2 us -> 21.1 us
  other arithmetic: 6.3 us -> 20.4 us
  between operations: 14.3 us -> 0.93 us
  blocking collectives: 89.7 us -> 102 us
  starting transfers between devices: 31 us -> 43.3 us
  Pallas kernels: 12.5 us -> 24.2 us
  matrix products: 7.41 us -> 0 us
    ppermute x0 -> x16, starting transfers between devices: none -> 17.6 us  [the longest x3 7.91 us: gather_tokens(): above = lax.ppermute(above, 'replica', down)]
    all_to_all x1, waiting for transfers between devices: 16.3 us -> 2.78 us  [on_device(): targets = lax.all_to_all(targets, 'replica', 0, 0, tiled=True)]
    ppermute x0 -> x16, waiting for transfers between devices: none -> 12.7 us  [the longest x3 10.9 us: gather_tokens(): below = lax.ppermute(below, 'replica', up)]
    pallas_call x0 -> x2, Pallas kernels: none -> 12.3 us  [the longest x1 6.67 us: outputs_by_owner(): pl.pallas_call(lambda *refs: outputs_kernel(pub, spans, *refs), grid=(qua...]
    all_to_all x6 -> x7, blocking collectives: 89.7 us -> 102 us  [exchange(): got = lax.all_to_all(sent, axis, 0, 0, tiled=True, axis_index_groups=groups)]
    dynamic_update_slice x0 -> x8, other arithmetic: none -> 10.9 us  [place(): return lax.dynamic_update_slice(held, pair, (0, lax.rem(chip, chips), 0, 0))]
    all_to_all x1, waiting for transfers between devices: 10.6 us -> 0.01 us  [on_device(): lax.all_to_all(everywhere(w_half, SIDE), 'tile', 0, 0, tiled=True, axis_i...]
    ppermute x1, waiting for transfers between devices: 7.51 us -> 0.01 us  [on_device(): targets = lax.ppermute(targets, ('replica', 'tile'), moves)]
  transfers between devices with their start and end apart: 6 -> 20, of which waited for: 5 -> 5; matrix products, arithmetic and copies ran while one was open for 2% -> 8% of each run, Pallas kernels for 0% -> 0%
where the time goes in v5:
time: 221 us; the launch traced here: 220 us
  blocking collectives  102 us (46%)
  starting transfers between devices  43.3 us (20%)
  Pallas kernels  24.2 us (11%)
  waiting for transfers between devices  21.1 us (10%)
  other arithmetic  20.4 us (9%)
  local copies, waits for them, and re-layouts  8.13 us (4%)
    all_to_all x7, blocking collectives, exchange(): got = lax.all_to_all(sent, axis, 0, 0, tiled=True, axis_index_groups=groups)  102 us
    all_to_all x1, starting transfers between devices, on_device(): targets = lax.all_to_all(targets, 'replica', 0, 0, tiled=True)  12.2 us
    dynamic_update_slice x8, other arithmetic, place(): return lax.dynamic_update_slice(held, pair, (0, lax.rem(chip, chips), 0, 0))  10.9 us
    ppermute x3, waiting for transfers between devices, gather_tokens(): below = lax.ppermute(below, 'replica', up)  10.9 us
    ppermute x3, starting transfers between devices, gather_tokens(): above = lax.ppermute(above, 'replica', down)  7.91 us
    pallas_call x1, Pallas kernels, outputs_by_owner(): pl.pallas_call(lambda *refs: outputs_kernel(pub, spans, *refs), grid=(qua...  6.67 us
    pallas_call x1, Pallas kernels, example_squares(): pl.pallas_call(lambda *refs: norms_kernel(pub, *refs), grid=(quads,), in_...  6.26 us
    ppermute x1, starting transfers between devices, on_device(): local = lax.ppermute(local, ('replica', 'tile'), moves)  6.03 us
  transfers between devices with their start and end apart: 20, of which 5 were waited for; matrix products, arithmetic and copies ran while one was open for 8% of the time, Pallas kernels for 0%

profile of v5, /device:TPU:1, one launch (start us, length us, event | category | flops | bytes accessed | tf_op | source)
XLA Modules:
  0.0 219.6 jit_solution(16362987391444436283)
XLA Ops:
  3.4 6.0 %collective-permute-start = (bf16[320,640]{1,0:T(8,128)(2,1)S(1)}, bf16[320,640]{1,0:T(8,128)(2,1)}, u32[]{:S(2)}, u32[]{:S(2)}) collective-permute-start(bf16[320,640]{1,0:T(8,128)(2,1)S(1)} %pad_maximum_fusion), channel_id=1, source_target_pairs={{0,0},{1,1},{2,2},{3,3},{4,16},{5,17},{6,18},{7,19},{8,32},{9,33},... | collective-permute-start | bytes 1228808 | tf_op jit(solution)/shard_map/ppermute | solution.py:287
  11.3 3.5 %all-to-all-start = ((bf16[4,320,256]{2,1,0:T(8,128)(2,1)}), bf16[4,320,256]{2,1,0:T(8,128)(2,1)S(1)}, u32[]{:S(2)}, u32[]{:S(2)}) async-start(bf16[4,320,256]{2,1,0:T(8,128)(2,1)} %broadcast_in_dim.81), calls=%async_computation | async-start | bytes 1310720 | tf_op jit(solution)/shard_map/all_to_all | solution.py:303
  14.8 5.6 %collective-permute-done = bf16[320,640]{1,0:T(8,128)(2,1)} collective-permute-done((bf16[320,640]{1,0:T(8,128)(2,1)S(1)}, bf16[320,640]{1,0:T(8,128)(2,1)}, u32[]{:S(2)}, u32[]{:S(2)}) %collective-permute-start) | collective-permute-done | bytes 409632 | tf_op jit(solution)/shard_map/ppermute | solution.py:287
  20.4 1.4 collective-permute-start.2
  21.8 3.9 %collective-permute-start.4 = (bf16[320,640]{1,0:T(8,128)(2,1)}, bf16[320,640]{1,0:T(8,128)(2,1)S(1)}, u32[]{:S(2)}, u32[]{:S(2)}) collective-permute-start(bf16[320,640]{1,0:T(8,128)(2,1)} %collective-permute-done), channel_id=1, source_target_pairs={{0,224},{16,240},{32,0},{48,16},{64,32},{80,48},{96,64},{112,80},{... | collective-permute-start | bytes 1228808 | tf_op jit(solution)/shard_map/ppermute | solution.py:243
  25.7 4.0 %collective-permute-start.17 = (bf16[40,4096]{1,0:T(8,128)(2,1)S(1)}, bf16[40,4096]{1,0:T(8,128)(2,1)S(1)}, u32[]{:S(2)}, u32[]{:S(2)}) collective-permute-start(bf16[40,4096]{1,0:T(8,128)(2,1)S(1)} %pad_maximum_fusion.1), channel_id=1, source_target_pairs={{0,0},{1,1},{2,2},{3,3},{4,16},{5,17},{6,18},{7,19},{8,32},{9,33},... | collective-permute-start | bytes 983048 | tf_op jit(solution)/shard_map/ppermute | solution.py:311
  29.8 4.8 %collective-permute-done.2 = bf16[320,640]{1,0:T(8,128)(2,1)S(1)} collective-permute-done((bf16[320,640]{1,0:T(8,128)(2,1)}, bf16[320,640]{1,0:T(8,128)(2,1)S(1)}, u32[]{:S(2)}, u32[]{:S(2)}) %collective-permute-start.2) | collective-permute-done | bytes 409632 | tf_op jit(solution)/shard_map/ppermute | solution.py:242
  34.6 2.7 %collective-permute-start.8 = (bf16[320,640]{1,0:T(8,128)(2,1)S(1)}, bf16[320,640]{1,0:T(8,128)(2,1)S(1)}, u32[]{:S(2)}, u32[]{:S(2)}) collective-permute-start(bf16[320,640]{1,0:T(8,128)(2,1)S(1)} %collective-permute-done.4), channel_id=1, source_target_pairs={{0,224},{16,240},{32,0},{48,16},{64,32},{80,48},{96,64},{112,80},{... | collective-permute-start | bytes 1228808 | tf_op jit(solution)/shard_map/ppermute | solution.py:243
  38.0 12.2 %all-to-all-start.1 = ((bf16[16,40,256]{2,1,0:T(8,128)(2,1)}), bf16[16,40,256]{2,1,0:T(8,128)(2,1)S(1)}, u32[]{:S(2)}, u32[]{:S(2)}) async-start(bf16[16,40,256]{2,1,0:T(8,128)(2,1)} %bitcast.99), calls=%async_computation.1 | async-start | bytes 655360 | tf_op jit(solution)/shard_map/all_to_all | solution.py:313
  50.9 1.5 collective-permute-start.10
  52.5 1.3 collective-permute-start.12
  54.8 3.5 %broadcast_in_dim.70 = bf16[2,8,320,640]{3,2,1,0:T(8,128)(2,1)} broadcast(bf16[]{:T(256)} %constant.61.clone.1), dimensions={} | broadcast | bytes 6553602 | tf_op jit(solution)/shard_map/broadcast_in_dim | solution.py:233
  58.3 2.1 fusion
  60.4 2.8 %all-to-all-done.1 = bf16[16,40,256]{2,1,0:T(8,128)(2,1)S(1)} async-done(((bf16[16,40,256]{2,1,0:T(8,128)(2,1)}), bf16[16,40,256]{2,1,0:T(8,128)(2,1)S(1)}, u32[]{:S(2)}, u32[]{:S(2)}) %all-to-all-start.1) | async-done | bytes 327712 | tf_op jit(solution)/shard_map/all_to_all | solution.py:313
  63.3 6.1 %collective-permute-done.10 = bf16[320,640]{1,0:T(8,128)(2,1)S(1)} collective-permute-done((bf16[320,640]{1,0:T(8,128)(2,1)S(1)}, bf16[320,640]{1,0:T(8,128)(2,1)S(1)}, u32[]{:S(2)}, u32[]{:S(2)}) %collective-permute-start.10) | collective-permute-done | bytes 409632 | tf_op jit(solution)/shard_map/ppermute | solution.py:242
  69.6 2.0 fusion.1
  72.5 3.0 %collective-permute-start.15 = (bf16[160,640]{1,0:T(8,128)(2,1)S(1)}, bf16[160,640]{1,0:T(8,128)(2,1)S(1)}, u32[]{:S(2)}, u32[]{:S(2)}) collective-permute-start(bf16[160,640]{1,0:T(8,128)(2,1)S(1)} %slice.21), channel_id=1, source_target_pairs={{0,224},{16,240},{32,0},{48,16},{64,32},{80,48},{96,64},{112,80},{... | collective-permute-start | bytes 614408 | tf_op jit(solution)/shard_map/ppermute | solution.py:250
  75.5 2.0 fusion.2
  78.3 1.7 collective-permute-done.15
  86.1 6.7 %outputs_by_owner.1 = bf16[4,4,160,256]{3,2,1,0:T(8,128)(2,1)} custom-call(bf16[2,4,2,320,640]{4,3,2,1,0:T(8,128)(2,1)} %bitcast.36.refs_0_.refs_1_, bf16[4,320,256]{2,1,0:T(8,128)(2,1)} %bitcast.102), custom_call_target="tpu_custom_call" | custom-call | tf_op jit(solution)/shard_map/outputs_by_owner/pallas_call | solution.py:81
  92.7 21.9 %all_to_all.45 = bf16[4,640,256]{2,1,0:T(8,128)(2,1)S(1)} all-to-all(bf16[4,640,256]{2,1,0:T(8,128)(2,1)} %bitcast.101), channel_id=1, replica_groups={{0,1,2,3},{4,5,6,7},{8,9,10,11},{12,13,14,15},{16,17,18,19},{20,21,22,2..., dimensions={0} | all-to-all | bytes 2621440 | tf_op jit(solution)/shard_map/all_to_all | solution.py:29
  115.0 20.0 %all_to_all.46 = bf16[4,640,256]{2,1,0:T(8,128)(2,1)} all-to-all(bf16[4,640,256]{2,1,0:T(8,128)(2,1)S(1)} %broadcast_in_dim.82), channel_id=1, replica_groups={{0,1,2,3},{4,5,6,7},{8,9,10,11},{12,13,14,15},{16,17,18,19},{20,21,22,2..., dimensions={0} | all-to-all | bytes 2621440 | tf_op jit(solution)/shard_map/all_to_all | solution.py:29
  135.0 5.6 %public_product.1 = (bf16[4,320,256]{2,1,0:T(8,128)(2,1)}, bf16[4,384,256]{2,1,0:T(8,128)(2,1)}) custom-call(bf16[2,4,2,320,640]{4,3,2,1,0:T(8,128)(2,1)} %bitcast.36.refs_0_.refs_1_, bf16[4,4,160,256]{3,2,1,0:T(8,128)(2,1)} %bitcast.100), custom_call_target="tpu_custom_call" | custom-call | tf_op jit(solution)/shard_map/public_product/pallas_call | solution.py:122
  140.6 1.5 fusion.9
  142.2 11.9 %all_to_all.47 = bf16[4,320,256]{2,1,0:T(8,128)(2,1)S(1)} all-to-all(bf16[4,320,256]{2,1,0:T(8,128)(2,1)S(1)} %bitcast.105), channel_id=1, replica_groups={{0,4,8,12},{1,5,9,13},{2,6,10,14},{3,7,11,15},{16,20,24,28},{17,21,25,2..., dimensions={0} | all-to-all | bytes 1310720 | tf_op jit(solution)/shard_map/all_to_all | solution.py:29
  154.4 10.0 %all_to_all.48 = bf16[4,320,256]{2,1,0:T(8,128)(2,1)S(1)} all-to-all(bf16[4,320,256]{2,1,0:T(8,128)(2,1)S(1)} %broadcast_in_dim.83), channel_id=1, replica_groups={{0,4,8,12},{1,5,9,13},{2,6,10,14},{3,7,11,15},{16,20,24,28},{17,21,25,2..., dimensions={0} | all-to-all | bytes 1310720 | tf_op jit(solution)/shard_map/all_to_all | solution.py:29
  165.5 6.3 %example_squares.1 = f32[4,8,128]{2,1,0:T(8,128)} custom-call(bf16[2,4,2,320,640]{4,3,2,1,0:T(8,128)(2,1)} %bitcast.36.refs_0_.refs_1_, bf16[4,384,256]{2,1,0:T(8,128)(2,1)} %get-tuple-element.31.refs_1_.refs_2_, bf16[4,320,256]{2,1,0:T(8,128)(2,1)} %bitcast.108), custom_call_target="tpu_custom_call" | custom-call | tf_op jit(solution)/shard_map/example_squares/pallas_call | solution.py:165
  172.5 6.5 %all_to_all.49 = f32[4,4,3]{2,1,0:T(4,128)S(1)} all-to-all(f32[4,4,3]{2,1,0:T(4,128)S(1)} %broadcast_in_dim.85), channel_id=1, replica_groups={{0,1,2,3},{4,5,6,7},{8,9,10,11},{12,13,14,15},{16,17,18,19},{20,21,22,2..., dimensions={0} | all-to-all | bytes 384 | tf_op jit(solution)/shard_map/all_to_all | solution.py:29
  179.0 18.2 %all_to_all.50 = f32[16,4,3]{2,1,0:T(4,128)S(1)} all-to-all(f32[16,4,3]{2,1,0:T(4,128)S(1)} %broadcast_in_dim.86), channel_id=1, replica_groups=mesh['replica'=16,'tile'=16] {'replica'}, dimensions={0} | all-to-all | bytes 1536 | tf_op jit(solution)/shard_map/all_to_all | solution.py:29
  197.9 5.7 %clipped_sum.1 = bf16[4,320,256]{2,1,0:T(8,128)(2,1)} custom-call(f32[4,3]{1,0:T(4,128)} %maximum_divide_fusion.refs_0_, bf16[2,4,2,320,640]{4,3,2,1,0:T(8,128)(2,1)} %bitcast.36.refs_0_.refs_1_, bf16[4,384,256]{2,1,0:T(8,128)(2,1)} %get-tuple-element.31.refs_1_.refs_2_), custom_call_target="tpu_custom_call" | custom-call | tf_op jit(solution)/shard_map/clipped_sum/pallas_call | solution.py:212
  203.6 1.5 fusion.11
  205.1 13.1 %all_to_all.51 = bf16[4,320,256]{2,1,0:T(8,128)(2,1)S(1)} all-to-all(bf16[4,320,256]{2,1,0:T(8,128)(2,1)S(1)} %bitcast.107), channel_id=1, replica_groups={{0,4,8,12},{1,5,9,13},{2,6,10,14},{3,7,11,15},{16,20,24,28},{17,21,25,2..., dimensions={0} | all-to-all | bytes 1310720 | tf_op jit(solution)/shard_map/all_to_all | solution.py:29
  (80 shorter events, 19.8 us)
Async XLA Ops:
  2.3 23.4 %copy-start.6 = (bf16[24,4096]{1,0:T(8,128)(2,1)S(1)}, bf16[24,4096]{1,0:T(8,128)(2,1)}, u32[]{:S(2)}) copy-start(bf16[24,4096]{1,0:T(8,128)(2,1)} %param.13) | copy-start | bytes 589828
  2.3 23.4 %copy-start.7 = (bf16[16,4096]{1,0:T(8,128)(2,1)S(1)}, bf16[16,4096]{1,0:T(8,128)(2,1)}, u32[]{:S(2)}) copy-start(bf16[16,4096]{1,0:T(8,128)(2,1)} %param.11) | copy-start | bytes 393220
  3.4 17.0 %collective-permute-start = (bf16[320,640]{1,0:T(8,128)(2,1)S(1)}, bf16[320,640]{1,0:T(8,128)(2,1)}, u32[]{:S(2)}, u32[]{:S(2)}) collective-permute-start(bf16[320,640]{1,0:T(8,128)(2,1)S(1)} %pad_maximum_fusion), channel_id=1, source_target_pairs={{0,0},{1,1},{2,2},{3,3},{4,16},{5,17},{6,18},{7,19},{8,32},{9,33},... | collective-permute-start | bytes 1228808 | tf_op jit(solution)/shard_map/ppermute | solution.py:287
  11.3 26.8 %all-to-all-start = ((bf16[4,320,256]{2,1,0:T(8,128)(2,1)}), bf16[4,320,256]{2,1,0:T(8,128)(2,1)S(1)}, u32[]{:S(2)}, u32[]{:S(2)}) async-start(bf16[4,320,256]{2,1,0:T(8,128)(2,1)} %broadcast_in_dim.81), calls=%async_computation | async-start | bytes 1310720 | tf_op jit(solution)/shard_map/all_to_all | solution.py:303
  20.4 14.2 %collective-permute-start.2 = (bf16[320,640]{1,0:T(8,128)(2,1)}, bf16[320,640]{1,0:T(8,128)(2,1)S(1)}, u32[]{:S(2)}, u32[]{:S(2)}) collective-permute-start(bf16[320,640]{1,0:T(8,128)(2,1)} %collective-permute-done), channel_id=1, source_target_pairs={{0,32},{16,48},{32,64},{48,80},{64,96},{80,112},{96,128},{112,144}... | collective-permute-start | bytes 1228808 | tf_op jit(solution)/shard_map/ppermute | solution.py:242
  21.8 12.9 %collective-permute-start.4 = (bf16[320,640]{1,0:T(8,128)(2,1)}, bf16[320,640]{1,0:T(8,128)(2,1)S(1)}, u32[]{:S(2)}, u32[]{:S(2)}) collective-permute-start(bf16[320,640]{1,0:T(8,128)(2,1)} %collective-permute-done), channel_id=1, source_target_pairs={{0,224},{16,240},{32,0},{48,16},{64,32},{80,48},{96,64},{112,80},{... | collective-permute-start | bytes 1228808 | tf_op jit(solution)/shard_map/ppermute | solution.py:243
  25.7 11.6 %collective-permute-start.17 = (bf16[40,4096]{1,0:T(8,128)(2,1)S(1)}, bf16[40,4096]{1,0:T(8,128)(2,1)S(1)}, u32[]{:S(2)}, u32[]{:S(2)}) collective-permute-start(bf16[40,4096]{1,0:T(8,128)(2,1)S(1)} %pad_maximum_fusion.1), channel_id=1, source_target_pairs={{0,0},{1,1},{2,2},{3,3},{4,16},{5,17},{6,18},{7,19},{8,32},{9,33},... | collective-permute-start | bytes 983048 | tf_op jit(solution)/shard_map/ppermute | solution.py:311
  34.6 16.3 %collective-permute-start.6 = (bf16[320,640]{1,0:T(8,128)(2,1)S(1)}, bf16[320,640]{1,0:T(8,128)(2,1)S(1)}, u32[]{:S(2)}, u32[]{:S(2)}) collective-permute-start(bf16[320,640]{1,0:T(8,128)(2,1)S(1)} %collective-permute-done.2), channel_id=1, source_target_pairs={{0,32},{16,48},{32,64},{48,80},{64,96},{80,112},{96,128},{112,144}... | collective-permute-start | bytes 1228808 | tf_op jit(solution)/shard_map/ppermute | solution.py:242
  34.6 17.8 %collective-permute-start.8 = (bf16[320,640]{1,0:T(8,128)(2,1)S(1)}, bf16[320,640]{1,0:T(8,128)(2,1)S(1)}, u32[]{:S(2)}, u32[]{:S(2)}) collective-permute-start(bf16[320,640]{1,0:T(8,128)(2,1)S(1)} %collective-permute-done.4), channel_id=1, source_target_pairs={{0,224},{16,240},{32,0},{48,16},{64,32},{80,48},{96,64},{112,80},{... | collective-permute-start | bytes 1228808 | tf_op jit(solution)/shard_map/ppermute | solution.py:243
  38.0 25.1 %all-to-all-start.1 = ((bf16[16,40,256]{2,1,0:T(8,128)(2,1)}), bf16[16,40,256]{2,1,0:T(8,128)(2,1)S(1)}, u32[]{:S(2)}, u32[]{:S(2)}) async-start(bf16[16,40,256]{2,1,0:T(8,128)(2,1)} %bitcast.99), calls=%async_computation.1 | async-start | bytes 655360 | tf_op jit(solution)/shard_map/all_to_all | solution.py:313
  50.2 4.6 %collective-permute-start.1 = (bf16[320,640]{1,0:T(8,128)(2,1)}, bf16[320,640]{1,0:T(8,128)(2,1)}, u32[]{:S(2)}, u32[]{:S(2)}) collective-permute-start(bf16[320,640]{1,0:T(8,128)(2,1)} %collective-permute-done), channel_id=1, source_target_pairs={{0,16},{16,0},{32,48},{48,32},{64,80},{80,64},{96,112},{112,96},{1... | collective-permute-start | bytes 1228808 | tf_op jit(solution)/shard_map/ppermute | solution.py:236
  50.4 19.2 %collective-permute-start.3 = (bf16[320,640]{1,0:T(8,128)(2,1)S(1)}, bf16[320,640]{1,0:T(8,128)(2,1)}, u32[]{:S(2)}, u32[]{:S(2)}) collective-permute-start(bf16[320,640]{1,0:T(8,128)(2,1)S(1)} %collective-permute-done.2), channel_id=1, source_target_pairs={{0,16},{16,0},{32,48},{48,32},{64,80},{80,64},{96,112},{112,96},{1... | collective-permute-start | bytes 1228808 | tf_op jit(solution)/shard_map/ppermute | solution.py:236
  50.7 24.8 %collective-permute-start.5 = (bf16[320,640]{1,0:T(8,128)(2,1)S(1)}, bf16[320,640]{1,0:T(8,128)(2,1)}, u32[]{:S(2)}, u32[]{:S(2)}) collective-permute-start(bf16[320,640]{1,0:T(8,128)(2,1)S(1)} %collective-permute-done.4), channel_id=1, source_target_pairs={{0,16},{16,0},{32,48},{48,32},{64,80},{80,64},{96,112},{112,96},{1... | collective-permute-start | bytes 1228808 | tf_op jit(solution)/shard_map/ppermute | solution.py:236
  50.9 18.5 %collective-permute-start.10 = (bf16[320,640]{1,0:T(8,128)(2,1)S(1)}, bf16[320,640]{1,0:T(8,128)(2,1)S(1)}, u32[]{:S(2)}, u32[]{:S(2)}) collective-permute-start(bf16[320,640]{1,0:T(8,128)(2,1)S(1)} %collective-permute-done.6), channel_id=1, source_target_pairs={{0,32},{16,48},{32,64},{48,80},{64,96},{80,112},{96,128},{112,144}... | collective-permute-start | bytes 1228808 | tf_op jit(solution)/shard_map/ppermute | solution.py:242
  52.5 20.0 %collective-permute-start.12 = (bf16[320,640]{1,0:T(8,128)(2,1)S(1)}, bf16[320,640]{1,0:T(8,128)(2,1)S(1)}, u32[]{:S(2)}, u32[]{:S(2)}) collective-permute-start(bf16[320,640]{1,0:T(8,128)(2,1)S(1)} %collective-permute-done.8), channel_id=1, source_target_pairs={{0,224},{16,240},{32,0},{48,16},{64,32},{80,48},{96,64},{112,80},{... | collective-permute-start | bytes 1228808 | tf_op jit(solution)/shard_map/ppermute | solution.py:243
  63.2 17.9 %collective-permute-start.7 = (bf16[320,640]{1,0:T(8,128)(2,1)S(1)}, bf16[320,640]{1,0:T(8,128)(2,1)S(1)}, u32[]{:S(2)}, u32[]{:S(2)}) collective-permute-start(bf16[320,640]{1,0:T(8,128)(2,1)S(1)} %collective-permute-done.6), channel_id=1, source_target_pairs={{0,16},{16,0},{32,48},{48,32},{64,80},{80,64},{96,112},{112,96},{1... | collective-permute-start | bytes 1228808 | tf_op jit(solution)/shard_map/ppermute | solution.py:236
  69.5 8.3 %collective-permute-start.14 = (bf16[160,640]{1,0:T(8,128)(2,1)S(1)}, bf16[160,640]{1,0:T(8,128)(2,1)S(1)}, u32[]{:S(2)}, u32[]{:S(2)}) collective-permute-start(bf16[160,640]{1,0:T(8,128)(2,1)S(1)} %slice.20), channel_id=1, source_target_pairs={{0,32},{16,48},{32,64},{48,80},{64,96},{80,112},{96,128},{112,144}... | collective-permute-start | bytes 614408 | tf_op jit(solution)/shard_map/ppermute | solution.py:249
  71.5 10.6 %collective-permute-start.9 = (bf16[320,640]{1,0:T(8,128)(2,1)S(1)}, bf16[320,640]{1,0:T(8,128)(2,1)S(1)}, u32[]{:S(2)}, u32[]{:S(2)}) collective-permute-start(bf16[320,640]{1,0:T(8,128)(2,1)S(1)} %collective-permute-done.8), channel_id=1, source_target_pairs={{0,16},{16,0},{32,48},{48,32},{64,80},{80,64},{96,112},{112,96},{1... | collective-permute-start | bytes 1228808 | tf_op jit(solution)/shard_map/ppermute | solution.py:236
  72.5 7.4 %collective-permute-start.15 = (bf16[160,640]{1,0:T(8,128)(2,1)S(1)}, bf16[160,640]{1,0:T(8,128)(2,1)S(1)}, u32[]{:S(2)}, u32[]{:S(2)}) collective-permute-start(bf16[160,640]{1,0:T(8,128)(2,1)S(1)} %slice.21), channel_id=1, source_target_pairs={{0,224},{16,240},{32,0},{48,16},{64,32},{80,48},{96,64},{112,80},{... | collective-permute-start | bytes 614408 | tf_op jit(solution)/shard_map/ppermute | solution.py:250
  77.5 5.6 %collective-permute-start.11 = (bf16[320,640]{1,0:T(8,128)(2,1)S(1)}, bf16[320,640]{1,0:T(8,128)(2,1)S(1)}, u32[]{:S(2)}, u32[]{:S(2)}) collective-permute-start(bf16[320,640]{1,0:T(8,128)(2,1)S(1)} %collective-permute-done.10), channel_id=1, source_target_pairs={{0,16},{16,0},{32,48},{48,32},{64,80},{80,64},{96,112},{112,96},{1... | collective-permute-start | bytes 1228808 | tf_op jit(solution)/shard_map/ppermute | solution.py:236
  77.8 6.3 %collective-permute-start.13 = (bf16[320,640]{1,0:T(8,128)(2,1)S(1)}, bf16[320,640]{1,0:T(8,128)(2,1)S(1)}, u32[]{:S(2)}, u32[]{:S(2)}) collective-permute-start(bf16[320,640]{1,0:T(8,128)(2,1)S(1)} %collective-permute-done.12), channel_id=1, source_target_pairs={{0,16},{16,0},{32,48},{48,32},{64,80},{80,64},{96,112},{112,96},{1... | collective-permute-start | bytes 1228808 | tf_op jit(solution)/shard_map/ppermute | solution.py:236
  80.0 5.1 %collective-permute-start.16 = (bf16[320,640]{1,0:T(8,128)(2,1)S(1)}, bf16[320,640]{1,0:T(8,128)(2,1)S(1)}, u32[]{:S(2)}, u32[]{:S(2)}) collective-permute-start(bf16[320,640]{1,0:T(8,128)(2,1)S(1)} %constant_dynamic-update-slice_fusion), channel_id=1, source_target_pairs={{0,16},{16,0},{32,48},{48,32},{64,80},{80,64},{96,112},{112,96},{1... | collective-permute-start | bytes 1228808 | tf_op jit(solution)/shard_map/ppermute | solution.py:236
  142.1 12.0 %copy-start.2 = (f32[320,256]{1,0:T(8,128)S(1)}, f32[320,256]{1,0:T(8,128)}, u32[]{:S(2)}) copy-start(f32[320,256]{1,0:T(8,128)} %param.16) | copy-start | bytes 983044
  154.3 64.0 %copy-start.1 = (f32[320,256]{1,0:T(8,128)}, f32[320,256]{1,0:T(8,128)S(1)}, u32[]{:S(2)}) copy-start(f32[320,256]{1,0:T(8,128)S(1)} %get-tuple-element.36) | copy-start | bytes 983044
  205.0 13.3 %copy-start = (f32[320,256]{1,0:T(8,128)S(1)}, f32[320,256]{1,0:T(8,128)}, u32[]{:S(2)}) copy-start(f32[320,256]{1,0:T(8,128)} %param.15) | copy-start | bytes 983044
  205.1 13.3 %copy-start.3 = (f32[320,256]{1,0:T(8,128)S(1)}, f32[320,256]{1,0:T(8,128)}, u32[]{:S(2)}) copy-start(f32[320,256]{1,0:T(8,128)} %param.19) | copy-start | bytes 983044
  205.1 13.3 %copy-start.4 = (f32[320,256]{1,0:T(8,128)S(1)}, f32[320,256]{1,0:T(8,128)}, u32[]{:S(2)}) copy-start(f32[320,256]{1,0:T(8,128)} %param.17) | copy-start | bytes 983044
  205.1 13.3 %copy-start.5 = (f32[320,256]{1,0:T(8,128)S(1)}, f32[320,256]{1,0:T(8,128)}, u32[]{:S(2)}) copy-start(f32[320,256]{1,0:T(8,128)} %param.18) | copy-start | bytes 983044

commit v6 on v5

--- a/solution.py
+++ b/solution.py
@@ -12,6 +12,7 @@
 Q = 4096
 CORES = 2
 SIDE = 4
+LANES = 128
 
 
 beta_first = 0.9
@@ -51,12 +52,12 @@
     return [(b, h) for b in range(tokens_ref.shape[0]) for h in range(tokens_ref.shape[2])]
 
 
-def token_spec(tokens):
-    cores, _, halves, rows, span = tokens.shape
-    return pl.BlockSpec((cores, 1, halves, rows, span), lambda q: (0, q, 0, 0, 0))
-
-
-def outputs_kernel(pub, spans, tokens_ref, w_ref, out_ref):
+def token_spec(tokens, lanes, at=0):
+    cores, _, halves, rows, _ = tokens.shape
+    return pl.BlockSpec((cores, 1, halves, rows, lanes), lambda q: (0, q, 0, 0, at))
+
+
+def outputs_kernel(priv, spans, tokens_ref, w_ref, out_ref):
     span = tokens_ref.shape[4]
     total = jnp.zeros((span, w_ref.shape[2]), jnp.float32)
     for side, (b, h) in enumerate(token_sides(tokens_ref)):
@@ -68,29 +69,37 @@
         )
     for owner in range(SIDE):
         pieces = []
-        for first, rows in ((0, spans[0]), (pub, spans[1])):
+        for first, rows in ((priv, spans[0]), (0, spans[1])):
             for x in range(SIDE):
                 at = first + (x * SIDE + owner) * rows
                 pieces.append(total[at : at + rows])
-        out_ref[owner, 0] = jnp.concatenate(pieces, axis=0).astype(out_ref.dtype)
-
-
-def outputs_by_owner(tokens, w_group, pub, spans):
+        owned = jnp.concatenate(pieces, axis=0).astype(out_ref.dtype)
+        for part in range(out_ref.shape[2]):
+            out_ref[owner, 0, part] = owned[:, part * LANES : (part + 1) * LANES]
+
+
+def outputs_by_owner(tokens, w_group, priv, spans):
     quads = tokens.shape[1]
     chunk, cols = SIDE * sum(spans), w_group.shape[2]
+    block = (SIDE, 1, cols // LANES, chunk, LANES)
     return pl.pallas_call(
-        lambda *refs: outputs_kernel(pub, spans, *refs),
+        lambda *refs: outputs_kernel(priv, spans, *refs),
         grid=(quads,),
-        in_specs=[token_spec(tokens), pl.BlockSpec(w_group.shape, lambda q: (0, 0, 0))],
-        out_specs=pl.BlockSpec((SIDE, 1, chunk, cols), lambda q: (0, q, 0, 0)),
-        out_shape=jax.ShapeDtypeStruct((SIDE, quads, chunk, cols), jnp.bfloat16),
+        in_specs=[
+            token_spec(tokens, tokens.shape[4]),
+            pl.BlockSpec(w_group.shape, lambda q: (0, 0, 0)),
+        ],
+        out_specs=pl.BlockSpec(block, lambda q: (0, q, 0, 0, 0)),
+        out_shape=jax.ShapeDtypeStruct((SIDE, quads, *block[2:]), jnp.bfloat16),
         name="outputs_by_owner",
     )(tokens, w_group)
 
 
-def public_kernel(pub, spans, tokens_ref, deltas_ref, out_ref, private_ref, acc_ref):
+def public_kernel(spans, low_ref, high_ref, deltas_ref, out_ref, private_ref, acc_ref):
     quad = pl.program_id(0)
-    deltas = deltas_ref[:, 0].astype(jnp.float32)
+    parts = deltas_ref.shape[2]
+    deltas = jnp.concatenate([deltas_ref[:, 0, part] for part in range(parts)], axis=-1)
+    deltas = deltas.astype(jnp.float32)
     ordered = []
     for first, rows in ((0, spans[0]), (SIDE * spans[0], spans[1])):
         pieces = [
@@ -105,48 +114,48 @@
     def _():
         acc_ref[...] = jnp.zeros_like(acc_ref)
 
-    for side, (b, h) in enumerate(token_sides(tokens_ref)):
-        acc_ref[side] += jnp.dot(
-            tokens_ref[b, 0, h, :, :pub], ordered[0], preferred_element_type=jnp.float32
-        )
+    for side, (b, h) in enumerate(token_sides(low_ref)):
+        block_x = jnp.concatenate([low_ref[b, 0, h], high_ref[b, 0, h]], axis=-1)
+        acc_ref[side] += jnp.dot(block_x, ordered[0], preferred_element_type=jnp.float32)
 
     @pl.when(quad == pl.num_programs(0) - 1)
     def _():
         out_ref[...] = acc_ref[...].astype(out_ref.dtype)
 
 
-def public_product(tokens, deltas, pub, spans):
-    cores, quads, halves, rows, span = tokens.shape
-    chunk, cols = deltas.shape[2:]
-    whole = (cores * halves, rows, cols)
+def public_product(tokens, deltas, priv, spans):
+    cores, quads, halves, rows, _ = tokens.shape
+    parts, chunk = deltas.shape[2:4]
+    whole = (cores * halves, rows, parts * LANES)
     return pl.pallas_call(
-        lambda *refs: public_kernel(pub, spans, *refs),
+        lambda *refs: public_kernel(spans, *refs),
         grid=(quads,),
         in_specs=[
-            token_spec(tokens),
-            pl.BlockSpec((SIDE, 1, chunk, cols), lambda q: (0, q, 0, 0)),
+            token_spec(tokens, L, priv // L),
+            token_spec(tokens, L, priv // L + 1),
+            pl.BlockSpec((SIDE, 1, parts, chunk, LANES), lambda q: (0, q, 0, 0, 0)),
         ],
         out_specs=[
             pl.BlockSpec(whole, lambda q: (0, 0, 0)),
-            pl.BlockSpec((1, span - pub, cols), lambda q: (q, 0, 0)),
+            pl.BlockSpec((1, priv, parts * LANES), lambda q: (q, 0, 0)),
         ],
         out_shape=[
             jax.ShapeDtypeStruct(whole, jnp.bfloat16),
-            jax.ShapeDtypeStruct((quads, span - pub, cols), jnp.bfloat16),
+            jax.ShapeDtypeStruct((quads, priv, parts * LANES), jnp.bfloat16),
         ],
         scratch_shapes=[pltpu.VMEM(whole, jnp.float32)],
         name="public_product",
-    )(tokens, deltas)
-
-
-def norms_kernel(pub, tokens_ref, delta_ref, precond_ref, out_ref):
+    )(tokens, tokens, deltas)
+
+
+def norms_kernel(tokens_ref, delta_ref, precond_ref, out_ref):
     rows = tokens_ref.shape[3]
     examples = delta_ref.shape[1] // L
     row_at = lax.broadcasted_iota(jnp.int32, out_ref.shape[1:], 0)
     found = jnp.zeros(out_ref.shape[1:], jnp.float32)
     for example in range(examples):
         block_d = delta_ref[0, example * L : (example + 1) * L, :]
-        first = pub + example * L
+        first = example * L
         acc = jnp.zeros((8, block_d.shape[1]), jnp.float32)
         for side, (b, h) in enumerate(token_sides(tokens_ref)):
             grads = jnp.dot(
@@ -160,13 +169,13 @@
     out_ref[0] = found
 
 
-def example_squares(tokens, deltas, precond, pub):
+def example_squares(tokens, deltas, precond):
     quads, priv, cols = deltas.shape
     out = pl.pallas_call(
-        lambda *refs: norms_kernel(pub, *refs),
+        norms_kernel,
         grid=(quads,),
         in_specs=[
-            token_spec(tokens),
+            token_spec(tokens, priv),
             pl.BlockSpec((1, priv, cols), lambda q: (q, 0, 0)),
             pl.BlockSpec(precond.shape, lambda q: (0, 0, 0)),
         ],
@@ -177,7 +186,7 @@
     return out[:, : priv // L, 0]
 
 
-def clipped_kernel(pub, factors_ref, tokens_ref, delta_ref, out_ref, acc_ref):
+def clipped_kernel(factors_ref, tokens_ref, delta_ref, out_ref, acc_ref):
     quad = pl.program_id(0)
     examples = delta_ref.shape[1] // L
     weighted = jnp.concatenate(
@@ -197,7 +206,7 @@
 
     for side, (b, h) in enumerate(token_sides(tokens_ref)):
         acc_ref[side] += jnp.dot(
-            tokens_ref[b, 0, h, :, pub:], weighted, preferred_element_type=jnp.float32
+            tokens_ref[b, 0, h], weighted, preferred_element_type=jnp.float32
         )
 
     @pl.when(quad == pl.num_programs(0) - 1)
@@ -205,16 +214,16 @@
         out_ref[...] = acc_ref[...].astype(out_ref.dtype)
 
 
-def clipped_sum(factors, tokens, deltas, pub):
-    cores, quads, halves, rows, span = tokens.shape
+def clipped_sum(factors, tokens, deltas):
+    cores, quads, halves, rows, _ = tokens.shape
     priv, cols = deltas.shape[1:]
     whole = (cores * halves, rows, cols)
     return pl.pallas_call(
-        lambda *refs: clipped_kernel(pub, *refs),
+        clipped_kernel,
         grid=(quads,),
         in_specs=[
             pl.BlockSpec(memory_space=pltpu.SMEM),
-            token_spec(tokens),
+            token_spec(tokens, priv),
             pl.BlockSpec((1, priv, cols), lambda q: (q, 0, 0)),
         ],
         out_specs=pl.BlockSpec(whole, lambda q: (0, 0, 0)),
@@ -224,7 +233,7 @@
     )(factors, tokens, deltas)
 
 
-def gather_tokens(own, replicas):
+def gather_tokens(own, moves, replicas, state, jobs):
     chips = replicas // CORES
     z = lax.div(lax.axis_index("replica"), CORES)
     up = [(r, (r + CORES) % replicas) for r in range(replicas)]
@@ -232,27 +241,37 @@
     swap = [(r, r ^ 1) for r in range(replicas)]
     held = jnp.zeros((CORES, chips, *own.shape), own.dtype)
 
-    def place(held, block, chip):
-        pair = jnp.stack([block, lax.ppermute(block, "replica", swap)])[:, None]
+    def swapped(block):
+        return jnp.stack([block, lax.ppermute(block, "replica", swap)])[:, None]
+
+    def place(held, pair, chip):
         return lax.dynamic_update_slice(held, pair, (0, lax.rem(chip, chips), 0, 0))
 
-    held = place(held, own, z)
+    own = lax.ppermute(own, ("replica", "tile"), moves)
+    state = jobs[0](state)
+    own, held, state = lax.optimization_barrier((own, held, state))
     below, above = own, own
+    waiting = [(swapped(own), z)]
     for step in range(1, chips // 2):
         below = lax.ppermute(below, "replica", up)
         above = lax.ppermute(above, "replica", down)
-        held = place(held, below, z + chips - step)
-        held = place(held, above, z + step)
+        for pair, chip in waiting:
+            held = place(held, pair, chip)
+        state = jobs[step](state)
+        below, above, held, state = lax.optimization_barrier((below, above, held, state))
+        waiting = [
+            (swapped(below), z + chips - step),
+            (swapped(above), z + step),
+        ]
     half = own.shape[0] // 2
-    last = jnp.concatenate(
-        [
-            lax.ppermute(below[:half], "replica", up),
-            lax.ppermute(above[half:], "replica", down),
-        ],
-        axis=0,
-    )
-    held = place(held, last, z + chips // 2)
-    return held.reshape(CORES, chips // 2, 2, *own.shape)
+    low = lax.ppermute(below[:half], "replica", up)
+    high = lax.ppermute(above[half:], "replica", down)
+    for pair, chip in waiting:
+        held = place(held, pair, chip)
+    low, high, held, state = lax.optimization_barrier((low, high, held, state))
+    last = jnp.concatenate([low, high], axis=0)
+    held = place(held, swapped(last), z + chips // 2)
+    return held.reshape(CORES, chips // 2, 2, *own.shape), state
 
 
 def on_device(
@@ -283,10 +302,11 @@
         jnp.arange(L, dtype=jnp.int32)[None, :] < token_counts[0][:, None]
     ).reshape(priv)
     live_tokens = jnp.where(live[:, None], private_tokens, jnp.zeros_like(private_tokens))
-    local = jnp.concatenate([public_tokens.T, live_tokens.T], axis=1)
-    local = lax.ppermute(local, ("replica", "tile"), moves)
-    tokens = gather_tokens(local, replicas)
+    local = jnp.concatenate([live_tokens.T, public_tokens.T], axis=1)
     core = lax.rem(lax.axis_index("replica"), CORES)
+    parts = cols // LANES
+    spans = (pub_rows, priv_rows)
+    chunk = SIDE * (pub_rows + priv_rows)
 
     def own_core_first(sides):
         split = sides.reshape(2, CORES, *sides.shape[1:])
@@ -298,29 +318,47 @@
         split = jnp.where(core == 0, split, split[::-1])
         return split.transpose(1, 0, 2, 3).reshape(mine.shape)
 
-    w_half = weight.astype(jnp.bfloat16)
-    w_group = own_core_first(
-        lax.all_to_all(
-            everywhere(w_half, SIDE), "tile", 0, 0, tiled=True, axis_index_groups=along_x
+    def across_x(sent):
+        return lax.all_to_all(sent, "tile", 0, 0, tiled=True, axis_index_groups=along_x)
+
+    def targets_to_columns(state):
+        targets, w_half = state
+        return lax.all_to_all(targets, "replica", 0, 0, tiled=True), w_half
+
+    def targets_to_class(state):
+        targets, w_half = state
+        targets = targets.reshape(quads, 2, CORES, -1, cols).transpose(2, 1, 0, 3, 4)
+        return across_x(targets.reshape(SIDE, -1, cols)), w_half
+
+    def weight_to_group(state):
+        targets, w_half = state
+        return targets, across_x(everywhere(w_half, SIDE))
+
+    def arranged(state):
+        targets, w_group = state
+        targets = targets.reshape(SIDE, quads, pub_rows + priv_rows, cols).transpose(1, 0, 2, 3)
+        targets = jnp.concatenate(
+            [
+                targets[:, :, :pub_rows].reshape(quads, SIDE * pub_rows, cols),
+                targets[:, :, pub_rows:].reshape(quads, SIDE * priv_rows, cols),
+            ],
+            axis=1,
         )
-    )
-
-    spans = (pub_rows, priv_rows)
-    chunk = SIDE * (pub_rows + priv_rows)
+        halves = [targets[:, None, :, p * LANES : (p + 1) * LANES] for p in range(parts)]
+        targets = jnp.concatenate(halves, axis=1).reshape(quads * parts * chunk, LANES)
+        return targets, own_core_first(w_group)
+
     targets = jnp.concatenate([public_targets, private_targets], axis=0)
-    targets = lax.ppermute(targets, ("replica", "tile"), moves)
     targets = targets.reshape(-1, replicas, cols).transpose(1, 0, 2)
-    targets = lax.all_to_all(targets, "replica", 0, 0, tiled=True)
-    targets = targets.reshape(quads, SIDE, pub_rows + priv_rows, cols)
-    targets = jnp.concatenate(
-        [
-            targets[:, :, :pub_rows].reshape(quads, SIDE * pub_rows, cols),
-            targets[:, :, pub_rows:].reshape(quads, SIDE * priv_rows, cols),
-        ],
-        axis=1,
-    ).reshape(quads * chunk, cols)
-
-    sent = outputs_by_owner(tokens, w_group, pub, spans).reshape(SIDE, quads * chunk, cols)
+    tokens, (targets, w_group) = gather_tokens(
+        local,
+        moves,
+        replicas,
+        (targets, weight.astype(jnp.bfloat16)),
+        [targets_to_columns, targets_to_class, weight_to_group, arranged],
+    )
+
+    sent = outputs_by_owner(tokens, w_group, priv, spans).reshape(SIDE, -1, LANES)
     got, (targets, tokens) = exchange(sent, "tile", along_y, (targets, tokens))
     total = jnp.sum(got.astype(jnp.float32), axis=0)
     delta = (total - targets.astype(jnp.float32)).astype(jnp.bfloat16)
@@ -333,7 +371,7 @@
         return jnp.sum(got.astype(jnp.float32), axis=0)
 
     product, private_delta = public_product(
-        tokens, deltas.reshape(SIDE, quads, chunk, cols), pub, spans
+        tokens, deltas.reshape(SIDE, quads, parts, chunk, LANES), priv, spans
     )
     public_grad = over_classes(product) / math.sqrt(pub * replicas)
     new_public = beta_public * public_moment + (1.0 - beta_public) * public_grad * public_grad
@@ -342,12 +380,12 @@
         everywhere(precond.astype(jnp.bfloat16), SIDE), "tile", along_x
     )
 
-    squares = example_squares(tokens, private_delta, own_core_first(precond_group), pub)
+    squares = example_squares(tokens, private_delta, own_core_first(precond_group))
     squares = jnp.sum(exchange(everywhere(squares, SIDE), "tile", along_y)[0], axis=0)
     squares = jnp.sum(exchange(everywhere(squares, replicas), "replica", None)[0], axis=0)
     clip_norm = clip_factor * math.sqrt(L * D * Q)
     factors = clip_norm / jnp.maximum(jnp.sqrt(squares), clip_norm)
-    summed = precond * over_classes(clipped_sum(factors, tokens, private_delta, pub))
+    summed = precond * over_classes(clipped_sum(factors, tokens, private_delta))
 
     examples_total = examples_here * replicas
     noise_scale = noise_level * clip_factor * math.sqrt(L)

time: 221 us -> 224 us (1.014)
  waiting for transfers between devices: 21.1 us -> 26.8 us
  other arithmetic: 20.4 us -> 15.9 us
  starting transfers between devices: 43.3 us -> 46.9 us
    ppermute x3, starting transfers between devices: 2.91 us -> 8.74 us  [gather_tokens(): below = lax.ppermute(below, 'replica', up)]
    ppermute x12 -> x11, starting transfers between devices: 16.8 us -> 13 us  [the longest x8 5 us: swapped(): return jnp.stack([block, lax.ppermute(block, 'replica', swap)])[:, None]]
    all_to_all x2 -> x3, waiting for transfers between devices: 2.78 us -> 5.58 us  [the longest x1 2.99 us: targets_to_columns(): return (lax.all_to_all(targets, 'replica', 0, 0, tiled=True), w_half)]
    ppermute x12 -> x11, waiting for transfers between devices: 7.35 us -> 9.2 us  [the longest x1 5.11 us: gather_tokens(): own = lax.ppermute(own, ('replica', 'tile'), moves)]
    all_to_all x2 -> x3, starting transfers between devices: 15.6 us -> 16.9 us  [the longest x1 9.97 us: targets_to_columns(): return (lax.all_to_all(targets, 'replica', 0, 0, tiled=True), w_half)]
  transfers between devices with their start and end apart: 20 -> 20, of which waited for: 5 -> 7; matrix products, arithmetic and copies ran while one was open for 8% -> 6% of each run, Pallas kernels for 0% -> 0%
where the time goes in v6:
time: 224 us; the launch traced here: 223 us
  blocking collectives  101 us (45%)
  starting transfers between devices  46.9 us (21%)
  waiting for transfers between devices  26.8 us (12%)
  Pallas kernels  22.7 us (10%)
  other arithmetic  15.9 us (7%)
  local copies, waits for them, and re-layouts  9.17 us (4%)
    all_to_all x7, blocking collectives, exchange(): got = lax.all_to_all(sent, axis, 0, 0, tiled=True, axis_index_groups=groups)  101 us
    ppermute x3, waiting for transfers between devices, gather_tokens(): below = lax.ppermute(below, 'replica', up)  12 us
    all_to_all x1, starting transfers between devices, targets_to_columns(): return (lax.all_to_all(targets, 'replica', 0, 0, tiled=True), w_half)  9.97 us
    dynamic_update_slice x8, other arithmetic, place(): return lax.dynamic_update_slice(held, pair, (0, lax.rem(chip, chips), 0, 0))  8.86 us
    ppermute x3, starting transfers between devices, gather_tokens(): below = lax.ppermute(below, 'replica', up)  8.74 us
    ppermute x3, starting transfers between devices, gather_tokens(): above = lax.ppermute(above, 'replica', down)  8.19 us
    all_to_all x2, starting transfers between devices, across_x(): lax.all_to_all(sent, 'tile', 0, 0, tiled=True, axis_index_groups=along_x)  6.94 us
    pallas_call x1, Pallas kernels, outputs_by_owner(): pl.pallas_call(lambda *refs: outputs_kernel(priv, spans, *refs), grid=(qu...  6.67 us
  transfers between devices with their start and end apart: 20, of which 7 were waited for; matrix products, arithmetic and copies ran while one was open for 6% of the time, Pallas kernels for 0%

profile of v6, /device:TPU:1, one launch (start us, length us, event | category | flops | bytes accessed | tf_op | source)
XLA Modules:
  0.0 223.1 jit_solution(11345012992003158960)
XLA Ops:
  2.6 10.0 %all-to-all-start = ((bf16[16,40,256]{2,1,0:T(8,128)(2,1)}), bf16[16,40,256]{2,1,0:T(8,128)(2,1)S(1)}, u32[]{:S(2)}, u32[]{:S(2)}) async-start(bf16[16,40,256]{2,1,0:T(8,128)(2,1)} %copy.70), calls=%async_computation | async-start | bytes 655360 | tf_op jit(solution)/shard_map/all_to_all | solution.py:326
  12.8 4.6 %collective-permute-start = (bf16[320,640]{1,0:T(8,128)(2,1)S(1)}, bf16[320,640]{1,0:T(8,128)(2,1)S(1)}, u32[]{:S(2)}, u32[]{:S(2)}) collective-permute-start(bf16[320,640]{1,0:T(8,128)(2,1)S(1)} %pad_maximum_fusion), channel_id=1, source_target_pairs={{0,0},{1,1},{2,2},{3,3},{4,16},{5,17},{6,18},{7,19},{8,32},{9,33},... | collective-permute-start | bytes 1228808 | tf_op jit(solution)/shard_map/ppermute | solution.py:250
  17.5 5.1 %collective-permute-done = bf16[320,640]{1,0:T(8,128)(2,1)S(1)} collective-permute-done((bf16[320,640]{1,0:T(8,128)(2,1)S(1)}, bf16[320,640]{1,0:T(8,128)(2,1)S(1)}, u32[]{:S(2)}, u32[]{:S(2)}) %collective-permute-start) | collective-permute-done | bytes 409632 | tf_op jit(solution)/shard_map/ppermute | solution.py:250
  22.6 3.0 %all-to-all-done = bf16[16,40,256]{2,1,0:T(8,128)(2,1)S(1)} async-done(((bf16[16,40,256]{2,1,0:T(8,128)(2,1)}), bf16[16,40,256]{2,1,0:T(8,128)(2,1)S(1)}, u32[]{:S(2)}, u32[]{:S(2)}) %all-to-all-start) | async-done | bytes 327712 | tf_op jit(solution)/shard_map/all_to_all | solution.py:326
  25.6 8.7 %collective-permute-start.1 = (bf16[320,640]{1,0:T(8,128)(2,1)S(1)}, bf16[320,640]{1,0:T(8,128)(2,1)S(1)}, u32[]{:S(2)}, u32[]{:S(2)}) collective-permute-start(bf16[320,640]{1,0:T(8,128)(2,1)S(1)} %collective-permute-done), channel_id=1, source_target_pairs={{0,32},{16,48},{32,64},{48,80},{64,96},{80,112},{96,128},{112,144}... | collective-permute-start | bytes 1228808 | tf_op jit(solution)/shard_map/ppermute | solution.py:256
  34.2 2.7 %collective-permute-start.2 = (bf16[320,640]{1,0:T(8,128)(2,1)S(1)}, bf16[320,640]{1,0:T(8,128)(2,1)S(1)}, u32[]{:S(2)}, u32[]{:S(2)}) collective-permute-start(bf16[320,640]{1,0:T(8,128)(2,1)S(1)} %collective-permute-done), channel_id=1, source_target_pairs={{0,224},{16,240},{32,0},{48,16},{64,32},{80,48},{96,64},{112,80},{... | collective-permute-start | bytes 1228808 | tf_op jit(solution)/shard_map/ppermute | solution.py:257
  37.7 3.5 %all-to-all-start.1 = ((bf16[4,160,256]{2,1,0:T(8,128)(2,1)}), bf16[4,160,256]{2,1,0:T(8,128)(2,1)S(1)}, u32[]{:S(2)}, u32[]{:S(2)}) async-start(bf16[4,160,256]{2,1,0:T(8,128)(2,1)} %bitcast.11), calls=%async_computation.1 | async-start | bytes 655360 | tf_op jit(solution)/shard_map/all_to_all | solution.py:322
  41.2 3.5 %broadcast_in_dim.78 = bf16[2,8,320,640]{3,2,1,0:T(8,128)(2,1)} broadcast(bf16[]{:T(256)} %constant.61.clone.1), dimensions={} | broadcast | bytes 6553602 | tf_op jit(solution)/shard_map/broadcast_in_dim | solution.py:242
  45.6 2.6 %all-to-all-done.1 = bf16[4,160,256]{2,1,0:T(8,128)(2,1)S(1)} async-done(((bf16[4,160,256]{2,1,0:T(8,128)(2,1)}), bf16[4,160,256]{2,1,0:T(8,128)(2,1)S(1)}, u32[]{:S(2)}, u32[]{:S(2)}) %all-to-all-start.1) | async-done | bytes 327712 | tf_op jit(solution)/shard_map/all_to_all | solution.py:322
  50.4 3.5 %all-to-all-start.2 = ((bf16[4,320,256]{2,1,0:T(8,128)(2,1)}), bf16[4,320,256]{2,1,0:T(8,128)(2,1)S(1)}, u32[]{:S(2)}, u32[]{:S(2)}) async-start(bf16[4,320,256]{2,1,0:T(8,128)(2,1)} %broadcast_in_dim.82), calls=%async_computation.2 | async-start | bytes 1310720 | tf_op jit(solution)/shard_map/all_to_all | solution.py:322
  54.0 2.7 %collective-permute-start.5 = (bf16[320,640]{1,0:T(8,128)(2,1)S(1)}, bf16[320,640]{1,0:T(8,128)(2,1)S(1)}, u32[]{:S(2)}, u32[]{:S(2)}) collective-permute-start(bf16[320,640]{1,0:T(8,128)(2,1)S(1)} %collective-permute-done.2), channel_id=1, source_target_pairs={{0,224},{16,240},{32,0},{48,16},{64,32},{80,48},{96,64},{112,80},{... | collective-permute-start | bytes 1228808 | tf_op jit(solution)/shard_map/ppermute | solution.py:257
  56.7 2.0 fusion.1
  59.6 6.2 %collective-permute-done.4 = bf16[320,640]{1,0:T(8,128)(2,1)S(1)} collective-permute-done((bf16[320,640]{1,0:T(8,128)(2,1)S(1)}, bf16[320,640]{1,0:T(8,128)(2,1)S(1)}, u32[]{:S(2)}, u32[]{:S(2)}) %collective-permute-start.4) | collective-permute-done | bytes 409632 | tf_op jit(solution)/shard_map/ppermute | solution.py:256
  65.8 1.4 collective-permute-start.10
  67.4 2.9 %collective-permute-start.9 = (bf16[320,640]{1,0:T(8,128)(2,1)S(1)}, bf16[320,640]{1,0:T(8,128)(2,1)S(1)}, u32[]{:S(2)}, u32[]{:S(2)}) collective-permute-start(bf16[320,640]{1,0:T(8,128)(2,1)S(1)} %collective-permute-done.5), channel_id=1, source_target_pairs={{0,224},{16,240},{32,0},{48,16},{64,32},{80,48},{96,64},{112,80},{... | collective-permute-start | bytes 1228808 | tf_op jit(solution)/shard_map/ppermute | solution.py:257
  73.5 5.8 %collective-permute-done.8 = bf16[320,640]{1,0:T(8,128)(2,1)S(1)} collective-permute-done((bf16[320,640]{1,0:T(8,128)(2,1)S(1)}, bf16[320,640]{1,0:T(8,128)(2,1)S(1)}, u32[]{:S(2)}, u32[]{:S(2)}) %collective-permute-start.8) | collective-permute-done | bytes 409632 | tf_op jit(solution)/shard_map/ppermute | solution.py:256
  81.6 2.2 collective-permute-start.13
  85.7 2.7 %collective-permute-done.12 = bf16[160,640]{1,0:T(8,128)(2,1)S(1)} collective-permute-done((bf16[160,640]{1,0:T(8,128)(2,1)S(1)}, bf16[160,640]{1,0:T(8,128)(2,1)S(1)}, u32[]{:S(2)}, u32[]{:S(2)}) %collective-permute-start.12) | collective-permute-done | bytes 204832 | tf_op jit(solution)/shard_map/ppermute | solution.py:267
  89.6 1.4 collective-permute-done.16
  92.0 6.7 %outputs_by_owner.1 = bf16[4,4,2,160,128]{4,3,2,1,0:T(8,128)(2,1)} custom-call(bf16[2,4,2,320,640]{4,3,2,1,0:T(8,128)(2,1)} %bitcast.51.refs_0_.refs_1_.tokens_ref, bf16[4,320,256]{2,1,0:T(8,128)(2,1)} %bitcast.109), custom_call_target="tpu_custom_call" | custom-call | tf_op jit(solution)/shard_map/outputs_by_owner/pallas_call | solution.py:85
  98.7 21.2 %all_to_all.50 = bf16[4,1280,128]{2,1,0:T(8,128)(2,1)S(1)} all-to-all(bf16[4,1280,128]{2,1,0:T(8,128)(2,1)} %bitcast.108), channel_id=1, replica_groups={{0,1,2,3},{4,5,6,7},{8,9,10,11},{12,13,14,15},{16,17,18,19},{20,21,22,2..., dimensions={0} | all-to-all | bytes 2621440 | tf_op jit(solution)/shard_map/all_to_all | solution.py:30
  120.4 19.4 %all_to_all.51 = bf16[4,1280,128]{2,1,0:T(8,128)(2,1)} all-to-all(bf16[4,1280,128]{2,1,0:T(8,128)(2,1)S(1)} %broadcast_in_dim.90), channel_id=1, replica_groups={{0,1,2,3},{4,5,6,7},{8,9,10,11},{12,13,14,15},{16,17,18,19},{20,21,22,2..., dimensions={0} | all-to-all | bytes 2621440 | tf_op jit(solution)/shard_map/all_to_all | solution.py:30
  139.7 5.0 %public_product.1 = (bf16[4,320,256]{2,1,0:T(8,128)(2,1)}, bf16[4,384,256]{2,1,0:T(8,128)(2,1)}) custom-call(bf16[2,4,2,320,640]{4,3,2,1,0:T(8,128)(2,1)} %bitcast.51.refs_0_.refs_1_.tokens_ref, bf16[2,4,2,320,640]{4,3,2,1,0:T(8,128)(2,1)} %bitcast.51.refs_0_.refs_1_.tokens_ref, bf16[4,4,2,160,128]{4,3,2,1,0:T(8,128)(2,1)} %bitcast.107), custom_call_target="tpu_custom_call" | custom-call | tf_op jit(solution)/shard_map/public_product/pallas_call | solution.py:130
  144.7 1.5 fusion.9
  146.3 11.8 %all_to_all.52 = bf16[4,320,256]{2,1,0:T(8,128)(2,1)S(1)} all-to-all(bf16[4,320,256]{2,1,0:T(8,128)(2,1)S(1)} %bitcast.112), channel_id=1, replica_groups={{0,4,8,12},{1,5,9,13},{2,6,10,14},{3,7,11,15},{16,20,24,28},{17,21,25,2..., dimensions={0} | all-to-all | bytes 1310720 | tf_op jit(solution)/shard_map/all_to_all | solution.py:30
  158.4 10.0 %all_to_all.53 = bf16[4,320,256]{2,1,0:T(8,128)(2,1)S(1)} all-to-all(bf16[4,320,256]{2,1,0:T(8,128)(2,1)S(1)} %broadcast_in_dim.91), channel_id=1, replica_groups={{0,4,8,12},{1,5,9,13},{2,6,10,14},{3,7,11,15},{16,20,24,28},{17,21,25,2..., dimensions={0} | all-to-all | bytes 1310720 | tf_op jit(solution)/shard_map/all_to_all | solution.py:30
  169.5 5.8 %example_squares.1 = f32[4,8,128]{2,1,0:T(8,128)} custom-call(bf16[2,4,2,320,640]{4,3,2,1,0:T(8,128)(2,1)} %bitcast.51.refs_0_.refs_1_.tokens_ref, bf16[4,384,256]{2,1,0:T(8,128)(2,1)} %get-tuple-element.79.delta_ref, bf16[4,320,256]{2,1,0:T(8,128)(2,1)} %bitcast.115), custom_call_target="tpu_custom_call" | custom-call | tf_op jit(solution)/shard_map/example_squares/pallas_call | solution.py:174
  176.1 6.5 %all_to_all.54 = f32[4,4,3]{2,1,0:T(4,128)S(1)} all-to-all(f32[4,4,3]{2,1,0:T(4,128)S(1)} %broadcast_in_dim.93), channel_id=1, replica_groups={{0,1,2,3},{4,5,6,7},{8,9,10,11},{12,13,14,15},{16,17,18,19},{20,21,22,2..., dimensions={0} | all-to-all | bytes 384 | tf_op jit(solution)/shard_map/all_to_all | solution.py:30
  182.7 18.6 %all_to_all.55 = f32[16,4,3]{2,1,0:T(4,128)S(1)} all-to-all(f32[16,4,3]{2,1,0:T(4,128)S(1)} %broadcast_in_dim.94), channel_id=1, replica_groups=mesh['replica'=16,'tile'=16] {'replica'}, dimensions={0} | all-to-all | bytes 1536 | tf_op jit(solution)/shard_map/all_to_all | solution.py:30
  201.8 5.2 %clipped_sum.1 = bf16[4,320,256]{2,1,0:T(8,128)(2,1)} custom-call(f32[4,3]{1,0:T(4,128)} %maximum_divide_fusion.factors_ref, bf16[2,4,2,320,640]{4,3,2,1,0:T(8,128)(2,1)} %bitcast.51.refs_0_.refs_1_.tokens_ref, bf16[4,384,256]{2,1,0:T(8,128)(2,1)} %get-tuple-element.79.delta_ref), custom_call_target="tpu_custom_call" | custom-call | tf_op jit(solution)/shard_map/clipped_sum/pallas_call | solution.py:221
  207.0 1.5 fusion.11
  208.6 13.1 %all_to_all.56 = bf16[4,320,256]{2,1,0:T(8,128)(2,1)S(1)} all-to-all(bf16[4,320,256]{2,1,0:T(8,128)(2,1)S(1)} %bitcast.114), channel_id=1, replica_groups={{0,4,8,12},{1,5,9,13},{2,6,10,14},{3,7,11,15},{16,20,24,28},{17,21,25,2..., dimensions={0} | all-to-all | bytes 1310720 | tf_op jit(solution)/shard_map/all_to_all | solution.py:30
  (88 shorter events, 21.6 us)
Async XLA Ops:
  0.6 12.0 %copy-start.8 = (s32[1,3]{1,0:T(1,128)S(1)}, s32[1,3]{1,0:T(1,128)}, u32[]{:S(2)}) copy-start(s32[1,3]{1,0:T(1,128)} %param.14) | copy-start | bytes 40
  0.6 12.1 %copy-start.6 = (bf16[384,320]{0,1:T(8,128)(2,1)S(1)}, bf16[384,320]{0,1:T(8,128)(2,1)}, u32[]{:S(2)}) copy-start(bf16[384,320]{0,1:T(8,128)(2,1)} %param.12) | copy-start | bytes 737284
  0.7 12.1 %copy-start.7 = (bf16[256,320]{0,1:T(8,128)(2,1)S(1)}, bf16[256,320]{0,1:T(8,128)(2,1)}, u32[]{:S(2)}) copy-start(bf16[256,320]{0,1:T(8,128)(2,1)} %param.10) | copy-start | bytes 491524
  1.7 15.7 %copy-start = (f32[320,256]{1,0:T(8,128)S(1)}, f32[320,256]{1,0:T(8,128)}, u32[]{:S(2)}) copy-start(f32[320,256]{1,0:T(8,128)} %param.15) | copy-start | bytes 983044
  2.6 22.9 %all-to-all-start = ((bf16[16,40,256]{2,1,0:T(8,128)(2,1)}), bf16[16,40,256]{2,1,0:T(8,128)(2,1)S(1)}, u32[]{:S(2)}, u32[]{:S(2)}) async-start(bf16[16,40,256]{2,1,0:T(8,128)(2,1)} %copy.70), calls=%async_computation | async-start | bytes 655360 | tf_op jit(solution)/shard_map/all_to_all | solution.py:326
  12.8 9.8 %collective-permute-start = (bf16[320,640]{1,0:T(8,128)(2,1)S(1)}, bf16[320,640]{1,0:T(8,128)(2,1)S(1)}, u32[]{:S(2)}, u32[]{:S(2)}) collective-permute-start(bf16[320,640]{1,0:T(8,128)(2,1)S(1)} %pad_maximum_fusion), channel_id=1, source_target_pairs={{0,0},{1,1},{2,2},{3,3},{4,16},{5,17},{6,18},{7,19},{8,32},{9,33},... | collective-permute-start | bytes 1228808 | tf_op jit(solution)/shard_map/ppermute | solution.py:250
  25.6 15.6 %collective-permute-start.3 = (bf16[320,640]{1,0:T(8,128)(2,1)S(1)}, bf16[320,640]{1,0:T(8,128)(2,1)S(1)}, u32[]{:S(2)}, u32[]{:S(2)}) collective-permute-start(bf16[320,640]{1,0:T(8,128)(2,1)S(1)} %collective-permute-done), channel_id=1, source_target_pairs={{0,16},{16,0},{32,48},{48,32},{64,80},{80,64},{96,112},{112,96},{1... | collective-permute-start | bytes 1228808 | tf_op jit(solution)/shard_map/ppermute | solution.py:245
  25.6 22.6 %collective-permute-start.1 = (bf16[320,640]{1,0:T(8,128)(2,1)S(1)}, bf16[320,640]{1,0:T(8,128)(2,1)S(1)}, u32[]{:S(2)}, u32[]{:S(2)}) collective-permute-start(bf16[320,640]{1,0:T(8,128)(2,1)S(1)} %collective-permute-done), channel_id=1, source_target_pairs={{0,32},{16,48},{32,64},{48,80},{64,96},{80,112},{96,128},{112,144}... | collective-permute-start | bytes 1228808 | tf_op jit(solution)/shard_map/ppermute | solution.py:256
  34.2 14.0 %collective-permute-start.2 = (bf16[320,640]{1,0:T(8,128)(2,1)S(1)}, bf16[320,640]{1,0:T(8,128)(2,1)S(1)}, u32[]{:S(2)}, u32[]{:S(2)}) collective-permute-start(bf16[320,640]{1,0:T(8,128)(2,1)S(1)} %collective-permute-done), channel_id=1, source_target_pairs={{0,224},{16,240},{32,0},{48,16},{64,32},{80,48},{96,64},{112,80},{... | collective-permute-start | bytes 1228808 | tf_op jit(solution)/shard_map/ppermute | solution.py:257
  37.7 10.5 %all-to-all-start.1 = ((bf16[4,160,256]{2,1,0:T(8,128)(2,1)}), bf16[4,160,256]{2,1,0:T(8,128)(2,1)S(1)}, u32[]{:S(2)}, u32[]{:S(2)}) async-start(bf16[4,160,256]{2,1,0:T(8,128)(2,1)} %bitcast.11), calls=%async_computation.1 | async-start | bytes 655360 | tf_op jit(solution)/shard_map/all_to_all | solution.py:322
  48.2 8.5 %collective-permute-start.6 = (bf16[320,640]{1,0:T(8,128)(2,1)S(1)}, bf16[320,640]{1,0:T(8,128)(2,1)}, u32[]{:S(2)}, u32[]{:S(2)}) collective-permute-start(bf16[320,640]{1,0:T(8,128)(2,1)S(1)} %collective-permute-done.1), channel_id=1, source_target_pairs={{0,16},{16,0},{32,48},{48,32},{64,80},{80,64},{96,112},{112,96},{1... | collective-permute-start | bytes 1228808 | tf_op jit(solution)/shard_map/ppermute | solution.py:245
  49.4 9.2 %collective-permute-start.7 = (bf16[320,640]{1,0:T(8,128)(2,1)S(1)}, bf16[320,640]{1,0:T(8,128)(2,1)S(1)}, u32[]{:S(2)}, u32[]{:S(2)}) collective-permute-start(bf16[320,640]{1,0:T(8,128)(2,1)S(1)} %collective-permute-done.2), channel_id=1, source_target_pairs={{0,16},{16,0},{32,48},{48,32},{64,80},{80,64},{96,112},{112,96},{1... | collective-permute-start | bytes 1228808 | tf_op jit(solution)/shard_map/ppermute | solution.py:245
  50.4 15.4 %all-to-all-start.2 = ((bf16[4,320,256]{2,1,0:T(8,128)(2,1)}), bf16[4,320,256]{2,1,0:T(8,128)(2,1)S(1)}, u32[]{:S(2)}, u32[]{:S(2)}) async-start(bf16[4,320,256]{2,1,0:T(8,128)(2,1)} %broadcast_in_dim.82), calls=%async_computation.2 | async-start | bytes 1310720 | tf_op jit(solution)/shard_map/all_to_all | solution.py:322
  53.9 11.9 %collective-permute-start.4 = (bf16[320,640]{1,0:T(8,128)(2,1)S(1)}, bf16[320,640]{1,0:T(8,128)(2,1)S(1)}, u32[]{:S(2)}, u32[]{:S(2)}) collective-permute-start(bf16[320,640]{1,0:T(8,128)(2,1)S(1)} %collective-permute-done.1), channel_id=1, source_target_pairs={{0,32},{16,48},{32,64},{48,80},{64,96},{80,112},{96,128},{112,144}... | collective-permute-start | bytes 1228808 | tf_op jit(solution)/shard_map/ppermute | solution.py:256
  54.0 11.8 %collective-permute-start.5 = (bf16[320,640]{1,0:T(8,128)(2,1)S(1)}, bf16[320,640]{1,0:T(8,128)(2,1)S(1)}, u32[]{:S(2)}, u32[]{:S(2)}) collective-permute-start(bf16[320,640]{1,0:T(8,128)(2,1)S(1)} %collective-permute-done.2), channel_id=1, source_target_pairs={{0,224},{16,240},{32,0},{48,16},{64,32},{80,48},{96,64},{112,80},{... | collective-permute-start | bytes 1228808 | tf_op jit(solution)/shard_map/ppermute | solution.py:257
  65.8 5.7 %collective-permute-start.10 = (bf16[320,640]{1,0:T(8,128)(2,1)S(1)}, bf16[320,640]{1,0:T(8,128)(2,1)S(1)}, u32[]{:S(2)}, u32[]{:S(2)}) collective-permute-start(bf16[320,640]{1,0:T(8,128)(2,1)S(1)} %collective-permute-done.4), channel_id=1, source_target_pairs={{0,16},{16,0},{32,48},{48,32},{64,80},{80,64},{96,112},{112,96},{1... | collective-permute-start | bytes 1228808 | tf_op jit(solution)/shard_map/ppermute | solution.py:245
  67.2 12.1 %collective-permute-start.8 = (bf16[320,640]{1,0:T(8,128)(2,1)S(1)}, bf16[320,640]{1,0:T(8,128)(2,1)S(1)}, u32[]{:S(2)}, u32[]{:S(2)}) collective-permute-start(bf16[320,640]{1,0:T(8,128)(2,1)S(1)} %collective-permute-done.4), channel_id=1, source_target_pairs={{0,32},{16,48},{32,64},{48,80},{64,96},{80,112},{96,128},{112,144}... | collective-permute-start | bytes 1228808 | tf_op jit(solution)/shard_map/ppermute | solution.py:256
  67.2 5.3 %collective-permute-start.11 = (bf16[320,640]{1,0:T(8,128)(2,1)S(1)}, bf16[320,640]{1,0:T(8,128)(2,1)S(1)}, u32[]{:S(2)}, u32[]{:S(2)}) collective-permute-start(bf16[320,640]{1,0:T(8,128)(2,1)S(1)} %collective-permute-done.5), channel_id=1, source_target_pairs={{0,16},{16,0},{32,48},{48,32},{64,80},{80,64},{96,112},{112,96},{1... | collective-permute-start | bytes 1228808 | tf_op jit(solution)/shard_map/ppermute | solution.py:245
  67.4 12.0 %collective-permute-start.9 = (bf16[320,640]{1,0:T(8,128)(2,1)S(1)}, bf16[320,640]{1,0:T(8,128)(2,1)S(1)}, u32[]{:S(2)}, u32[]{:S(2)}) collective-permute-start(bf16[320,640]{1,0:T(8,128)(2,1)S(1)} %collective-permute-done.5), channel_id=1, source_target_pairs={{0,224},{16,240},{32,0},{48,16},{64,32},{80,48},{96,64},{112,80},{... | collective-permute-start | bytes 1228808 | tf_op jit(solution)/shard_map/ppermute | solution.py:257
  79.3 4.4 %collective-permute-start.14 = (bf16[320,640]{1,0:T(8,128)(2,1)S(1)}, bf16[320,640]{1,0:T(8,128)(2,1)S(1)}, u32[]{:S(2)}, u32[]{:S(2)}) collective-permute-start(bf16[320,640]{1,0:T(8,128)(2,1)S(1)} %collective-permute-done.8), channel_id=1, source_target_pairs={{0,16},{16,0},{32,48},{48,32},{64,80},{80,64},{96,112},{112,96},{1... | collective-permute-start | bytes 1228808 | tf_op jit(solution)/shard_map/ppermute | solution.py:245
  80.3 4.4 %collective-permute-start.15 = (bf16[320,640]{1,0:T(8,128)(2,1)S(1)}, bf16[320,640]{1,0:T(8,128)(2,1)S(1)}, u32[]{:S(2)}, u32[]{:S(2)}) collective-permute-start(bf16[320,640]{1,0:T(8,128)(2,1)S(1)} %collective-permute-done.9), channel_id=1, source_target_pairs={{0,16},{16,0},{32,48},{48,32},{64,80},{80,64},{96,112},{112,96},{1... | collective-permute-start | bytes 1228808 | tf_op jit(solution)/shard_map/ppermute | solution.py:245
  80.3 8.1 %collective-permute-start.12 = (bf16[160,640]{1,0:T(8,128)(2,1)S(1)}, bf16[160,640]{1,0:T(8,128)(2,1)S(1)}, u32[]{:S(2)}, u32[]{:S(2)}) collective-permute-start(bf16[160,640]{1,0:T(8,128)(2,1)S(1)} %slice.25), channel_id=1, source_target_pairs={{0,32},{16,48},{32,64},{48,80},{64,96},{80,112},{96,128},{112,144}... | collective-permute-start | bytes 614408 | tf_op jit(solution)/shard_map/ppermute | solution.py:267
  81.6 6.8 %collective-permute-start.13 = (bf16[160,640]{1,0:T(8,128)(2,1)S(1)}, bf16[160,640]{1,0:T(8,128)(2,1)S(1)}, u32[]{:S(2)}, u32[]{:S(2)}) collective-permute-start(bf16[160,640]{1,0:T(8,128)(2,1)S(1)} %slice.26), channel_id=1, source_target_pairs={{0,224},{16,240},{32,0},{48,16},{64,32},{80,48},{96,64},{112,80},{... | collective-permute-start | bytes 614408 | tf_op jit(solution)/shard_map/ppermute | solution.py:268
  88.5 2.5 %collective-permute-start.16 = (bf16[320,640]{1,0:T(8,128)(2,1)S(1)}, bf16[320,640]{1,0:T(8,128)(2,1)S(1)}, u32[]{:S(2)}, u32[]{:S(2)}) collective-permute-start(bf16[320,640]{1,0:T(8,128)(2,1)S(1)} %constant_dynamic-update-slice_fusion), channel_id=1, source_target_pairs={{0,16},{16,0},{32,48},{48,32},{64,80},{80,64},{96,112},{112,96},{1... | collective-permute-start | bytes 1228808 | tf_op jit(solution)/shard_map/ppermute | solution.py:245
  146.2 12.0 %copy-start.2 = (f32[320,256]{1,0:T(8,128)S(1)}, f32[320,256]{1,0:T(8,128)}, u32[]{:S(2)}) copy-start(f32[320,256]{1,0:T(8,128)} %param.16) | copy-start | bytes 983044
  158.4 63.4 %copy-start.1 = (f32[320,256]{1,0:T(8,128)}, f32[320,256]{1,0:T(8,128)S(1)}, u32[]{:S(2)}) copy-start(f32[320,256]{1,0:T(8,128)S(1)} %get-tuple-element.84) | copy-start | bytes 983044
  208.5 13.3 %copy-start.3 = (f32[320,256]{1,0:T(8,128)S(1)}, f32[320,256]{1,0:T(8,128)}, u32[]{:S(2)}) copy-start(f32[320,256]{1,0:T(8,128)} %param.19) | copy-start | bytes 983044
  208.5 13.3 %copy-start.4 = (f32[320,256]{1,0:T(8,128)S(1)}, f32[320,256]{1,0:T(8,128)}, u32[]{:S(2)}) copy-start(f32[320,256]{1,0:T(8,128)} %param.17) | copy-start | bytes 983044
  208.5 13.3 %copy-start.5 = (f32[320,256]{1,0:T(8,128)S(1)}, f32[320,256]{1,0:T(8,128)}, u32[]{:S(2)}) copy-start(f32[320,256]{1,0:T(8,128)} %param.18) | copy-start | bytes 983044

commit v7 on v4

--- a/solution.py
+++ b/solution.py
@@ -47,14 +47,14 @@
     return moves
 
 
-def norms_kernel(pub, tokens_ref, delta_ref, precond_ref, out_ref):
+def norms_kernel(tokens_ref, delta_ref, precond_ref, out_ref):
     sides, rows = tokens_ref.shape[1], tokens_ref.shape[2]
     examples = delta_ref.shape[1] // L
     row_at = lax.broadcasted_iota(jnp.int32, out_ref.shape[1:], 0)
     found = jnp.zeros(out_ref.shape[1:], jnp.float32)
     for example in range(examples):
         block_d = delta_ref[0, example * L : (example + 1) * L, :]
-        first = pub + example * L
+        first = example * L
         acc = jnp.zeros((8, block_d.shape[1]), jnp.float32)
         for side in range(sides):
             grads = jnp.dot(
@@ -68,14 +68,14 @@
     out_ref[0] = found
 
 
-def example_squares(tokens, deltas, precond, pub):
-    quads, sides, rows, span = tokens.shape
+def example_squares(tokens, deltas, precond):
+    quads, sides, rows, _ = tokens.shape
     priv, cols = deltas.shape[1:]
     out = pl.pallas_call(
-        lambda *refs: norms_kernel(pub, *refs),
+        norms_kernel,
         grid=(quads,),
         in_specs=[
-            pl.BlockSpec((1, sides, rows, span), lambda q: (q, 0, 0, 0)),
+            pl.BlockSpec((1, sides, rows, priv), lambda q: (q, 0, 0, 0)),
             pl.BlockSpec((1, priv, cols), lambda q: (q, 0, 0)),
             pl.BlockSpec((sides, rows, cols), lambda q: (0, 0, 0)),
         ],
@@ -86,7 +86,7 @@
     return out[:, : priv // L, 0]
 
 
-def clipped_kernel(pub, factors_ref, tokens_ref, delta_ref, out_ref, acc_ref):
+def clipped_kernel(factors_ref, tokens_ref, delta_ref, out_ref, acc_ref):
     quad = pl.program_id(0)
     examples = delta_ref.shape[1] // L
     weighted = jnp.concatenate(
@@ -106,7 +106,7 @@
 
     for side in range(tokens_ref.shape[1]):
         acc_ref[side] += jnp.dot(
-            tokens_ref[0, side, :, pub:], weighted, preferred_element_type=jnp.float32
+            tokens_ref[0, side], weighted, preferred_element_type=jnp.float32
         )
 
     @pl.when(quad == pl.num_programs(0) - 1)
@@ -114,15 +114,15 @@
         out_ref[...] = acc_ref[...].astype(out_ref.dtype)
 
 
-def clipped_sum(factors, tokens, deltas, pub):
-    quads, sides, rows, span = tokens.shape
+def clipped_sum(factors, tokens, deltas):
+    quads, sides, rows, _ = tokens.shape
     priv, cols = deltas.shape[1:]
     return pl.pallas_call(
-        lambda *refs: clipped_kernel(pub, *refs),
+        clipped_kernel,
         grid=(quads,),
         in_specs=[
             pl.BlockSpec(memory_space=pltpu.SMEM),
-            pl.BlockSpec((1, sides, rows, span), lambda q: (q, 0, 0, 0)),
+            pl.BlockSpec((1, sides, rows, priv), lambda q: (q, 0, 0, 0)),
             pl.BlockSpec((1, priv, cols), lambda q: (q, 0, 0)),
         ],
         out_specs=pl.BlockSpec((sides, rows, cols), lambda q: (0, 0, 0)),
@@ -147,6 +147,10 @@
     replicas = lax.axis_size("replica")
     along_x = [[x * SIDE + y for x in range(SIDE)] for y in range(SIDE)]
     along_y = [[x * SIDE + y for y in range(SIDE)] for x in range(SIDE)]
+    same_class = [
+        [r * SIDE * SIDE + x * SIDE + y for r in range(replicas) for y in range(SIDE)]
+        for x in range(SIDE)
+    ]
     quads = replicas // SIDE
     pub = public_tokens.shape[0]
     priv = private_tokens.shape[0]
@@ -162,24 +166,28 @@
         jnp.arange(L, dtype=jnp.int32)[None, :] < token_counts[0][:, None]
     ).reshape(priv)
     live_tokens = jnp.where(live[:, None], private_tokens, jnp.zeros_like(private_tokens))
-    local = jnp.concatenate([public_tokens.T, live_tokens.T], axis=1)
+    local = jnp.concatenate([live_tokens.T, public_tokens.T], axis=1)
+    def across_x(sent):
+        return lax.all_to_all(sent, "tile", 0, 0, tiled=True, axis_index_groups=along_x)
+
+    targets = jnp.concatenate([public_targets, private_targets], axis=0)
+    targets = targets.reshape(-1, replicas, cols).transpose(1, 0, 2)
     local = lax.ppermute(local, ("replica", "tile"), moves)
+    targets = lax.all_to_all(targets, "replica", 0, 0, tiled=True)
+    w_half = weight.astype(jnp.bfloat16)
+    local, targets, w_half = lax.optimization_barrier((local, targets, w_half))
+
     tokens = lax.all_gather(local, "replica", axis=0)
     tokens = tokens.reshape(quads, SIDE, rows, pub + priv)
 
-    w_half = weight.astype(jnp.bfloat16)
-    w_group = lax.all_to_all(
-        everywhere(w_half, SIDE), "tile", 0, 0, tiled=True, axis_index_groups=along_x
-    )
-
-    targets = jnp.concatenate([public_targets, private_targets], axis=0)
-    targets = lax.ppermute(targets, ("replica", "tile"), moves)
-    targets = targets.reshape(-1, replicas, cols).transpose(1, 0, 2)
-    targets = lax.all_to_all(targets, "replica", 0, 0, tiled=True)
+    targets = targets.reshape(quads, 2, CORES, -1, cols).transpose(2, 1, 0, 3, 4)
+    targets = across_x(targets.reshape(SIDE, -1, cols))
+    w_group = across_x(everywhere(w_half, SIDE))
+    targets = targets.reshape(SIDE, quads, pub_rows + priv_rows, cols).transpose(1, 0, 2, 3)
     targets = jnp.concatenate(
         [
-            targets[:, :pub_rows].reshape(pub_all, cols),
-            targets[:, pub_rows:].reshape(priv_all, cols),
+            targets[:, :, :pub_rows].reshape(pub_all, cols),
+            targets[:, :, pub_rows:].reshape(priv_all, cols),
         ],
         axis=0,
     )
@@ -196,7 +204,7 @@
         "qxfn,xfk->qnk", tokens, w_group, preferred_element_type=jnp.float32
     ).astype(jnp.bfloat16)
     sent = jnp.concatenate(
-        [by_owner(out[:, :pub], pub_rows), by_owner(out[:, pub:], priv_rows)], axis=1
+        [by_owner(out[:, priv:], pub_rows), by_owner(out[:, :priv], priv_rows)], axis=1
     )
     got, (targets, tokens) = exchange(sent, "tile", along_y, (targets, tokens))
     total = jnp.sum(got.astype(jnp.float32), axis=0)
@@ -214,7 +222,7 @@
     public_grad = over_classes(
         jnp.einsum(
             "qxfn,qnk->xfk",
-            tokens[:, :, :, :pub],
+            tokens[:, :, :, priv:],
             public_delta,
             preferred_element_type=jnp.float32,
         )
@@ -225,14 +233,13 @@
         everywhere(precond.astype(jnp.bfloat16), SIDE), "tile", along_x
     )
 
-    squares = example_squares(
-        tokens, private_delta, precond_group, pub
-    )
-    squares = jnp.sum(exchange(everywhere(squares, SIDE), "tile", along_y)[0], axis=0)
-    squares = jnp.sum(exchange(everywhere(squares, replicas), "replica", None)[0], axis=0)
+    squares = example_squares(tokens, private_delta, precond_group)
+    peers = replicas * SIDE
+    squares, _ = exchange(everywhere(squares, peers), ("replica", "tile"), same_class)
+    squares = jnp.sum(squares, axis=0)
     clip_norm = clip_factor * math.sqrt(L * D * Q)
     factors = clip_norm / jnp.maximum(jnp.sqrt(squares), clip_norm)
-    summed = precond * over_classes(clipped_sum(factors, tokens, private_delta, pub))
+    summed = precond * over_classes(clipped_sum(factors, tokens, private_delta))
 
     examples_total = examples_here * replicas
     noise_scale = noise_level * clip_factor * math.sqrt(L)

time: 219 us -> 215 us (0.982)
  blocking collectives: 89.7 us -> 102 us
  starting transfers between devices: 31 us -> 21.6 us
  waiting for transfers between devices: 50.2 us -> 47 us
  other arithmetic: 6.3 us -> 3.86 us
    all_gather x1, waiting for transfers between devices: 0.01 us -> 22.4 us  [on_device(): tokens = lax.all_gather(local, 'replica', axis=0)]
    all_to_all x0 -> x1, blocking collectives: none -> 17.3 us  [across_x(): lax.all_to_all(sent, 'tile', 0, 0, tiled=True, axis_index_groups=along_x)]
    all_to_all x1, waiting for transfers between devices: 16.3 us -> 2.89 us  [on_device(): targets = lax.all_to_all(targets, 'replica', 0, 0, tiled=True)]
    ppermute x1 -> x0, waiting for transfers between devices: 7.51 us -> none  [on_device(): targets = lax.ppermute(targets, ('replica', 'tile'), moves)]
    ppermute x1 -> x0, starting transfers between devices: 5.89 us -> none  [on_device(): targets = lax.ppermute(targets, ('replica', 'tile'), moves)]
    all_to_all x6 -> x5, blocking collectives: 89.7 us -> 84.6 us  [exchange(): got = lax.all_to_all(sent, axis, 0, 0, tiled=True, axis_index_groups=groups)]
    ppermute x1, waiting for transfers between devices: 9.2 us -> 5.16 us  [on_device(): local = lax.ppermute(local, ('replica', 'tile'), moves)]
  transfers between devices with their start and end apart: 6 -> 5, of which waited for: 5 -> 5; matrix products, arithmetic and copies ran while one was open for 2% -> 1% of each run, Pallas kernels for 0% -> 0%
where the time goes in v7:
time: 215 us; the launch traced here: 213 us
  blocking collectives  102 us (47%)
  waiting for transfers between devices  47 us (22%)
  starting transfers between devices  21.6 us (10%)
  between operations  14.3 us (7%)
  Pallas kernels  11.3 us (5%)
  matrix products  7.41 us (3%)
  local copies, waits for them, and re-layouts  5.93 us (3%)
  other arithmetic  3.86 us (2%)
    all_to_all x5, blocking collectives, exchange(): got = lax.all_to_all(sent, axis, 0, 0, tiled=True, axis_index_groups=groups)  84.6 us
    all_gather x1, waiting for transfers between devices, on_device(): tokens = lax.all_gather(local, 'replica', axis=0)  22.4 us
    all_to_all x1, blocking collectives, across_x(): lax.all_to_all(sent, 'tile', 0, 0, tiled=True, axis_index_groups=along_x)  17.3 us
    all_to_all x1, starting transfers between devices, on_device(): targets = lax.all_to_all(targets, 'replica', 0, 0, tiled=True)  9.97 us
    all_to_all x1, waiting for transfers between devices, across_x(): lax.all_to_all(sent, 'tile', 0, 0, tiled=True, axis_index_groups=along_x)  9.94 us
    all_to_all x1, waiting for transfers between devices, exchange(): got = lax.all_to_all(sent, axis, 0, 0, tiled=True, axis_index_groups=groups)  6.55 us
    pallas_call x1, Pallas kernels, example_squares(): pl.pallas_call(norms_kernel, grid=(quads,), in_specs=[pl.BlockSpec((1, si...  6.09 us
    pallas_call x1, Pallas kernels, clipped_sum(): pl.pallas_call(clipped_kernel, grid=(quads,), in_specs=[pl.BlockSpec(memo...  5.26 us
  transfers between devices with their start and end apart: 5, of which 5 were waited for; matrix products, arithmetic and copies ran while one was open for 1% of the time, Pallas kernels for 0%

profile of v7, /device:TPU:1, one launch (start us, length us, event | category | flops | bytes accessed | tf_op | source)
XLA Modules:
  0.0 213.4 jit_solution(10840776186491940900)
XLA Ops:
  7.2 1.1 pad_maximum_fusion.2
  8.4 0.8 copy.34
  9.2 10.0 %all-to-all-start = ((bf16[16,40,256]{2,1,0:T(8,128)(2,1)}), bf16[16,40,256]{2,1,0:T(8,128)(2,1)S(1)}, u32[]{:S(2)}, u32[]{:S(2)}) async-start(bf16[16,40,256]{2,1,0:T(8,128)(2,1)} %copy.34), calls=%async_computation | async-start | bytes 655360 | tf_op jit(solution)/shard_map/all_to_all | solution.py:176
  19.4 4.6 %collective-permute-start = (bf16[320,640]{1,0:T(8,128)(2,1)S(1)}, bf16[320,640]{1,0:T(8,128)(2,1)S(1)}, u32[]{:S(2)}, u32[]{:S(2)}) collective-permute-start(bf16[320,640]{1,0:T(8,128)(2,1)S(1)} %pad_maximum_fusion.1), channel_id=1, source_target_pairs={{0,0},{1,1},{2,2},{3,3},{4,16},{5,17},{6,18},{7,19},{8,32},{9,33},... | collective-permute-start | bytes 1228808 | tf_op jit(solution)/shard_map/ppermute | solution.py:175
  24.1 5.2 %collective-permute-done = bf16[320,640]{1,0:T(8,128)(2,1)S(1)} collective-permute-done((bf16[320,640]{1,0:T(8,128)(2,1)S(1)}, bf16[320,640]{1,0:T(8,128)(2,1)S(1)}, u32[]{:S(2)}, u32[]{:S(2)}) %collective-permute-start) | collective-permute-done | bytes 409632 | tf_op jit(solution)/shard_map/ppermute | solution.py:175
  29.2 2.9 %all-to-all-done = bf16[16,40,256]{2,1,0:T(8,128)(2,1)S(1)} async-done(((bf16[16,40,256]{2,1,0:T(8,128)(2,1)}), bf16[16,40,256]{2,1,0:T(8,128)(2,1)S(1)}, u32[]{:S(2)}, u32[]{:S(2)}) %all-to-all-start) | async-done | bytes 327712 | tf_op jit(solution)/shard_map/all_to_all | solution.py:176
  32.2 17.3 %all_to_all.45 = bf16[4,160,256]{2,1,0:T(8,128)(2,1)S(1)} all-to-all(bf16[4,160,256]{2,1,0:T(8,128)(2,1)S(1)} %bitcast.70), channel_id=1, replica_groups={{0,4,8,12},{1,5,9,13},{2,6,10,14},{3,7,11,15},{16,20,24,28},{17,21,25,2..., dimensions={0} | all-to-all | bytes 655360 | tf_op jit(solution)/shard_map/all_to_all | solution.py:171
  49.5 0.9 broadcast_in_dim.22
  50.4 3.5 %all-to-all-start.1 = ((bf16[4,320,256]{2,1,0:T(8,128)(2,1)}), bf16[4,320,256]{2,1,0:T(8,128)(2,1)S(1)}, u32[]{:S(2)}, u32[]{:S(2)}) async-start(bf16[4,320,256]{2,1,0:T(8,128)(2,1)} %broadcast_in_dim.22), calls=%async_computation.1 | async-start | bytes 1310720 | tf_op jit(solution)/shard_map/all_to_all | solution.py:171
  54.0 9.9 %all-to-all-done.1 = bf16[4,320,256]{2,1,0:T(8,128)(2,1)S(1)} async-done(((bf16[4,320,256]{2,1,0:T(8,128)(2,1)}), bf16[4,320,256]{2,1,0:T(8,128)(2,1)S(1)}, u32[]{:S(2)}, u32[]{:S(2)}) %all-to-all-start.1) | async-done | bytes 655392 | tf_op jit(solution)/shard_map/all_to_all | solution.py:171
  64.0 22.4 %all-gather.3.cloned.1.call-done = bf16[5120,640]{1,0:T(8,128)(2,1)} async-done(((bf16[320,640]{1,0:T(8,128)(2,1)}), bf16[5120,640]{1,0:T(8,128)(2,1)}) %all-gather.3.cloned.1.call-update) | async-done | bytes 6553616 | tf_op jit(solution)/shard_map/all_gather | solution.py:180
  86.4 4.8 %bitcast_convert_fusion = bf16[4,640,256]{2,1,0:T(8,128)(2,1)S(1)} fusion(bf16[4,4,320,640]{3,2,1,0:T(8,128)(2,1)} %bitcast.53, bf16[4,320,256]{2,1,0:T(8,128)(2,1)S(1)} %all-to-all-done.1), kind=kOutput, calls=%fused_computation | convolution fusion | flops 1678376960 | bytes 8519680 | tf_op jit(solution)/shard_map/qxfn,xfk->qnk/dot_general | solution.py:203
  91.4 0.1 pad_maximum_fusion
  91.5 21.2 %all_to_all.46 = bf16[4,640,256]{2,1,0:T(8,128)(2,1)S(1)} all-to-all(bf16[4,640,256]{2,1,0:T(8,128)(2,1)S(1)} %pad_maximum_fusion), channel_id=1, replica_groups={{0,1,2,3},{4,5,6,7},{8,9,10,11},{12,13,14,15},{16,17,18,19},{20,21,22,2..., dimensions={0} | all-to-all | bytes 2621440 | tf_op jit(solution)/shard_map/all_to_all | solution.py:29
  112.7 0.2 convert_reduce_fusion
  112.9 0.1 subtract_convert_fusion
  113.1 18.7 %all_to_all.47 = bf16[4,640,256]{2,1,0:T(8,128)(2,1)S(1)} all-to-all(bf16[4,640,256]{2,1,0:T(8,128)(2,1)S(1)} %broadcast_in_dim.40), channel_id=1, replica_groups={{0,1,2,3},{4,5,6,7},{8,9,10,11},{12,13,14,15},{16,17,18,19},{20,21,22,2..., dimensions={0} | all-to-all | bytes 2621440 | tf_op jit(solution)/shard_map/all_to_all | solution.py:29
  132.0 2.6 %fusion.5 = bf16[4,320,256]{2,1,0:T(8,128)(2,1)S(1)} fusion(bf16[4,256,256,1]{2,1,3,0:T(8,128)(2,1)S(1)} %bitcast.74, bf16[4,4,320,640]{3,2,1,0:T(8,128)(2,1)} %bitcast.54), kind=kOutput, calls=%fused_computation.5 | convolution fusion | flops 671416320 | bytes 3801088 | tf_op jit(solution)/shard_map/qxfn,qnk->xfk/dot_general | solution.py:223
  134.6 11.6 %all_to_all.48 = bf16[4,320,256]{2,1,0:T(8,128)(2,1)S(1)} all-to-all(bf16[4,320,256]{2,1,0:T(8,128)(2,1)S(1)} %fusion.5), channel_id=1, replica_groups={{0,4,8,12},{1,5,9,13},{2,6,10,14},{3,7,11,15},{16,20,24,28},{17,21,25,2..., dimensions={0} | all-to-all | bytes 1310720 | tf_op jit(solution)/shard_map/all_to_all | solution.py:29
  146.3 0.2 fusion.9
  146.5 0.9 broadcast_in_dim.41
  147.4 3.5 %all-to-all-start.6 = ((bf16[4,320,256]{2,1,0:T(8,128)(2,1)}), bf16[4,320,256]{2,1,0:T(8,128)(2,1)S(1)}, u32[]{:S(2)}, u32[]{:S(2)}) async-start(bf16[4,320,256]{2,1,0:T(8,128)(2,1)} %broadcast_in_dim.41), calls=%async_computation.6 | async-start | bytes 1310720 | tf_op jit(solution)/shard_map/all_to_all | solution.py:29
  151.0 1.0 copy.40
  152.0 6.6 %all-to-all-done.6.precond_ref = bf16[4,320,256]{2,1,0:T(8,128)(2,1)S(1)} async-done(((bf16[4,320,256]{2,1,0:T(8,128)(2,1)}), bf16[4,320,256]{2,1,0:T(8,128)(2,1)S(1)}, u32[]{:S(2)}, u32[]{:S(2)}) %all-to-all-start.6) | async-done | bytes 655392 | tf_op jit(solution)/shard_map/all_to_all | solution.py:29
  158.5 0.8 copy-done
  159.4 6.1 %example_squares.1 = f32[4,8,128]{2,1,0:T(8,128)} custom-call(bf16[4,4,320,640]{3,2,1,0:T(8,128)(2,1)} %bitcast.55, bf16[4,384,256]{2,1,0:T(8,128)(2,1)} %bitcast.57, bf16[4,320,256]{2,1,0:T(8,128)(2,1)} %copy-done), custom_call_target="tpu_custom_call" | custom-call | tf_op jit(solution)/shard_map/example_squares/pallas_call | solution.py:74
  165.5 0.8 slice_reduce_fusion
  166.3 20.4 %all_to_all.49 = f32[64,4,3]{2,1,0:T(4,128)S(1)} all-to-all(f32[64,4,3]{2,1,0:T(4,128)S(1)} %broadcast_in_dim.43), channel_id=1, replica_groups={{0,1,2,3,16,17,18,19,32,33,34,35,48,49,50,51,64,65,66,67,80,81,82,83,96..., dimensions={0} | all-to-all | bytes 6144 | tf_op jit(solution)/shard_map/all_to_all | solution.py:29
  186.8 0.6 maximum_divide_fusion.factors_ref
  187.4 5.3 %clipped_sum.1 = bf16[4,320,256]{2,1,0:T(8,128)(2,1)} custom-call(f32[4,3]{1,0:T(4,128)} %maximum_divide_fusion.factors_ref, bf16[4,4,320,640]{3,2,1,0:T(8,128)(2,1)} %bitcast.56, bf16[4,384,256]{2,1,0:T(8,128)(2,1)} %bitcast.58), custom_call_target="tpu_custom_call" | custom-call | tf_op jit(solution)/shard_map/clipped_sum/pallas_call | solution.py:120
  192.6 12.6 %all_to_all.50 = bf16[4,320,256]{2,1,0:T(8,128)(2,1)S(1)} all-to-all(bf16[4,320,256]{2,1,0:T(8,128)(2,1)} %clipped_sum.1), channel_id=1, replica_groups={{0,4,8,12},{1,5,9,13},{2,6,10,14},{3,7,11,15},{16,20,24,28},{17,21,25,2..., dimensions={0} | all-to-all | bytes 1310720 | tf_op jit(solution)/shard_map/all_to_all | solution.py:29
  205.3 1.2 divide_subtract_fusion
  (45 shorter events, 1.1 us)
Async XLA Ops:
  7.2 12.0 %copy-start.10 = (s32[1,3]{1,0:T(1,128)S(1)}, s32[1,3]{1,0:T(1,128)}, u32[]{:S(2)}) copy-start(s32[1,3]{1,0:T(1,128)} %param.14) | copy-start | bytes 40
  7.2 12.1 %copy-start.8 = (bf16[384,320]{0,1:T(8,128)(2,1)S(1)}, bf16[384,320]{0,1:T(8,128)(2,1)}, u32[]{:S(2)}) copy-start(bf16[384,320]{0,1:T(8,128)(2,1)} %param.12) | copy-start | bytes 737284
  7.2 12.1 %copy-start.9 = (bf16[256,320]{0,1:T(8,128)(2,1)S(1)}, bf16[256,320]{0,1:T(8,128)(2,1)}, u32[]{:S(2)}) copy-start(bf16[256,320]{0,1:T(8,128)(2,1)} %param.10) | copy-start | bytes 491524
  7.2 16.8 %copy-start.1 = (f32[320,256]{1,0:T(8,128)S(1)}, f32[320,256]{1,0:T(8,128)}, u32[]{:S(2)}) copy-start(f32[320,256]{1,0:T(8,128)} %param.15) | copy-start | bytes 983044
  9.2 22.9 %all-to-all-start = ((bf16[16,40,256]{2,1,0:T(8,128)(2,1)}), bf16[16,40,256]{2,1,0:T(8,128)(2,1)S(1)}, u32[]{:S(2)}, u32[]{:S(2)}) async-start(bf16[16,40,256]{2,1,0:T(8,128)(2,1)} %copy.34), calls=%async_computation | async-start | bytes 655360 | tf_op jit(solution)/shard_map/all_to_all | solution.py:176
  19.2 67.2 %all-gather.3.cloned.1.call-start = ((), (), s32[]{:S(2)}) async-start(), calls=%async_computation.9 | async-start | bytes 6963200 | tf_op jit(solution)/shard_map/all_gather | solution.py:180
  19.4 9.8 %collective-permute-start = (bf16[320,640]{1,0:T(8,128)(2,1)S(1)}, bf16[320,640]{1,0:T(8,128)(2,1)S(1)}, u32[]{:S(2)}, u32[]{:S(2)}) collective-permute-start(bf16[320,640]{1,0:T(8,128)(2,1)S(1)} %pad_maximum_fusion.1), channel_id=1, source_target_pairs={{0,0},{1,1},{2,2},{3,3},{4,16},{5,17},{6,18},{7,19},{8,32},{9,33},... | collective-permute-start | bytes 1228808 | tf_op jit(solution)/shard_map/ppermute | solution.py:175
  29.2 2.9 %copy-start.3 = (bf16[320,640]{1,0:T(8,128)(2,1)}, bf16[320,640]{1,0:T(8,128)(2,1)S(1)}, u32[]{:S(2)}) copy-start(bf16[320,640]{1,0:T(8,128)(2,1)S(1)} %collective-permute-done) | copy-start | bytes 1228804
  50.4 13.5 %all-to-all-start.1 = ((bf16[4,320,256]{2,1,0:T(8,128)(2,1)}), bf16[4,320,256]{2,1,0:T(8,128)(2,1)S(1)}, u32[]{:S(2)}, u32[]{:S(2)}) async-start(bf16[4,320,256]{2,1,0:T(8,128)(2,1)} %broadcast_in_dim.22), calls=%async_computation.1 | async-start | bytes 1310720 | tf_op jit(solution)/shard_map/all_to_all | solution.py:171
  131.9 14.4 %copy-start.4 = (f32[320,256]{1,0:T(8,128)S(1)}, f32[320,256]{1,0:T(8,128)}, u32[]{:S(2)}) copy-start(f32[320,256]{1,0:T(8,128)} %param.16) | copy-start | bytes 983044
  146.5 58.8 %copy-start.2 = (f32[320,256]{1,0:T(8,128)}, f32[320,256]{1,0:T(8,128)S(1)}, u32[]{:S(2)}) copy-start(f32[320,256]{1,0:T(8,128)S(1)} %get-tuple-element.38) | copy-start | bytes 983044
  147.4 11.1 %all-to-all-start.6 = ((bf16[4,320,256]{2,1,0:T(8,128)(2,1)}), bf16[4,320,256]{2,1,0:T(8,128)(2,1)S(1)}, u32[]{:S(2)}, u32[]{:S(2)}) async-start(bf16[4,320,256]{2,1,0:T(8,128)(2,1)} %broadcast_in_dim.41), calls=%async_computation.6 | async-start | bytes 1310720 | tf_op jit(solution)/shard_map/all_to_all | solution.py:29
  158.5 0.8 copy-start
  187.4 17.9 %copy-start.5 = (f32[320,256]{1,0:T(8,128)S(1)}, f32[320,256]{1,0:T(8,128)}, u32[]{:S(2)}) copy-start(f32[320,256]{1,0:T(8,128)} %param.19) | copy-start | bytes 983044
  187.4 17.9 %copy-start.6 = (f32[320,256]{1,0:T(8,128)S(1)}, f32[320,256]{1,0:T(8,128)}, u32[]{:S(2)}) copy-start(f32[320,256]{1,0:T(8,128)} %param.17) | copy-start | bytes 983044
  187.4 18.0 %copy-start.7 = (f32[320,256]{1,0:T(8,128)S(1)}, f32[320,256]{1,0:T(8,128)}, u32[]{:S(2)}) copy-start(f32[320,256]{1,0:T(8,128)} %param.18) | copy-start | bytes 983044
Sparse Core Ops, SparseCore 0:
  32.3 54.0 all-gather.2

commit v8 on v7

--- a/solution.py
+++ b/solution.py
@@ -12,6 +12,7 @@
 Q = 4096
 CORES = 2
 SIDE = 4
+KERNEL_VMEM = 58 * 2**20
 
 
 beta_first = 0.9
@@ -49,11 +50,12 @@
 
 def norms_kernel(tokens_ref, delta_ref, precond_ref, out_ref):
     sides, rows = tokens_ref.shape[1], tokens_ref.shape[2]
+    quad = pl.program_id(0)
     examples = delta_ref.shape[1] // L
     row_at = lax.broadcasted_iota(jnp.int32, out_ref.shape[1:], 0)
     found = jnp.zeros(out_ref.shape[1:], jnp.float32)
     for example in range(examples):
-        block_d = delta_ref[0, example * L : (example + 1) * L, :]
+        block_d = delta_ref[quad, example * L : (example + 1) * L, :]
         first = example * L
         acc = jnp.zeros((8, block_d.shape[1]), jnp.float32)
         for side in range(sides):
@@ -76,11 +78,12 @@
         grid=(quads,),
         in_specs=[
             pl.BlockSpec((1, sides, rows, priv), lambda q: (q, 0, 0, 0)),
-            pl.BlockSpec((1, priv, cols), lambda q: (q, 0, 0)),
-            pl.BlockSpec((sides, rows, cols), lambda q: (0, 0, 0)),
+            pl.BlockSpec(memory_space=pltpu.VMEM),
+            pl.BlockSpec(memory_space=pltpu.VMEM),
         ],
         out_specs=pl.BlockSpec((1, 8, L), lambda q: (q, 0, 0)),
         out_shape=jax.ShapeDtypeStruct((quads, 8, L), jnp.float32),
+        compiler_params=pltpu.CompilerParams(vmem_limit_bytes=KERNEL_VMEM),
         name="example_squares",
     )(tokens, deltas, precond)
     return out[:, : priv // L, 0]
@@ -93,7 +96,7 @@
         [
             (
                 factors_ref[quad, example]
-                * delta_ref[0, example * L : (example + 1) * L, :].astype(jnp.float32)
+                * delta_ref[quad, example * L : (example + 1) * L, :].astype(jnp.float32)
             ).astype(jnp.bfloat16)
             for example in range(examples)
         ],
@@ -123,11 +126,12 @@
         in_specs=[
             pl.BlockSpec(memory_space=pltpu.SMEM),
             pl.BlockSpec((1, sides, rows, priv), lambda q: (q, 0, 0, 0)),
-            pl.BlockSpec((1, priv, cols), lambda q: (q, 0, 0)),
+            pl.BlockSpec(memory_space=pltpu.VMEM),
         ],
         out_specs=pl.BlockSpec((sides, rows, cols), lambda q: (0, 0, 0)),
         out_shape=jax.ShapeDtypeStruct((sides, rows, cols), jnp.bfloat16),
         scratch_shapes=[pltpu.VMEM((sides, rows, cols), jnp.float32)],
+        compiler_params=pltpu.CompilerParams(vmem_limit_bytes=KERNEL_VMEM),
         name="clipped_sum",
     )(factors, tokens, deltas)
 
@@ -175,7 +179,6 @@
     local = lax.ppermute(local, ("replica", "tile"), moves)
     targets = lax.all_to_all(targets, "replica", 0, 0, tiled=True)
     w_half = weight.astype(jnp.bfloat16)
-    local, targets, w_half = lax.optimization_barrier((local, targets, w_half))
 
     tokens = lax.all_gather(local, "replica", axis=0)
     tokens = tokens.reshape(quads, SIDE, rows, pub + priv)

time: 215 us -> 210 us (0.977)
  waiting for transfers between devices: 47 us -> 35.9 us
  blocking collectives: 102 us -> 110 us
  starting transfers between devices: 21.6 us -> 16.6 us
  other arithmetic: 3.86 us -> 6.35 us
    all_gather x1, waiting for transfers between devices: 22.4 us -> 1.89 us  [on_device(): tokens = lax.all_gather(local, 'replica', axis=0)]
    all_to_all x1 -> x0, starting transfers between devices: 9.97 us -> none  [on_device(): targets = lax.all_to_all(targets, 'replica', 0, 0, tiled=True)]
    all_to_all x1 -> x2, waiting for transfers between devices: 9.94 us -> 18.2 us  [across_x(): lax.all_to_all(sent, 'tile', 0, 0, tiled=True, axis_index_groups=along_x)]
    all_to_all x1, blocking collectives: 17.3 us -> 24.8 us  [on_device(): targets = lax.all_to_all(targets, 'replica', 0, 0, tiled=True)]
    ppermute x1, waiting for transfers between devices: 5.16 us -> 9.2 us  [on_device(): local = lax.ppermute(local, ('replica', 'tile'), moves)]
    all_to_all x1 -> x2, starting transfers between devices: 3.48 us -> 7.08 us  [across_x(): lax.all_to_all(sent, 'tile', 0, 0, tiled=True, axis_index_groups=along_x)]
    all_to_all x1 -> x0, waiting for transfers between devices: 2.89 us -> none  [on_device(): targets = lax.all_to_all(targets, 'replica', 0, 0, tiled=True)]
  transfers between devices with their start and end apart: 5 -> 5, of which waited for: 5 -> 5; matrix products, arithmetic and copies ran while one was open for 1% -> 2% of each run, Pallas kernels for 0% -> 0%
where the time goes in v8:
time: 210 us; the launch traced here: 208 us
  blocking collectives  110 us (52%)
  waiting for transfers between devices  35.9 us (17%)
  starting transfers between devices  16.6 us (8%)
  between operations  14.3 us (7%)
  Pallas kernels  11.4 us (5%)
  matrix products  7.41 us (4%)
  local copies, waits for them, and re-layouts  6.66 us (3%)
  other arithmetic  6.35 us (3%)
    all_to_all x5, blocking collectives, exchange(): got = lax.all_to_all(sent, axis, 0, 0, tiled=True, axis_index_groups=groups)  84.7 us
    all_to_all x1, blocking collectives, on_device(): targets = lax.all_to_all(targets, 'replica', 0, 0, tiled=True)  24.8 us
    all_to_all x2, waiting for transfers between devices, across_x(): lax.all_to_all(sent, 'tile', 0, 0, tiled=True, axis_index_groups=along_x)  18.2 us
    ppermute x1, waiting for transfers between devices, on_device(): local = lax.ppermute(local, ('replica', 'tile'), moves)  9.2 us
    all_to_all x2, starting transfers between devices, across_x(): lax.all_to_all(sent, 'tile', 0, 0, tiled=True, axis_index_groups=along_x)  7.08 us
    all_to_all x1, waiting for transfers between devices, exchange(): got = lax.all_to_all(sent, axis, 0, 0, tiled=True, axis_index_groups=groups)  6.54 us
    ppermute x1, starting transfers between devices, on_device(): local = lax.ppermute(local, ('replica', 'tile'), moves)  6.03 us
    pallas_call x1, Pallas kernels, example_squares(): pl.pallas_call(norms_kernel, grid=(quads,), in_specs=[pl.BlockSpec((1, si...  5.94 us
  transfers between devices with their start and end apart: 5, of which 5 were waited for; matrix products, arithmetic and copies ran while one was open for 2% of the time, Pallas kernels for 0%

profile of v8, /device:TPU:1, one launch (start us, length us, event | category | flops | bytes accessed | tf_op | source)
XLA Modules:
  0.0 208.1 jit_solution(8719799656741949412)
XLA Ops:
  7.2 0.7 fusion.10
  7.9 1.0 select_bitcast_fusion
  8.9 1.0 pad_maximum_fusion.1
  9.9 6.0 %collective-permute-start = (bf16[320,640]{1,0:T(8,128)(2,1)S(1)}, bf16[320,640]{1,0:T(8,128)(2,1)S(1)}, u32[]{:S(2)}, u32[]{:S(2)}) collective-permute-start(bf16[320,640]{1,0:T(8,128)(2,1)S(1)} %pad_maximum_fusion.1), channel_id=1, source_target_pairs={{0,0},{1,1},{2,2},{3,3},{4,16},{5,17},{6,18},{7,19},{8,32},{9,33},... | collective-permute-start | bytes 1228808 | tf_op jit(solution)/shard_map/ppermute | solution.py:179
  16.0 9.2 %collective-permute-done = bf16[320,640]{1,0:T(8,128)(2,1)S(1)} collective-permute-done((bf16[320,640]{1,0:T(8,128)(2,1)S(1)}, bf16[320,640]{1,0:T(8,128)(2,1)S(1)}, u32[]{:S(2)}, u32[]{:S(2)}) %collective-permute-start) | collective-permute-done | bytes 409632 | tf_op jit(solution)/shard_map/ppermute | solution.py:179
  25.2 0.8 copy-done.3
  26.0 1.0 pad_maximum_fusion.2
  27.2 24.8 %all_to_all.45 = bf16[16,40,256]{2,1,0:T(8,128)(2,1)S(1)} all-to-all(bf16[16,40,256]{2,1,0:T(8,128)(2,1)S(1)} %copy.36), channel_id=1, replica_groups=mesh['replica'=16,'tile'=16] {'replica'}, dimensions={0} | all-to-all | bytes 655360 | tf_op jit(solution)/shard_map/all_to_all | solution.py:180
  52.0 0.7 copy.37
  52.8 3.6 %all-to-all-start.2 = ((bf16[4,160,256]{2,1,0:T(8,128)(2,1)}), bf16[4,160,256]{2,1,0:T(8,128)(2,1)S(1)}, u32[]{:S(2)}, u32[]{:S(2)}) async-start(bf16[4,160,256]{2,1,0:T(8,128)(2,1)} %bitcast.17), calls=%async_computation.2 | async-start | bytes 655360 | tf_op jit(solution)/shard_map/all_to_all | solution.py:175
  56.4 7.8 %all-to-all-done.2 = bf16[4,160,256]{2,1,0:T(8,128)(2,1)S(1)} async-done(((bf16[4,160,256]{2,1,0:T(8,128)(2,1)}), bf16[4,160,256]{2,1,0:T(8,128)(2,1)S(1)}, u32[]{:S(2)}, u32[]{:S(2)}) %all-to-all-start.2) | async-done | bytes 327712 | tf_op jit(solution)/shard_map/all_to_all | solution.py:175
  64.2 0.9 broadcast_in_dim.22
  65.1 3.5 %all-to-all-start = ((bf16[4,320,256]{2,1,0:T(8,128)(2,1)}), bf16[4,320,256]{2,1,0:T(8,128)(2,1)S(1)}, u32[]{:S(2)}, u32[]{:S(2)}) async-start(bf16[4,320,256]{2,1,0:T(8,128)(2,1)} %broadcast_in_dim.22), calls=%async_computation | async-start | bytes 1310720 | tf_op jit(solution)/shard_map/all_to_all | solution.py:175
  68.7 10.4 %all-to-all-done = bf16[4,320,256]{2,1,0:T(8,128)(2,1)S(1)} async-done(((bf16[4,320,256]{2,1,0:T(8,128)(2,1)}), bf16[4,320,256]{2,1,0:T(8,128)(2,1)S(1)}, u32[]{:S(2)}, u32[]{:S(2)}) %all-to-all-start) | async-done | bytes 655392 | tf_op jit(solution)/shard_map/all_to_all | solution.py:175
  79.1 1.9 all-gather.3.cloned.1.call-done
  81.0 4.8 %bitcast_convert_fusion = bf16[4,640,256]{2,1,0:T(8,128)(2,1)S(1)} fusion(bf16[4,4,320,640]{3,2,1,0:T(8,128)(2,1)} %bitcast.53, bf16[4,320,256]{2,1,0:T(8,128)(2,1)S(1)} %all-to-all-done), kind=kOutput, calls=%fused_computation | convolution fusion | flops 1678376960 | bytes 8519680 | tf_op jit(solution)/shard_map/qxfn,xfk->qnk/dot_general | solution.py:206
  86.1 21.4 %all_to_all.46 = bf16[4,640,256]{2,1,0:T(8,128)(2,1)S(1)} all-to-all(bf16[4,640,256]{2,1,0:T(8,128)(2,1)S(1)} %pad_maximum_fusion), channel_id=1, replica_groups={{0,1,2,3},{4,5,6,7},{8,9,10,11},{12,13,14,15},{16,17,18,19},{20,21,22,2..., dimensions={0} | all-to-all | bytes 2621440 | tf_op jit(solution)/shard_map/all_to_all | solution.py:30
  107.9 18.7 %all_to_all.47 = bf16[4,640,256]{2,1,0:T(8,128)(2,1)S(1)} all-to-all(bf16[4,640,256]{2,1,0:T(8,128)(2,1)S(1)} %broadcast_in_dim.40), channel_id=1, replica_groups={{0,1,2,3},{4,5,6,7},{8,9,10,11},{12,13,14,15},{16,17,18,19},{20,21,22,2..., dimensions={0} | all-to-all | bytes 2621440 | tf_op jit(solution)/shard_map/all_to_all | solution.py:30
  126.8 2.6 %fusion.5 = bf16[4,320,256]{2,1,0:T(8,128)(2,1)S(1)} fusion(bf16[4,256,256,1]{2,1,3,0:T(8,128)(2,1)S(1)} %bitcast.73, bf16[4,4,320,640]{3,2,1,0:T(8,128)(2,1)} %bitcast.54), kind=kOutput, calls=%fused_computation.5 | convolution fusion | flops 671416320 | bytes 3801088 | tf_op jit(solution)/shard_map/qxfn,qnk->xfk/dot_general | solution.py:226
  129.4 11.3 %all_to_all.48 = bf16[4,320,256]{2,1,0:T(8,128)(2,1)S(1)} all-to-all(bf16[4,320,256]{2,1,0:T(8,128)(2,1)S(1)} %fusion.5), channel_id=1, replica_groups={{0,4,8,12},{1,5,9,13},{2,6,10,14},{3,7,11,15},{16,20,24,28},{17,21,25,2..., dimensions={0} | all-to-all | bytes 1310720 | tf_op jit(solution)/shard_map/all_to_all | solution.py:30
  141.0 0.9 broadcast_in_dim.41
  141.9 3.5 %all-to-all-start.6 = ((bf16[4,320,256]{2,1,0:T(8,128)(2,1)}), bf16[4,320,256]{2,1,0:T(8,128)(2,1)S(1)}, u32[]{:S(2)}, u32[]{:S(2)}) async-start(bf16[4,320,256]{2,1,0:T(8,128)(2,1)} %broadcast_in_dim.41), calls=%async_computation.6 | async-start | bytes 1310720 | tf_op jit(solution)/shard_map/all_to_all | solution.py:30
  145.4 1.0 copy.40
  146.4 6.5 %all-to-all-done.6.precond_ref = bf16[4,320,256]{2,1,0:T(8,128)(2,1)S(1)} async-done(((bf16[4,320,256]{2,1,0:T(8,128)(2,1)}), bf16[4,320,256]{2,1,0:T(8,128)(2,1)S(1)}, u32[]{:S(2)}, u32[]{:S(2)}) %all-to-all-start.6) | async-done | bytes 655392 | tf_op jit(solution)/shard_map/all_to_all | solution.py:30
  153.0 0.8 copy-done
  153.8 5.9 %example_squares.1 = f32[4,8,128]{2,1,0:T(8,128)} custom-call(bf16[4,4,320,640]{3,2,1,0:T(8,128)(2,1)} %bitcast.55, bf16[4,384,256]{2,1,0:T(8,128)(2,1)} %bitcast.57, bf16[4,320,256]{2,1,0:T(8,128)(2,1)} %copy-done), custom_call_target="tpu_custom_call" | custom-call | tf_op jit(solution)/shard_map/example_squares/pallas_call | solution.py:76
  159.7 0.8 slice_reduce_fusion
  160.6 20.7 %all_to_all.49 = f32[64,4,3]{2,1,0:T(4,128)S(1)} all-to-all(f32[64,4,3]{2,1,0:T(4,128)S(1)} %broadcast_in_dim.43), channel_id=1, replica_groups={{0,1,2,3,16,17,18,19,32,33,34,35,48,49,50,51,64,65,66,67,80,81,82,83,96..., dimensions={0} | all-to-all | bytes 6144 | tf_op jit(solution)/shard_map/all_to_all | solution.py:30
  181.3 0.6 maximum_divide_fusion.factors_ref
  181.9 5.4 %clipped_sum.1 = bf16[4,320,256]{2,1,0:T(8,128)(2,1)} custom-call(f32[4,3]{1,0:T(4,128)} %maximum_divide_fusion.factors_ref, bf16[4,4,320,640]{3,2,1,0:T(8,128)(2,1)} %bitcast.56, bf16[4,384,256]{2,1,0:T(8,128)(2,1)} %bitcast.58), custom_call_target="tpu_custom_call" | custom-call | tf_op jit(solution)/shard_map/clipped_sum/pallas_call | solution.py:123
  187.4 12.6 %all_to_all.50 = bf16[4,320,256]{2,1,0:T(8,128)(2,1)S(1)} all-to-all(bf16[4,320,256]{2,1,0:T(8,128)(2,1)} %clipped_sum.1), channel_id=1, replica_groups={{0,4,8,12},{1,5,9,13},{2,6,10,14},{3,7,11,15},{16,20,24,28},{17,21,25,2..., dimensions={0} | all-to-all | bytes 1310720 | tf_op jit(solution)/shard_map/all_to_all | solution.py:30
  200.1 1.2 divide_subtract_fusion
  (39 shorter events, 1.6 us)
Async XLA Ops:
  7.2 73.8 %all-gather.3.cloned.1.call-start = ((), (), s32[]{:S(2)}) async-start(), calls=%async_computation.9 | async-start | bytes 6963200 | tf_op jit(solution)/shard_map/all_gather | solution.py:183
  8.9 47.4 %copy-start.1 = (f32[320,256]{1,0:T(8,128)S(1)}, f32[320,256]{1,0:T(8,128)}, u32[]{:S(2)}) copy-start(f32[320,256]{1,0:T(8,128)} %param.15) | copy-start | bytes 983044
  9.9 15.2 %collective-permute-start = (bf16[320,640]{1,0:T(8,128)(2,1)S(1)}, bf16[320,640]{1,0:T(8,128)(2,1)S(1)}, u32[]{:S(2)}, u32[]{:S(2)}) collective-permute-start(bf16[320,640]{1,0:T(8,128)(2,1)S(1)} %pad_maximum_fusion.1), channel_id=1, source_target_pairs={{0,0},{1,1},{2,2},{3,3},{4,16},{5,17},{6,18},{7,19},{8,32},{9,33},... | collective-permute-start | bytes 1228808 | tf_op jit(solution)/shard_map/ppermute | solution.py:179
  25.2 0.8 copy-start.3
  52.8 11.4 %all-to-all-start.2 = ((bf16[4,160,256]{2,1,0:T(8,128)(2,1)}), bf16[4,160,256]{2,1,0:T(8,128)(2,1)S(1)}, u32[]{:S(2)}, u32[]{:S(2)}) async-start(bf16[4,160,256]{2,1,0:T(8,128)(2,1)} %bitcast.17), calls=%async_computation.2 | async-start | bytes 655360 | tf_op jit(solution)/shard_map/all_to_all | solution.py:175
  65.1 14.0 %all-to-all-start = ((bf16[4,320,256]{2,1,0:T(8,128)(2,1)}), bf16[4,320,256]{2,1,0:T(8,128)(2,1)S(1)}, u32[]{:S(2)}, u32[]{:S(2)}) async-start(bf16[4,320,256]{2,1,0:T(8,128)(2,1)} %broadcast_in_dim.22), calls=%async_computation | async-start | bytes 1310720 | tf_op jit(solution)/shard_map/all_to_all | solution.py:175
  126.8 14.0 %copy-start.4 = (f32[320,256]{1,0:T(8,128)S(1)}, f32[320,256]{1,0:T(8,128)}, u32[]{:S(2)}) copy-start(f32[320,256]{1,0:T(8,128)} %param.16) | copy-start | bytes 983044
  140.9 59.1 %copy-start.2 = (f32[320,256]{1,0:T(8,128)}, f32[320,256]{1,0:T(8,128)S(1)}, u32[]{:S(2)}) copy-start(f32[320,256]{1,0:T(8,128)S(1)} %get-tuple-element.32) | copy-start | bytes 983044
  141.9 11.1 %all-to-all-start.6 = ((bf16[4,320,256]{2,1,0:T(8,128)(2,1)}), bf16[4,320,256]{2,1,0:T(8,128)(2,1)S(1)}, u32[]{:S(2)}, u32[]{:S(2)}) async-start(bf16[4,320,256]{2,1,0:T(8,128)(2,1)} %broadcast_in_dim.41), calls=%async_computation.6 | async-start | bytes 1310720 | tf_op jit(solution)/shard_map/all_to_all | solution.py:30
  153.0 0.8 copy-start
  181.9 18.1 %copy-start.5 = (f32[320,256]{1,0:T(8,128)S(1)}, f32[320,256]{1,0:T(8,128)}, u32[]{:S(2)}) copy-start(f32[320,256]{1,0:T(8,128)} %param.19) | copy-start | bytes 983044
  181.9 18.1 %copy-start.6 = (f32[320,256]{1,0:T(8,128)S(1)}, f32[320,256]{1,0:T(8,128)}, u32[]{:S(2)}) copy-start(f32[320,256]{1,0:T(8,128)} %param.17) | copy-start | bytes 983044
  181.9 18.1 %copy-start.7 = (f32[320,256]{1,0:T(8,128)S(1)}, f32[320,256]{1,0:T(8,128)}, u32[]{:S(2)}) copy-start(f32[320,256]{1,0:T(8,128)} %param.18) | copy-start | bytes 983044
Sparse Core Ops, SparseCore 0:
  26.1 54.8 all-gather.2

commit v9 on v8

--- a/solution.py
+++ b/solution.py
@@ -48,9 +48,41 @@
     return moves
 
 
-def norms_kernel(tokens_ref, delta_ref, precond_ref, out_ref):
+def live_kernel(counts_ref, private_ref, public_ref, out_ref):
+    rows, priv = private_ref.shape
+    slot = lax.broadcasted_iota(jnp.int32, (rows, L), 1)
+    for example in range(priv // L):
+        lanes = slice(example * L, (example + 1) * L)
+        block = private_ref[:, lanes].astype(jnp.float32)
+        block = jnp.where(slot < counts_ref[0, example], block, 0.0)
+        out_ref[:, lanes] = block.astype(out_ref.dtype)
+    out_ref[:, priv:] = public_ref[...]
+
+
+def live_block(counts, private, public):
+    return pl.pallas_call(
+        live_kernel,
+        in_specs=[
+            pl.BlockSpec(memory_space=pltpu.SMEM),
+            pl.BlockSpec(memory_space=pltpu.VMEM),
+            pl.BlockSpec(memory_space=pltpu.VMEM),
+        ],
+        out_specs=pl.BlockSpec(memory_space=pltpu.VMEM),
+        out_shape=jax.ShapeDtypeStruct(
+            (private.shape[0], private.shape[1] + public.shape[1]), private.dtype
+        ),
+        name="live_block",
+    )(counts, private, public)
+
+
+def norms_kernel(tokens_ref, delta_ref, precond_ref, out_ref, wide_ref):
     sides, rows = tokens_ref.shape[1], tokens_ref.shape[2]
     quad = pl.program_id(0)
+
+    @pl.when(quad == 0)
+    def _():
+        wide_ref[...] = precond_ref[...].astype(jnp.float32)
+
     examples = delta_ref.shape[1] // L
     row_at = lax.broadcasted_iota(jnp.int32, out_ref.shape[1:], 0)
     found = jnp.zeros(out_ref.shape[1:], jnp.float32)
@@ -64,7 +96,7 @@
                 block_d,
                 preferred_element_type=jnp.float32,
             )
-            scaled = grads * precond_ref[side].astype(jnp.float32)
+            scaled = grads * wide_ref[side]
             acc = acc + jnp.sum((scaled * scaled).reshape(rows // 8, 8, -1), axis=0)
         found = jnp.where(row_at == example, jnp.sum(acc), found)
     out_ref[0] = found
@@ -83,6 +115,7 @@
         ],
         out_specs=pl.BlockSpec((1, 8, L), lambda q: (q, 0, 0)),
         out_shape=jax.ShapeDtypeStruct((quads, 8, L), jnp.float32),
+        scratch_shapes=[pltpu.VMEM(precond.shape, jnp.float32)],
         compiler_params=pltpu.CompilerParams(vmem_limit_bytes=KERNEL_VMEM),
         name="example_squares",
     )(tokens, deltas, precond)
@@ -166,11 +199,7 @@
     priv_all = quads * SIDE * priv_rows
     moves = to_class(replicas)
 
-    live = (
-        jnp.arange(L, dtype=jnp.int32)[None, :] < token_counts[0][:, None]
-    ).reshape(priv)
-    live_tokens = jnp.where(live[:, None], private_tokens, jnp.zeros_like(private_tokens))
-    local = jnp.concatenate([live_tokens.T, public_tokens.T], axis=1)
+    local = live_block(token_counts, private_tokens.T, public_tokens.T)
     def across_x(sent):
         return lax.all_to_all(sent, "tile", 0, 0, tiled=True, axis_index_groups=along_x)
 

time: 210 us -> 209 us (level)
  other arithmetic: 6.35 us -> 3.65 us
where the time goes in v9:
time: 209 us; the launch traced here: 208 us
  blocking collectives  109 us (52%)
  waiting for transfers between devices  36.2 us (17%)
  starting transfers between devices  16.6 us (8%)
  between operations  14.3 us (7%)
  Pallas kernels  13.3 us (6%)
  matrix products  7.41 us (4%)
  local copies, waits for them, and re-layouts  6.66 us (3%)
  other arithmetic  3.65 us (2%)
    all_to_all x5, blocking collectives, exchange(): got = lax.all_to_all(sent, axis, 0, 0, tiled=True, axis_index_groups=groups)  84.7 us
    all_to_all x1, blocking collectives, on_device(): targets = lax.all_to_all(targets, 'replica', 0, 0, tiled=True)  24.7 us
    all_to_all x2, waiting for transfers between devices, across_x(): lax.all_to_all(sent, 'tile', 0, 0, tiled=True, axis_index_groups=along_x)  18.2 us
    ppermute x1, waiting for transfers between devices, on_device(): local = lax.ppermute(local, ('replica', 'tile'), moves)  9.52 us
    all_to_all x2, starting transfers between devices, across_x(): lax.all_to_all(sent, 'tile', 0, 0, tiled=True, axis_index_groups=along_x)  7.08 us
    all_to_all x1, waiting for transfers between devices, exchange(): got = lax.all_to_all(sent, axis, 0, 0, tiled=True, axis_index_groups=groups)  6.54 us
    ppermute x1, starting transfers between devices, on_device(): local = lax.ppermute(local, ('replica', 'tile'), moves)  6.02 us
    pallas_call x1, Pallas kernels, example_squares(): pl.pallas_call(norms_kernel, grid=(quads,), in_specs=[pl.BlockSpec((1, si...  6.01 us
  transfers between devices with their start and end apart: 5, of which 5 were waited for; matrix products, arithmetic and copies ran while one was open for 2% of the time, Pallas kernels for 0%

profile of v9, /device:TPU:1, one launch (start us, length us, event | category | flops | bytes accessed | tf_op | source)
XLA Modules:
  0.0 207.5 jit_solution(13306553225247859372)
XLA Ops:
  7.2 1.9 live_block.1
  9.1 6.0 %collective-permute-start = (bf16[320,640]{1,0:T(8,128)(2,1)}, bf16[320,640]{1,0:T(8,128)(2,1)S(1)}, u32[]{:S(2)}, u32[]{:S(2)}) collective-permute-start(bf16[320,640]{1,0:T(8,128)(2,1)} %live_block.1), channel_id=1, source_target_pairs={{0,0},{1,1},{2,2},{3,3},{4,16},{5,17},{6,18},{7,19},{8,32},{9,33},... | collective-permute-start | bytes 1228808 | tf_op jit(solution)/shard_map/ppermute | solution.py:208
  15.1 9.5 %collective-permute-done = bf16[320,640]{1,0:T(8,128)(2,1)S(1)} collective-permute-done((bf16[320,640]{1,0:T(8,128)(2,1)}, bf16[320,640]{1,0:T(8,128)(2,1)S(1)}, u32[]{:S(2)}, u32[]{:S(2)}) %collective-permute-start) | collective-permute-done | bytes 409632 | tf_op jit(solution)/shard_map/ppermute | solution.py:208
  24.7 0.8 copy-done.3
  25.4 1.0 pad_maximum_fusion.1
  26.7 24.7 %all_to_all.45 = bf16[16,40,256]{2,1,0:T(8,128)(2,1)S(1)} all-to-all(bf16[16,40,256]{2,1,0:T(8,128)(2,1)S(1)} %copy.36), channel_id=1, replica_groups=mesh['replica'=16,'tile'=16] {'replica'}, dimensions={0} | all-to-all | bytes 655360 | tf_op jit(solution)/shard_map/all_to_all | solution.py:209
  51.4 0.7 copy.37
  52.1 3.6 %all-to-all-start.2 = ((bf16[4,160,256]{2,1,0:T(8,128)(2,1)}), bf16[4,160,256]{2,1,0:T(8,128)(2,1)S(1)}, u32[]{:S(2)}, u32[]{:S(2)}) async-start(bf16[4,160,256]{2,1,0:T(8,128)(2,1)} %bitcast.15), calls=%async_computation.2 | async-start | bytes 655360 | tf_op jit(solution)/shard_map/all_to_all | solution.py:204
  55.8 7.8 %all-to-all-done.2 = bf16[4,160,256]{2,1,0:T(8,128)(2,1)S(1)} async-done(((bf16[4,160,256]{2,1,0:T(8,128)(2,1)}), bf16[4,160,256]{2,1,0:T(8,128)(2,1)S(1)}, u32[]{:S(2)}, u32[]{:S(2)}) %all-to-all-start.2) | async-done | bytes 327712 | tf_op jit(solution)/shard_map/all_to_all | solution.py:204
  63.5 0.9 broadcast_in_dim.10
  64.4 3.5 %all-to-all-start = ((bf16[4,320,256]{2,1,0:T(8,128)(2,1)}), bf16[4,320,256]{2,1,0:T(8,128)(2,1)S(1)}, u32[]{:S(2)}, u32[]{:S(2)}) async-start(bf16[4,320,256]{2,1,0:T(8,128)(2,1)} %broadcast_in_dim.10), calls=%async_computation | async-start | bytes 1310720 | tf_op jit(solution)/shard_map/all_to_all | solution.py:204
  68.0 10.4 %all-to-all-done = bf16[4,320,256]{2,1,0:T(8,128)(2,1)S(1)} async-done(((bf16[4,320,256]{2,1,0:T(8,128)(2,1)}), bf16[4,320,256]{2,1,0:T(8,128)(2,1)S(1)}, u32[]{:S(2)}, u32[]{:S(2)}) %all-to-all-start) | async-done | bytes 655392 | tf_op jit(solution)/shard_map/all_to_all | solution.py:204
  78.5 1.9 all-gather.3.cloned.1.call-done
  80.4 4.8 %bitcast_convert_fusion = bf16[4,640,256]{2,1,0:T(8,128)(2,1)S(1)} fusion(bf16[4,4,320,640]{3,2,1,0:T(8,128)(2,1)} %bitcast.49, bf16[4,320,256]{2,1,0:T(8,128)(2,1)S(1)} %all-to-all-done), kind=kOutput, calls=%fused_computation | convolution fusion | flops 1678376960 | bytes 8519680 | tf_op jit(solution)/shard_map/qxfn,xfk->qnk/dot_general | solution.py:235
  85.5 21.4 %all_to_all.46 = bf16[4,640,256]{2,1,0:T(8,128)(2,1)S(1)} all-to-all(bf16[4,640,256]{2,1,0:T(8,128)(2,1)S(1)} %pad_maximum_fusion), channel_id=1, replica_groups={{0,1,2,3},{4,5,6,7},{8,9,10,11},{12,13,14,15},{16,17,18,19},{20,21,22,2..., dimensions={0} | all-to-all | bytes 2621440 | tf_op jit(solution)/shard_map/all_to_all | solution.py:30
  106.9 0.2 convert_reduce_fusion
  107.3 18.7 %all_to_all.47 = bf16[4,640,256]{2,1,0:T(8,128)(2,1)S(1)} all-to-all(bf16[4,640,256]{2,1,0:T(8,128)(2,1)S(1)} %broadcast_in_dim.11), channel_id=1, replica_groups={{0,1,2,3},{4,5,6,7},{8,9,10,11},{12,13,14,15},{16,17,18,19},{20,21,22,2..., dimensions={0} | all-to-all | bytes 2621440 | tf_op jit(solution)/shard_map/all_to_all | solution.py:30
  126.2 2.6 %fusion.5 = bf16[4,320,256]{2,1,0:T(8,128)(2,1)S(1)} fusion(bf16[4,256,256,1]{2,1,3,0:T(8,128)(2,1)S(1)} %bitcast.69, bf16[4,4,320,640]{3,2,1,0:T(8,128)(2,1)} %bitcast.50), kind=kOutput, calls=%fused_computation.5 | convolution fusion | flops 671416320 | bytes 3801088 | tf_op jit(solution)/shard_map/qxfn,qnk->xfk/dot_general | solution.py:255
  128.8 11.3 %all_to_all.48 = bf16[4,320,256]{2,1,0:T(8,128)(2,1)S(1)} all-to-all(bf16[4,320,256]{2,1,0:T(8,128)(2,1)S(1)} %fusion.5), channel_id=1, replica_groups={{0,4,8,12},{1,5,9,13},{2,6,10,14},{3,7,11,15},{16,20,24,28},{17,21,25,2..., dimensions={0} | all-to-all | bytes 1310720 | tf_op jit(solution)/shard_map/all_to_all | solution.py:30
  140.1 0.2 fusion.9
  140.3 0.9 broadcast_in_dim.12
  141.3 3.5 %all-to-all-start.6 = ((bf16[4,320,256]{2,1,0:T(8,128)(2,1)}), bf16[4,320,256]{2,1,0:T(8,128)(2,1)S(1)}, u32[]{:S(2)}, u32[]{:S(2)}) async-start(bf16[4,320,256]{2,1,0:T(8,128)(2,1)} %broadcast_in_dim.12), calls=%async_computation.6 | async-start | bytes 1310720 | tf_op jit(solution)/shard_map/all_to_all | solution.py:30
  144.8 1.0 copy.40
  145.8 6.5 %all-to-all-done.6.precond_ref = bf16[4,320,256]{2,1,0:T(8,128)(2,1)S(1)} async-done(((bf16[4,320,256]{2,1,0:T(8,128)(2,1)}), bf16[4,320,256]{2,1,0:T(8,128)(2,1)S(1)}, u32[]{:S(2)}, u32[]{:S(2)}) %all-to-all-start.6) | async-done | bytes 655392 | tf_op jit(solution)/shard_map/all_to_all | solution.py:30
  152.3 0.8 copy-done
  153.2 6.0 %example_squares.1 = f32[4,8,128]{2,1,0:T(8,128)} custom-call(bf16[4,4,320,640]{3,2,1,0:T(8,128)(2,1)} %bitcast.51, bf16[4,384,256]{2,1,0:T(8,128)(2,1)} %bitcast.53, bf16[4,320,256]{2,1,0:T(8,128)(2,1)} %copy-done), custom_call_target="tpu_custom_call" | custom-call | tf_op jit(solution)/shard_map/example_squares/pallas_call | solution.py:108
  159.2 0.8 slice_reduce_fusion
  160.0 20.7 %all_to_all.49 = f32[64,4,3]{2,1,0:T(4,128)S(1)} all-to-all(f32[64,4,3]{2,1,0:T(4,128)S(1)} %broadcast_in_dim.14), channel_id=1, replica_groups={{0,1,2,3,16,17,18,19,32,33,34,35,48,49,50,51,64,65,66,67,80,81,82,83,96..., dimensions={0} | all-to-all | bytes 6144 | tf_op jit(solution)/shard_map/all_to_all | solution.py:30
  180.8 0.6 maximum_divide_fusion.factors_ref
  181.4 5.4 %clipped_sum.1 = bf16[4,320,256]{2,1,0:T(8,128)(2,1)} custom-call(f32[4,3]{1,0:T(4,128)} %maximum_divide_fusion.factors_ref, bf16[4,4,320,640]{3,2,1,0:T(8,128)(2,1)} %bitcast.52, bf16[4,384,256]{2,1,0:T(8,128)(2,1)} %bitcast.54), custom_call_target="tpu_custom_call" | custom-call | tf_op jit(solution)/shard_map/clipped_sum/pallas_call | solution.py:156
  186.8 12.6 %all_to_all.50 = bf16[4,320,256]{2,1,0:T(8,128)(2,1)S(1)} all-to-all(bf16[4,320,256]{2,1,0:T(8,128)(2,1)} %clipped_sum.1), channel_id=1, replica_groups={{0,4,8,12},{1,5,9,13},{2,6,10,14},{3,7,11,15},{16,20,24,28},{17,21,25,2..., dimensions={0} | all-to-all | bytes 1310720 | tf_op jit(solution)/shard_map/all_to_all | solution.py:30
  199.5 1.2 divide_subtract_fusion
  (37 shorter events, 1.2 us)
Async XLA Ops:
  7.2 48.6 %copy-start.1 = (f32[320,256]{1,0:T(8,128)S(1)}, f32[320,256]{1,0:T(8,128)}, u32[]{:S(2)}) copy-start(f32[320,256]{1,0:T(8,128)} %param.15) | copy-start | bytes 983044
  7.2 73.2 %all-gather.3.cloned.1.call-start = ((), (), s32[]{:S(2)}) async-start(), calls=%async_computation.9 | async-start | bytes 6963200 | tf_op jit(solution)/shard_map/all_gather | solution.py:212
  9.1 15.5 %collective-permute-start = (bf16[320,640]{1,0:T(8,128)(2,1)}, bf16[320,640]{1,0:T(8,128)(2,1)S(1)}, u32[]{:S(2)}, u32[]{:S(2)}) collective-permute-start(bf16[320,640]{1,0:T(8,128)(2,1)} %live_block.1), channel_id=1, source_target_pairs={{0,0},{1,1},{2,2},{3,3},{4,16},{5,17},{6,18},{7,19},{8,32},{9,33},... | collective-permute-start | bytes 1228808 | tf_op jit(solution)/shard_map/ppermute | solution.py:208
  24.7 0.8 copy-start.3
  52.1 11.4 %all-to-all-start.2 = ((bf16[4,160,256]{2,1,0:T(8,128)(2,1)}), bf16[4,160,256]{2,1,0:T(8,128)(2,1)S(1)}, u32[]{:S(2)}, u32[]{:S(2)}) async-start(bf16[4,160,256]{2,1,0:T(8,128)(2,1)} %bitcast.15), calls=%async_computation.2 | async-start | bytes 655360 | tf_op jit(solution)/shard_map/all_to_all | solution.py:204
  64.4 14.0 %all-to-all-start = ((bf16[4,320,256]{2,1,0:T(8,128)(2,1)}), bf16[4,320,256]{2,1,0:T(8,128)(2,1)S(1)}, u32[]{:S(2)}, u32[]{:S(2)}) async-start(bf16[4,320,256]{2,1,0:T(8,128)(2,1)} %broadcast_in_dim.10), calls=%async_computation | async-start | bytes 1310720 | tf_op jit(solution)/shard_map/all_to_all | solution.py:204
  126.1 14.0 %copy-start.4 = (f32[320,256]{1,0:T(8,128)S(1)}, f32[320,256]{1,0:T(8,128)}, u32[]{:S(2)}) copy-start(f32[320,256]{1,0:T(8,128)} %param.16) | copy-start | bytes 983044
  140.3 59.2 %copy-start.2 = (f32[320,256]{1,0:T(8,128)}, f32[320,256]{1,0:T(8,128)S(1)}, u32[]{:S(2)}) copy-start(f32[320,256]{1,0:T(8,128)S(1)} %get-tuple-element.32) | copy-start | bytes 983044
  141.3 11.1 %all-to-all-start.6 = ((bf16[4,320,256]{2,1,0:T(8,128)(2,1)}), bf16[4,320,256]{2,1,0:T(8,128)(2,1)S(1)}, u32[]{:S(2)}, u32[]{:S(2)}) async-start(bf16[4,320,256]{2,1,0:T(8,128)(2,1)} %broadcast_in_dim.12), calls=%async_computation.6 | async-start | bytes 1310720 | tf_op jit(solution)/shard_map/all_to_all | solution.py:30
  152.3 0.8 copy-start
  181.4 18.1 %copy-start.5 = (f32[320,256]{1,0:T(8,128)S(1)}, f32[320,256]{1,0:T(8,128)}, u32[]{:S(2)}) copy-start(f32[320,256]{1,0:T(8,128)} %param.19) | copy-start | bytes 983044
  181.4 18.1 %copy-start.6 = (f32[320,256]{1,0:T(8,128)S(1)}, f32[320,256]{1,0:T(8,128)}, u32[]{:S(2)}) copy-start(f32[320,256]{1,0:T(8,128)} %param.17) | copy-start | bytes 983044
  181.4 18.1 %copy-start.7 = (f32[320,256]{1,0:T(8,128)S(1)}, f32[320,256]{1,0:T(8,128)}, u32[]{:S(2)}) copy-start(f32[320,256]{1,0:T(8,128)} %param.18) | copy-start | bytes 983044
Sparse Core Ops, SparseCore 0:
  25.6 54.7 all-gather.2

commit v10 on v9

--- a/solution.py
+++ b/solution.py
@@ -43,7 +43,9 @@
         odd, core = divmod(inner, CORES)
         for tile in range(tiles):
             x, y = divmod(tile, SIDE)
-            target = (quad * SIDE + x) * tiles + (odd + 2 * core) * SIDE + y
+            chip, side = x % 2, x // 2
+            target = (quad * SIDE + chip * CORES + side) * tiles
+            target = target + (odd + 2 * core) * SIDE + y
             moves.append((replica * tiles + tile, target))
     return moves
 
@@ -183,6 +185,7 @@
 ):
     replicas = lax.axis_size("replica")
     along_x = [[x * SIDE + y for x in range(SIDE)] for y in range(SIDE)]
+    by_side = [[x * SIDE + y for x in (0, 2, 1, 3)] for y in range(SIDE)]
     along_y = [[x * SIDE + y for y in range(SIDE)] for x in range(SIDE)]
     same_class = [
         [r * SIDE * SIDE + x * SIDE + y for r in range(replicas) for y in range(SIDE)]
@@ -214,7 +217,9 @@
 
     targets = targets.reshape(quads, 2, CORES, -1, cols).transpose(2, 1, 0, 3, 4)
     targets = across_x(targets.reshape(SIDE, -1, cols))
-    w_group = across_x(everywhere(w_half, SIDE))
+    w_group = lax.all_to_all(
+        everywhere(w_half, SIDE), "tile", 0, 0, tiled=True, axis_index_groups=by_side
+    )
     targets = targets.reshape(SIDE, quads, pub_rows + priv_rows, cols).transpose(1, 0, 2, 3)
     targets = jnp.concatenate(
         [
@@ -248,7 +253,7 @@
     private_delta = by_token(deltas[:, pub_all:], priv_rows)
 
     def over_classes(part):
-        got, _ = exchange(part.astype(jnp.bfloat16), "tile", along_x)
+        got, _ = exchange(part.astype(jnp.bfloat16), "tile", by_side)
         return jnp.sum(got.astype(jnp.float32), axis=0)
 
     public_grad = over_classes(
@@ -262,7 +267,7 @@
     new_public = beta_public * public_moment + (1.0 - beta_public) * public_grad * public_grad
     precond = 1.0 / (jnp.sqrt(new_public) + public_epsilon)
     precond_group, _ = exchange(
-        everywhere(precond.astype(jnp.bfloat16), SIDE), "tile", along_x
+        everywhere(precond.astype(jnp.bfloat16), SIDE), "tile", by_side
     )
 
     squares = example_squares(tokens, private_delta, precond_group)

time: 209 us -> 208 us (level)
    all_to_all x0 -> x1, waiting for transfers between devices: none -> 10.6 us  [on_device(): lax.all_to_all(everywhere(w_half, SIDE), 'tile', 0, 0, tiled=True, axis_i...]
    all_to_all x2 -> x1, waiting for transfers between devices: 18.2 us -> 7.77 us  [across_x(): lax.all_to_all(sent, 'tile', 0, 0, tiled=True, axis_index_groups=along_x)]
    all_to_all x0 -> x1, starting transfers between devices: none -> 3.49 us  [on_device(): lax.all_to_all(everywhere(w_half, SIDE), 'tile', 0, 0, tiled=True, axis_i...]
    all_to_all x2 -> x1, starting transfers between devices: 7.08 us -> 4.9 us  [across_x(): lax.all_to_all(sent, 'tile', 0, 0, tiled=True, axis_index_groups=along_x)]
where the time goes in v10:
time: 208 us; the launch traced here: 206 us
  blocking collectives  108 us (52%)
  waiting for transfers between devices  35.2 us (17%)
  starting transfers between devices  17.9 us (9%)
  between operations  14.3 us (7%)
  Pallas kernels  13.3 us (6%)
  matrix products  7.41 us (4%)
  local copies, waits for them, and re-layouts  6.66 us (3%)
  other arithmetic  3.65 us (2%)
    all_to_all x5, blocking collectives, exchange(): got = lax.all_to_all(sent, axis, 0, 0, tiled=True, axis_index_groups=groups)  85.1 us
    all_to_all x1, blocking collectives, on_device(): targets = lax.all_to_all(targets, 'replica', 0, 0, tiled=True)  22.9 us
    all_to_all x1, waiting for transfers between devices, on_device(): lax.all_to_all(everywhere(w_half, SIDE), 'tile', 0, 0, tiled=True, axis_i...  10.6 us
    ppermute x1, waiting for transfers between devices, on_device(): local = lax.ppermute(local, ('replica', 'tile'), moves)  9.67 us
    all_to_all x1, waiting for transfers between devices, across_x(): lax.all_to_all(sent, 'tile', 0, 0, tiled=True, axis_index_groups=along_x)  7.77 us
    all_to_all x1, waiting for transfers between devices, exchange(): got = lax.all_to_all(sent, axis, 0, 0, tiled=True, axis_index_groups=groups)  6.25 us
    ppermute x1, starting transfers between devices, on_device(): local = lax.ppermute(local, ('replica', 'tile'), moves)  6.02 us
    pallas_call x1, Pallas kernels, example_squares(): pl.pallas_call(norms_kernel, grid=(quads,), in_specs=[pl.BlockSpec((1, si...  6.01 us
  transfers between devices with their start and end apart: 5, of which 5 were waited for; matrix products, arithmetic and copies ran while one was open for 2% of the time, Pallas kernels for 0%

profile of v10, /device:TPU:1, one launch (start us, length us, event | category | flops | bytes accessed | tf_op | source)
XLA Modules:
  0.0 206.4 jit_solution(11438662464468818524)
XLA Ops:
  7.2 1.9 live_block.1
  9.1 6.0 %collective-permute-start = (bf16[320,640]{1,0:T(8,128)(2,1)}, bf16[320,640]{1,0:T(8,128)(2,1)S(1)}, u32[]{:S(2)}, u32[]{:S(2)}) collective-permute-start(bf16[320,640]{1,0:T(8,128)(2,1)} %live_block.1), channel_id=1, source_target_pairs={{0,0},{1,1},{2,2},{3,3},{4,32},{5,33},{6,34},{7,35},{8,16},{9,17},... | collective-permute-start | bytes 1228808 | tf_op jit(solution)/shard_map/ppermute | solution.py:211
  15.1 9.7 %collective-permute-done = bf16[320,640]{1,0:T(8,128)(2,1)S(1)} collective-permute-done((bf16[320,640]{1,0:T(8,128)(2,1)}, bf16[320,640]{1,0:T(8,128)(2,1)S(1)}, u32[]{:S(2)}, u32[]{:S(2)}) %collective-permute-start) | collective-permute-done | bytes 409632 | tf_op jit(solution)/shard_map/ppermute | solution.py:211
  24.8 0.8 copy-done.3
  25.6 1.0 pad_maximum_fusion.1
  26.8 22.9 %all_to_all.45 = bf16[16,40,256]{2,1,0:T(8,128)(2,1)S(1)} all-to-all(bf16[16,40,256]{2,1,0:T(8,128)(2,1)S(1)} %copy.36), channel_id=1, replica_groups=mesh['replica'=16,'tile'=16] {'replica'}, dimensions={0} | all-to-all | bytes 655360 | tf_op jit(solution)/shard_map/all_to_all | solution.py:212
  49.7 0.7 copy.37
  50.5 4.9 %all-to-all-start.2 = ((bf16[4,160,256]{2,1,0:T(8,128)(2,1)}), bf16[4,160,256]{2,1,0:T(8,128)(2,1)S(1)}, u32[]{:S(2)}, u32[]{:S(2)}) async-start(bf16[4,160,256]{2,1,0:T(8,128)(2,1)} %bitcast.15), calls=%async_computation.2 | async-start | bytes 655360 | tf_op jit(solution)/shard_map/all_to_all | solution.py:207
  55.4 7.8 %all-to-all-done.2 = bf16[4,160,256]{2,1,0:T(8,128)(2,1)S(1)} async-done(((bf16[4,160,256]{2,1,0:T(8,128)(2,1)}), bf16[4,160,256]{2,1,0:T(8,128)(2,1)S(1)}, u32[]{:S(2)}, u32[]{:S(2)}) %all-to-all-start.2) | async-done | bytes 327712 | tf_op jit(solution)/shard_map/all_to_all | solution.py:207
  63.1 0.9 broadcast_in_dim.10
  64.0 3.5 %all-to-all-start = ((bf16[4,320,256]{2,1,0:T(8,128)(2,1)}), bf16[4,320,256]{2,1,0:T(8,128)(2,1)S(1)}, u32[]{:S(2)}, u32[]{:S(2)}) async-start(bf16[4,320,256]{2,1,0:T(8,128)(2,1)} %broadcast_in_dim.10), calls=%async_computation | async-start | bytes 1310720 | tf_op jit(solution)/shard_map/all_to_all | solution.py:220
  67.6 10.6 %all-to-all-done = bf16[4,320,256]{2,1,0:T(8,128)(2,1)S(1)} async-done(((bf16[4,320,256]{2,1,0:T(8,128)(2,1)}), bf16[4,320,256]{2,1,0:T(8,128)(2,1)S(1)}, u32[]{:S(2)}, u32[]{:S(2)}) %all-to-all-start) | async-done | bytes 655392 | tf_op jit(solution)/shard_map/all_to_all | solution.py:220
  78.3 0.9 all-gather.3.cloned.1.call-done
  79.1 4.8 %bitcast_convert_fusion = bf16[4,640,256]{2,1,0:T(8,128)(2,1)S(1)} fusion(bf16[4,4,320,640]{3,2,1,0:T(8,128)(2,1)} %bitcast.49, bf16[4,320,256]{2,1,0:T(8,128)(2,1)S(1)} %all-to-all-done), kind=kOutput, calls=%fused_computation | convolution fusion | flops 1678376960 | bytes 8519680 | tf_op jit(solution)/shard_map/qxfn,xfk->qnk/dot_general | solution.py:240
  84.3 21.4 %all_to_all.46 = bf16[4,640,256]{2,1,0:T(8,128)(2,1)S(1)} all-to-all(bf16[4,640,256]{2,1,0:T(8,128)(2,1)S(1)} %pad_maximum_fusion), channel_id=1, replica_groups={{0,1,2,3},{4,5,6,7},{8,9,10,11},{12,13,14,15},{16,17,18,19},{20,21,22,2..., dimensions={0} | all-to-all | bytes 2621440 | tf_op jit(solution)/shard_map/all_to_all | solution.py:30
  105.7 0.2 convert_reduce_fusion
  106.1 18.7 %all_to_all.47 = bf16[4,640,256]{2,1,0:T(8,128)(2,1)S(1)} all-to-all(bf16[4,640,256]{2,1,0:T(8,128)(2,1)S(1)} %broadcast_in_dim.11), channel_id=1, replica_groups={{0,1,2,3},{4,5,6,7},{8,9,10,11},{12,13,14,15},{16,17,18,19},{20,21,22,2..., dimensions={0} | all-to-all | bytes 2621440 | tf_op jit(solution)/shard_map/all_to_all | solution.py:30
  124.9 2.6 %fusion.5 = bf16[4,320,256]{2,1,0:T(8,128)(2,1)S(1)} fusion(bf16[4,256,256,1]{2,1,3,0:T(8,128)(2,1)S(1)} %bitcast.69, bf16[4,4,320,640]{3,2,1,0:T(8,128)(2,1)} %bitcast.50), kind=kOutput, calls=%fused_computation.5 | convolution fusion | flops 671416320 | bytes 3801088 | tf_op jit(solution)/shard_map/qxfn,qnk->xfk/dot_general | solution.py:260
  127.6 12.1 %all_to_all.48 = bf16[4,320,256]{2,1,0:T(8,128)(2,1)S(1)} all-to-all(bf16[4,320,256]{2,1,0:T(8,128)(2,1)S(1)} %fusion.5), channel_id=1, replica_groups={{0,8,4,12},{1,9,5,13},{2,10,6,14},{3,11,7,15},{16,24,20,28},{17,25,21,2..., dimensions={0} | all-to-all | bytes 1310720 | tf_op jit(solution)/shard_map/all_to_all | solution.py:30
  139.7 0.2 fusion.9
  139.9 0.9 broadcast_in_dim.12
  140.8 3.5 %all-to-all-start.6 = ((bf16[4,320,256]{2,1,0:T(8,128)(2,1)}), bf16[4,320,256]{2,1,0:T(8,128)(2,1)S(1)}, u32[]{:S(2)}, u32[]{:S(2)}) async-start(bf16[4,320,256]{2,1,0:T(8,128)(2,1)} %broadcast_in_dim.12), calls=%async_computation.6 | async-start | bytes 1310720 | tf_op jit(solution)/shard_map/all_to_all | solution.py:30
  144.4 1.0 copy.40
  145.4 6.2 %all-to-all-done.6.precond_ref = bf16[4,320,256]{2,1,0:T(8,128)(2,1)S(1)} async-done(((bf16[4,320,256]{2,1,0:T(8,128)(2,1)}), bf16[4,320,256]{2,1,0:T(8,128)(2,1)S(1)}, u32[]{:S(2)}, u32[]{:S(2)}) %all-to-all-start.6) | async-done | bytes 655392 | tf_op jit(solution)/shard_map/all_to_all | solution.py:30
  151.6 0.8 copy-done
  152.5 6.0 %example_squares.1 = f32[4,8,128]{2,1,0:T(8,128)} custom-call(bf16[4,4,320,640]{3,2,1,0:T(8,128)(2,1)} %bitcast.51, bf16[4,384,256]{2,1,0:T(8,128)(2,1)} %bitcast.53, bf16[4,320,256]{2,1,0:T(8,128)(2,1)} %copy-done), custom_call_target="tpu_custom_call" | custom-call | tf_op jit(solution)/shard_map/example_squares/pallas_call | solution.py:110
  158.5 0.8 slice_reduce_fusion
  159.3 20.5 %all_to_all.49 = f32[64,4,3]{2,1,0:T(4,128)S(1)} all-to-all(f32[64,4,3]{2,1,0:T(4,128)S(1)} %broadcast_in_dim.14), channel_id=1, replica_groups={{0,1,2,3,16,17,18,19,32,33,34,35,48,49,50,51,64,65,66,67,80,81,82,83,96..., dimensions={0} | all-to-all | bytes 6144 | tf_op jit(solution)/shard_map/all_to_all | solution.py:30
  179.9 0.6 maximum_divide_fusion.factors_ref
  180.5 5.4 %clipped_sum.1 = bf16[4,320,256]{2,1,0:T(8,128)(2,1)} custom-call(f32[4,3]{1,0:T(4,128)} %maximum_divide_fusion.factors_ref, bf16[4,4,320,640]{3,2,1,0:T(8,128)(2,1)} %bitcast.52, bf16[4,384,256]{2,1,0:T(8,128)(2,1)} %bitcast.54), custom_call_target="tpu_custom_call" | custom-call | tf_op jit(solution)/shard_map/clipped_sum/pallas_call | solution.py:158
  185.9 12.3 %all_to_all.50 = bf16[4,320,256]{2,1,0:T(8,128)(2,1)S(1)} all-to-all(bf16[4,320,256]{2,1,0:T(8,128)(2,1)} %clipped_sum.1), channel_id=1, replica_groups={{0,8,4,12},{1,9,5,13},{2,10,6,14},{3,11,7,15},{16,24,20,28},{17,25,21,2..., dimensions={0} | all-to-all | bytes 1310720 | tf_op jit(solution)/shard_map/all_to_all | solution.py:30
  198.4 1.2 divide_subtract_fusion
  (37 shorter events, 1.2 us)
Async XLA Ops:
  7.2 48.2 %copy-start.1 = (f32[320,256]{1,0:T(8,128)S(1)}, f32[320,256]{1,0:T(8,128)}, u32[]{:S(2)}) copy-start(f32[320,256]{1,0:T(8,128)} %param.15) | copy-start | bytes 983044
  7.2 72.0 %all-gather.3.cloned.1.call-start = ((), (), s32[]{:S(2)}) async-start(), calls=%async_computation.9 | async-start | bytes 6963200 | tf_op jit(solution)/shard_map/all_gather | solution.py:215
  9.1 15.7 %collective-permute-start = (bf16[320,640]{1,0:T(8,128)(2,1)}, bf16[320,640]{1,0:T(8,128)(2,1)S(1)}, u32[]{:S(2)}, u32[]{:S(2)}) collective-permute-start(bf16[320,640]{1,0:T(8,128)(2,1)} %live_block.1), channel_id=1, source_target_pairs={{0,0},{1,1},{2,2},{3,3},{4,32},{5,33},{6,34},{7,35},{8,16},{9,17},... | collective-permute-start | bytes 1228808 | tf_op jit(solution)/shard_map/ppermute | solution.py:211
  24.8 0.8 copy-start.3
  50.5 12.7 %all-to-all-start.2 = ((bf16[4,160,256]{2,1,0:T(8,128)(2,1)}), bf16[4,160,256]{2,1,0:T(8,128)(2,1)S(1)}, u32[]{:S(2)}, u32[]{:S(2)}) async-start(bf16[4,160,256]{2,1,0:T(8,128)(2,1)} %bitcast.15), calls=%async_computation.2 | async-start | bytes 655360 | tf_op jit(solution)/shard_map/all_to_all | solution.py:207
  64.0 14.2 %all-to-all-start = ((bf16[4,320,256]{2,1,0:T(8,128)(2,1)}), bf16[4,320,256]{2,1,0:T(8,128)(2,1)S(1)}, u32[]{:S(2)}, u32[]{:S(2)}) async-start(bf16[4,320,256]{2,1,0:T(8,128)(2,1)} %broadcast_in_dim.10), calls=%async_computation | async-start | bytes 1310720 | tf_op jit(solution)/shard_map/all_to_all | solution.py:220
  124.9 14.8 %copy-start.4 = (f32[320,256]{1,0:T(8,128)S(1)}, f32[320,256]{1,0:T(8,128)}, u32[]{:S(2)}) copy-start(f32[320,256]{1,0:T(8,128)} %param.16) | copy-start | bytes 983044
  139.9 58.4 %copy-start.2 = (f32[320,256]{1,0:T(8,128)}, f32[320,256]{1,0:T(8,128)S(1)}, u32[]{:S(2)}) copy-start(f32[320,256]{1,0:T(8,128)S(1)} %get-tuple-element.32) | copy-start | bytes 983044
  140.8 10.8 %all-to-all-start.6 = ((bf16[4,320,256]{2,1,0:T(8,128)(2,1)}), bf16[4,320,256]{2,1,0:T(8,128)(2,1)S(1)}, u32[]{:S(2)}, u32[]{:S(2)}) async-start(bf16[4,320,256]{2,1,0:T(8,128)(2,1)} %broadcast_in_dim.12), calls=%async_computation.6 | async-start | bytes 1310720 | tf_op jit(solution)/shard_map/all_to_all | solution.py:30
  151.6 0.8 copy-start
  180.5 17.8 %copy-start.5 = (f32[320,256]{1,0:T(8,128)S(1)}, f32[320,256]{1,0:T(8,128)}, u32[]{:S(2)}) copy-start(f32[320,256]{1,0:T(8,128)} %param.19) | copy-start | bytes 983044
  180.5 17.8 %copy-start.6 = (f32[320,256]{1,0:T(8,128)S(1)}, f32[320,256]{1,0:T(8,128)}, u32[]{:S(2)}) copy-start(f32[320,256]{1,0:T(8,128)} %param.17) | copy-start | bytes 983044
  180.5 17.8 %copy-start.7 = (f32[320,256]{1,0:T(8,128)S(1)}, f32[320,256]{1,0:T(8,128)}, u32[]{:S(2)}) copy-start(f32[320,256]{1,0:T(8,128)} %param.18) | copy-start | bytes 983044
Sparse Core Ops, SparseCore 0:
  25.7 53.3 all-gather.2

commit v11 on v10

--- a/solution.py
+++ b/solution.py
@@ -12,7 +12,7 @@
 Q = 4096
 CORES = 2
 SIDE = 4
-KERNEL_VMEM = 58 * 2**20
+KERNEL_VMEM = 52 * 2**20
 
 
 beta_first = 0.9

time: 208 us -> 203 us (0.976)
  local copies, waits for them, and re-layouts: 6.66 us -> 4.24 us
  Pallas kernels: 13.3 us -> 11.2 us
where the time goes in v11:
time: 203 us; the launch traced here: 201 us
  blocking collectives  107 us (53%)
  waiting for transfers between devices  36.1 us (18%)
  starting transfers between devices  17.9 us (9%)
  between operations  14.3 us (7%)
  Pallas kernels  11.2 us (6%)
  matrix products  7.41 us (4%)
  local copies, waits for them, and re-layouts  4.24 us (2%)
  other arithmetic  3.06 us (2%)
    all_to_all x5, blocking collectives, exchange(): got = lax.all_to_all(sent, axis, 0, 0, tiled=True, axis_index_groups=groups)  83.7 us
    all_to_all x1, blocking collectives, on_device(): targets = lax.all_to_all(targets, 'replica', 0, 0, tiled=True)  22.9 us
    all_to_all x1, waiting for transfers between devices, on_device(): lax.all_to_all(everywhere(w_half, SIDE), 'tile', 0, 0, tiled=True, axis_i...  10.6 us
    ppermute x1, waiting for transfers between devices, on_device(): local = lax.ppermute(local, ('replica', 'tile'), moves)  9.67 us
    all_to_all x1, waiting for transfers between devices, across_x(): lax.all_to_all(sent, 'tile', 0, 0, tiled=True, axis_index_groups=along_x)  7.77 us
    all_to_all x1, waiting for transfers between devices, exchange(): got = lax.all_to_all(sent, axis, 0, 0, tiled=True, axis_index_groups=groups)  7.16 us
    ppermute x1, starting transfers between devices, on_device(): local = lax.ppermute(local, ('replica', 'tile'), moves)  6.02 us
    pallas_call x1, Pallas kernels, example_squares(): pl.pallas_call(norms_kernel, grid=(quads,), in_specs=[pl.BlockSpec((1, si...  4.99 us
  transfers between devices with their start and end apart: 5, of which 5 were waited for; matrix products, arithmetic and copies ran while one was open for 2% of the time, Pallas kernels for 0%

profile of v11, /device:TPU:1, one launch (start us, length us, event | category | flops | bytes accessed | tf_op | source)
XLA Modules:
  0.0 200.9 jit_solution(10330000630242299262)
XLA Ops:
  7.2 1.9 live_block.1
  9.1 6.0 %collective-permute-start = (bf16[320,640]{1,0:T(8,128)(2,1)}, bf16[320,640]{1,0:T(8,128)(2,1)S(1)}, u32[]{:S(2)}, u32[]{:S(2)}) collective-permute-start(bf16[320,640]{1,0:T(8,128)(2,1)} %live_block.1), channel_id=1, source_target_pairs={{0,0},{1,1},{2,2},{3,3},{4,32},{5,33},{6,34},{7,35},{8,16},{9,17},... | collective-permute-start | bytes 1228808 | tf_op jit(solution)/shard_map/ppermute | solution.py:211
  15.1 9.7 %collective-permute-done = bf16[320,640]{1,0:T(8,128)(2,1)S(1)} collective-permute-done((bf16[320,640]{1,0:T(8,128)(2,1)}, bf16[320,640]{1,0:T(8,128)(2,1)S(1)}, u32[]{:S(2)}, u32[]{:S(2)}) %collective-permute-start) | collective-permute-done | bytes 409632 | tf_op jit(solution)/shard_map/ppermute | solution.py:211
  24.8 0.8 copy-done.2
  25.6 1.0 pad_maximum_fusion.1
  26.7 0.1 copy.36
  26.8 22.9 %all_to_all.45 = bf16[16,40,256]{2,1,0:T(8,128)(2,1)S(1)} all-to-all(bf16[16,40,256]{2,1,0:T(8,128)(2,1)S(1)} %copy.36), channel_id=1, replica_groups=mesh['replica'=16,'tile'=16] {'replica'}, dimensions={0} | all-to-all | bytes 655360 | tf_op jit(solution)/shard_map/all_to_all | solution.py:212
  49.7 0.7 copy.37
  50.4 4.9 %all-to-all-start.2 = ((bf16[4,160,256]{2,1,0:T(8,128)(2,1)}), bf16[4,160,256]{2,1,0:T(8,128)(2,1)S(1)}, u32[]{:S(2)}, u32[]{:S(2)}) async-start(bf16[4,160,256]{2,1,0:T(8,128)(2,1)} %bitcast.15), calls=%async_computation.2 | async-start | bytes 655360 | tf_op jit(solution)/shard_map/all_to_all | solution.py:207
  55.4 7.8 %all-to-all-done.2 = bf16[4,160,256]{2,1,0:T(8,128)(2,1)S(1)} async-done(((bf16[4,160,256]{2,1,0:T(8,128)(2,1)}), bf16[4,160,256]{2,1,0:T(8,128)(2,1)S(1)}, u32[]{:S(2)}, u32[]{:S(2)}) %all-to-all-start.2) | async-done | bytes 327712 | tf_op jit(solution)/shard_map/all_to_all | solution.py:207
  63.1 0.9 broadcast_in_dim.10
  64.0 3.5 %all-to-all-start = ((bf16[4,320,256]{2,1,0:T(8,128)(2,1)}), bf16[4,320,256]{2,1,0:T(8,128)(2,1)S(1)}, u32[]{:S(2)}, u32[]{:S(2)}) async-start(bf16[4,320,256]{2,1,0:T(8,128)(2,1)} %broadcast_in_dim.10), calls=%async_computation | async-start | bytes 1310720 | tf_op jit(solution)/shard_map/all_to_all | solution.py:220
  67.6 10.6 %all-to-all-done = bf16[4,320,256]{2,1,0:T(8,128)(2,1)S(1)} async-done(((bf16[4,320,256]{2,1,0:T(8,128)(2,1)}), bf16[4,320,256]{2,1,0:T(8,128)(2,1)S(1)}, u32[]{:S(2)}, u32[]{:S(2)}) %all-to-all-start) | async-done | bytes 655392 | tf_op jit(solution)/shard_map/all_to_all | solution.py:220
  78.3 0.9 all-gather.3.cloned.1.call-done
  79.1 4.8 %bitcast_convert_fusion = bf16[4,640,256]{2,1,0:T(8,128)(2,1)S(1)} fusion(bf16[4,4,320,640]{3,2,1,0:T(8,128)(2,1)} %bitcast.51, bf16[4,320,256]{2,1,0:T(8,128)(2,1)S(1)} %all-to-all-done), kind=kOutput, calls=%fused_computation | convolution fusion | flops 1678376960 | bytes 8519680 | tf_op jit(solution)/shard_map/qxfn,xfk->qnk/dot_general | solution.py:240
  84.2 0.1 pad_maximum_fusion
  84.2 21.4 %all_to_all.46 = bf16[4,640,256]{2,1,0:T(8,128)(2,1)S(1)} all-to-all(bf16[4,640,256]{2,1,0:T(8,128)(2,1)S(1)} %pad_maximum_fusion), channel_id=1, replica_groups={{0,1,2,3},{4,5,6,7},{8,9,10,11},{12,13,14,15},{16,17,18,19},{20,21,22,2..., dimensions={0} | all-to-all | bytes 2621440 | tf_op jit(solution)/shard_map/all_to_all | solution.py:30
  105.7 0.2 convert_reduce_fusion
  105.9 0.1 subtract_convert_fusion
  106.1 18.7 %all_to_all.47 = bf16[4,640,256]{2,1,0:T(8,128)(2,1)S(1)} all-to-all(bf16[4,640,256]{2,1,0:T(8,128)(2,1)S(1)} %broadcast_in_dim.11), channel_id=1, replica_groups={{0,1,2,3},{4,5,6,7},{8,9,10,11},{12,13,14,15},{16,17,18,19},{20,21,22,2..., dimensions={0} | all-to-all | bytes 2621440 | tf_op jit(solution)/shard_map/all_to_all | solution.py:30
  124.9 2.6 %fusion.5 = bf16[4,320,256]{2,1,0:T(8,128)(2,1)S(1)} fusion(bf16[4,256,256,1]{2,1,3,0:T(8,128)(2,1)S(1)} %bitcast.69, bf16[4,4,320,640]{3,2,1,0:T(8,128)(2,1)} %bitcast.52), kind=kOutput, calls=%fused_computation.5 | convolution fusion | flops 671416320 | bytes 3801088 | tf_op jit(solution)/shard_map/qxfn,qnk->xfk/dot_general | solution.py:260
  127.6 12.1 %all_to_all.48 = bf16[4,320,256]{2,1,0:T(8,128)(2,1)S(1)} all-to-all(bf16[4,320,256]{2,1,0:T(8,128)(2,1)S(1)} %fusion.5), channel_id=1, replica_groups={{0,8,4,12},{1,9,5,13},{2,10,6,14},{3,11,7,15},{16,24,20,28},{17,25,21,2..., dimensions={0} | all-to-all | bytes 1310720 | tf_op jit(solution)/shard_map/all_to_all | solution.py:30
  139.7 0.2 fusion.9
  139.9 1.0 broadcast_in_dim.12
  140.9 3.5 %all-to-all-start.6 = ((bf16[4,320,256]{2,1,0:T(8,128)(2,1)}), bf16[4,320,256]{2,1,0:T(8,128)(2,1)S(1)}, u32[]{:S(2)}, u32[]{:S(2)}) async-start(bf16[4,320,256]{2,1,0:T(8,128)(2,1)} %broadcast_in_dim.12), calls=%async_computation.6 | async-start | bytes 1310720 | tf_op jit(solution)/shard_map/all_to_all | solution.py:30
  144.5 7.2 %all-to-all-done.6.precond_ref = bf16[4,320,256]{2,1,0:T(8,128)(2,1)S(1)} async-done(((bf16[4,320,256]{2,1,0:T(8,128)(2,1)}), bf16[4,320,256]{2,1,0:T(8,128)(2,1)S(1)}, u32[]{:S(2)}, u32[]{:S(2)}) %all-to-all-start.6) | async-done | bytes 655392 | tf_op jit(solution)/shard_map/all_to_all | solution.py:30
  151.7 5.0 %example_squares.1 = f32[4,8,128]{2,1,0:T(8,128)S(1)} custom-call(bf16[4,4,320,640]{3,2,1,0:T(8,128)(2,1)} %bitcast.53, bf16[4,384,256]{2,1,0:T(8,128)(2,1)S(1)} %bitcast.49, bf16[4,320,256]{2,1,0:T(8,128)(2,1)S(1)} %all-to-all-done.6.precond_ref), custom_call_target="tpu_custom_call" | custom-call | tf_op jit(solution)/shard_map/example_squares/pallas_call | solution.py:110
  156.7 0.1 slice_reduce_fusion
  156.8 20.5 %all_to_all.49 = f32[64,4,3]{2,1,0:T(4,128)S(1)} all-to-all(f32[64,4,3]{2,1,0:T(4,128)S(1)} %broadcast_in_dim.14), channel_id=1, replica_groups={{0,1,2,3,16,17,18,19,32,33,34,35,48,49,50,51,64,65,66,67,80,81,82,83,96..., dimensions={0} | all-to-all | bytes 6144 | tf_op jit(solution)/shard_map/all_to_all | solution.py:30
  177.4 4.4 %clipped_sum.1 = bf16[4,320,256]{2,1,0:T(8,128)(2,1)S(1)} custom-call(f32[4,3]{1,0:T(4,128)S(1)} %maximum_divide_fusion.factors_ref, bf16[4,4,320,640]{3,2,1,0:T(8,128)(2,1)} %bitcast.54, bf16[4,384,256]{2,1,0:T(8,128)(2,1)S(1)} %bitcast.50), custom_call_target="tpu_custom_call" | custom-call | tf_op jit(solution)/shard_map/clipped_sum/pallas_call | solution.py:158
  181.8 10.9 %all_to_all.50 = bf16[4,320,256]{2,1,0:T(8,128)(2,1)S(1)} all-to-all(bf16[4,320,256]{2,1,0:T(8,128)(2,1)S(1)} %clipped_sum.1), channel_id=1, replica_groups={{0,8,4,12},{1,9,5,13},{2,10,6,14},{3,11,7,15},{16,24,20,28},{17,25,21,2..., dimensions={0} | all-to-all | bytes 1310720 | tf_op jit(solution)/shard_map/all_to_all | solution.py:30
  192.9 1.2 divide_subtract_fusion
  (35 shorter events, 1.0 us)
Async XLA Ops:
  7.2 48.2 %copy-start = (f32[320,256]{1,0:T(8,128)S(1)}, f32[320,256]{1,0:T(8,128)}, u32[]{:S(2)}) copy-start(f32[320,256]{1,0:T(8,128)} %param.15) | copy-start | bytes 983044
  7.2 72.0 %all-gather.3.cloned.1.call-start = ((), (), s32[]{:S(2)}) async-start(), calls=%async_computation.9 | async-start | bytes 6963200 | tf_op jit(solution)/shard_map/all_gather | solution.py:215
  9.1 15.7 %collective-permute-start = (bf16[320,640]{1,0:T(8,128)(2,1)}, bf16[320,640]{1,0:T(8,128)(2,1)S(1)}, u32[]{:S(2)}, u32[]{:S(2)}) collective-permute-start(bf16[320,640]{1,0:T(8,128)(2,1)} %live_block.1), channel_id=1, source_target_pairs={{0,0},{1,1},{2,2},{3,3},{4,32},{5,33},{6,34},{7,35},{8,16},{9,17},... | collective-permute-start | bytes 1228808 | tf_op jit(solution)/shard_map/ppermute | solution.py:211
  24.8 0.8 copy-start.2
  50.4 12.7 %all-to-all-start.2 = ((bf16[4,160,256]{2,1,0:T(8,128)(2,1)}), bf16[4,160,256]{2,1,0:T(8,128)(2,1)S(1)}, u32[]{:S(2)}, u32[]{:S(2)}) async-start(bf16[4,160,256]{2,1,0:T(8,128)(2,1)} %bitcast.15), calls=%async_computation.2 | async-start | bytes 655360 | tf_op jit(solution)/shard_map/all_to_all | solution.py:207
  64.0 14.2 %all-to-all-start = ((bf16[4,320,256]{2,1,0:T(8,128)(2,1)}), bf16[4,320,256]{2,1,0:T(8,128)(2,1)S(1)}, u32[]{:S(2)}, u32[]{:S(2)}) async-start(bf16[4,320,256]{2,1,0:T(8,128)(2,1)} %broadcast_in_dim.10), calls=%async_computation | async-start | bytes 1310720 | tf_op jit(solution)/shard_map/all_to_all | solution.py:220
  124.9 14.8 %copy-start.3 = (f32[320,256]{1,0:T(8,128)S(1)}, f32[320,256]{1,0:T(8,128)}, u32[]{:S(2)}) copy-start(f32[320,256]{1,0:T(8,128)} %param.16) | copy-start | bytes 983044
  139.9 52.9 %copy-start.1 = (f32[320,256]{1,0:T(8,128)}, f32[320,256]{1,0:T(8,128)S(1)}, u32[]{:S(2)}) copy-start(f32[320,256]{1,0:T(8,128)S(1)} %get-tuple-element.32) | copy-start | bytes 983044
  140.9 10.8 %all-to-all-start.6 = ((bf16[4,320,256]{2,1,0:T(8,128)(2,1)}), bf16[4,320,256]{2,1,0:T(8,128)(2,1)S(1)}, u32[]{:S(2)}, u32[]{:S(2)}) async-start(bf16[4,320,256]{2,1,0:T(8,128)(2,1)} %broadcast_in_dim.12), calls=%async_computation.6 | async-start | bytes 1310720 | tf_op jit(solution)/shard_map/all_to_all | solution.py:30
  177.4 15.4 %copy-start.4 = (f32[320,256]{1,0:T(8,128)S(1)}, f32[320,256]{1,0:T(8,128)}, u32[]{:S(2)}) copy-start(f32[320,256]{1,0:T(8,128)} %param.19) | copy-start | bytes 983044
  177.4 15.4 %copy-start.5 = (f32[320,256]{1,0:T(8,128)S(1)}, f32[320,256]{1,0:T(8,128)}, u32[]{:S(2)}) copy-start(f32[320,256]{1,0:T(8,128)} %param.17) | copy-start | bytes 983044
  177.4 15.4 %copy-start.6 = (f32[320,256]{1,0:T(8,128)S(1)}, f32[320,256]{1,0:T(8,128)}, u32[]{:S(2)}) copy-start(f32[320,256]{1,0:T(8,128)} %param.18) | copy-start | bytes 983044
Sparse Core Ops, SparseCore 0:
  25.7 53.3 all-gather.2
